TPU v7x, 512 devices: a whole 4x4x16 slice. The times are simulated.
512 devices in a mesh: rows: 64 (over y, z_lo, core), maps: 8 (over z_hi, x).
Axes of the slice: x: 4, y: 4, z: 16 (z_hi: 2, z_lo: 8; z = z_hi * 8 + z_lo), core: 2. Of those that a mesh axis runs over, the one named last changes fastest.
Arguments:
- counts: int32 [8, 1024, 32768], P(None, 'rows', 'maps'), may hold values from 0 to 2999, as said below
- weights: float32 [8], replicated, may hold values from 0.2 to 5
Outputs:
- barycenter: float32 [1024, 32768], P('rows', 'maps')
Inputs may be any that keep to these rules, and one draw needn't show every extreme that they name: `counts`: each count is drawn evenly below a ceiling that grows with the row from 1000 (first row) to 3000 (last row), times a level of 1 to 4 over 4 that is drawn for each run of 64 columns; the largest count, 2999, is reached in every draw.
All inputs are finite; a program needn't handle non-finite values.
Results may differ from a plain program's by a relative error of at most 0.0001.
Values sent between devices are 32-bit elements; how exact they have to be, the bound alone decides.
No kernel may reach another device: no remote copies, remote signals or barrier semaphores. Data moves between devices by JAX's collectives and lax.ppermute only.
A program may use at most 64 MiB of HBM per device.

v0:
```python
import functools

import jax
import jax.numpy as jnp
import numpy as np
from jax import lax
from jax.experimental import pallas as pl
from jax.experimental.pallas import tpu as pltpu
from jax.sharding import PartitionSpec as P

HALF = 8
K = 8
LANES = 128
EDGE = -1

SPLIT_A, SPLIT_B = 14, 24
CHUNKS = (
    (31,) + tuple(range(SPLIT_A)),
    tuple(range(SPLIT_A, SPLIT_B)),
    tuple(range(SPLIT_B, 31)),
)
READS = (
    tuple(range(SPLIT_A)),
    tuple(range(SPLIT_A - 2, SPLIT_B)),
    tuple(range(SPLIT_B - 2, 32)) + (EDGE, 0, 1, 2),
)


def taps():
    spread = 0.45 * HALF
    a = np.arange(-HALF, HALF + 1, dtype=np.float64)
    g = np.exp(-a * a / (2.0 * spread * spread))
    return g / g.sum()


def band(out_pos, in_pos):
    g = taps()
    d = np.asarray(in_pos)[None, :] - np.asarray(out_pos)[:, None]
    return np.where(np.abs(d) <= HALF, g[np.clip(d + HALF, 0, 2 * HALF)], 0.0)


def split_np(x):
    x = np.asarray(x, np.float32)
    hi = x.astype(jnp.bfloat16)
    lo = (x - hi.astype(np.float32)).astype(jnp.bfloat16)
    return hi, lo


def positions(core):
    own = np.arange(16)
    if core == 0:
        zo, zq, q, f = np.arange(-24, -16), np.arange(-16, 0), np.arange(16, 32), np.arange(32, 40)
        z8, q8 = np.arange(-8, 0), np.arange(16, 24)
    else:
        zo, zq, q, f = np.arange(32, 40), np.arange(16, 32), np.arange(-16, 0), np.arange(-24, -16)
        z8, q8 = np.arange(16, 24), np.arange(-8, 0)
    return np.concatenate([zo, zq, own, q, f]), np.concatenate([zq, own, q]), np.concatenate([z8, own, q8]), own


def matrices():
    out = []
    for s in range(3):
        both = [split_np(band(positions(c)[s + 1], positions(c)[s])) for c in (0, 1)]
        out += [np.stack([b[0] for b in both]), np.stack([b[1] for b in both])]
    cols = band(np.arange(256), np.arange(512) - 128).T
    return out + list(split_np(cols))


def split(x):
    hi = x.astype(jnp.bfloat16)
    lo = (x - hi.astype(jnp.float32)).astype(jnp.bfloat16)
    return hi, lo


def dot(a, b):
    return jnp.dot(a, b, preferred_element_type=jnp.float32)


def dot3(ah, al, bh, bl):
    return dot(ah, bh) + (dot(al, bh) + dot(ah, bl))


def window_sum(pos, size):
    g = taps()
    total = jnp.zeros(pos.shape, jnp.float32)
    for i, a in enumerate(range(-HALF, HALF + 1)):
        total = total + jnp.where((pos + a >= 0) & (pos + a < size), np.float32(g[i]), np.float32(0.0))
    return total


def kernel(reads, sources, height, width, scal, mix, relcol, *refs):
    n_in = 1 + 4 * len(sources) + (2 if EDGE in reads else 0)
    zo = refs[0]
    parts = {c: refs[1 + 4 * i : 5 + 4 * i] for i, c in enumerate(sources)}
    halo = refs[1 + 4 * len(sources) : n_in]
    g1h, g1l, g2h, g2l, g3h, g3l, bh, bl = refs[n_in : n_in + 8]
    out = refs[n_in + 8]
    n_ref, rr, rc, cv, h1h, h1l, h2h, h2l, h3h, h3l, u_ref, w_ref = refs[n_in + 9 :]
    blocks = len(reads)
    tiles = blocks // 2
    core, outer, row0, col0 = scal[0], scal[1], scal[2], scal[3]
    foff = pl.multiple_of(core * 8, 8)

    where = {b: (c, i) for c, ids in enumerate(CHUNKS) for i, b in enumerate(ids)}
    at = 0
    while at < blocks:
        dst = pl.ds(at * LANES, LANES)
        if reads[at] == EDGE:
            lane = lax.broadcasted_iota(jnp.int32, (K, 8, LANES), 2)
            left, right = halo
            for r in range(0, 56, 8):
                n_ref[:, r : r + 8, dst] = jnp.where(lane < 64, right[:, r : r + 8, :], left[:, r : r + 8, :])
            fr = pl.ds(56 + foff, 8)
            n_ref[:, 56:64, dst] = jnp.where(lane < 64, right[:, fr, :], left[:, fr, :])
            at += 1
            continue
        c, i = where[reads[at]]
        run = 1
        while at + run < blocks and where.get(reads[at + run]) == (c, i + run) and reads[at + run] == reads[at] + run:
            run += 1
        own, q, zq, f = parts[c]
        dst = pl.ds(at * LANES, run * LANES)
        src = pl.ds(i * LANES, run * LANES)
        n_ref[:, 0:8, dst] = zo[:, :, pl.ds(reads[at] * LANES, run * LANES)]
        n_ref[:, 8:24, dst] = zq[:, :, src]
        n_ref[:, 24:40, dst] = own[:, :, src]
        n_ref[:, 40:56, dst] = q[:, :, src]
        n_ref[:, 56:64, dst] = f[:, pl.ds(foff, 8), src]
        at += run

    i = lax.broadcasted_iota(jnp.int32, (64, 256), 0)
    flipped = jnp.where(i < 8, i + 32, jnp.where(i < 24, i + 8, jnp.where(i < 40, i - 24, jnp.where(i < 56, i - 56, i - 80))))
    row = row0 + jnp.where(core == 0, i - 24, flipped)
    total = window_sum(row, height)
    rr[...] = jnp.where(total > 0.0, 1.0 / jnp.where(total > 0.0, total, 1.0), 0.0)
    col = col0 + relcol[...]
    total = window_sum(col, width)
    rc[...] = jnp.where(total > 0.0, 1.0 / jnp.where(total > 0.0, total, 1.0), 0.0)
    cv[...] = jnp.where((col >= 0) & (col < width), 1.0, 0.0)

    for ref in (h1h, h1l, h2h, h2l, h3h, h3l):
        rows = ref.shape[0]
        ref[:, 0:LANES] = jnp.zeros((rows, LANES), jnp.bfloat16)
        ref[:, pl.ds((blocks + 1) * LANES, LANES)] = jnp.zeros((rows, LANES), jnp.bfloat16)

    def tile(j):
        return pl.ds(pl.multiple_of(j * 256, 256), 256)

    def inner(j):
        return pl.ds(pl.multiple_of(j * 256 + LANES, LANES), 256)

    def wide(j):
        return pl.ds(pl.multiple_of(j * 256, 256), 512)

    g1 = (g1h[core], g1l[core])
    g2 = (g2h[core], g2l[core])
    g3 = (g3h[core], g3l[core])

    @pl.loop(0, tiles)
    def _(j):
        scale = rr[...] * rc[0:1, tile(j)]
        for k in range(K):
            dh, dl = split(n_ref[k, :, tile(j)] * scale)
            hh, hl = split(dot3(*g1, dh, dl))
            h1h[48 * k : 48 * k + 48, inner(j)] = hh
            h1l[48 * k : 48 * k + 48, inner(j)] = hl

    @pl.loop(0, tiles)
    def _(j):
        u_ref[...] = dot3(h1h[:, wide(j)], h1l[:, wide(j)], bh[...], bl[...])
        acc = jnp.zeros((48, 256), jnp.float32)
        for k in range(K):
            acc = acc + mix[k] * jnp.log(u_ref[48 * k : 48 * k + 48, :])
        valid = cv[0:1, tile(j)] > 0.0
        index = lax.broadcasted_iota(jnp.int32, (48, 256), 0)
        valid = valid & ((index >= 16) | (outer == 0))
        geo = jnp.exp(acc)
        for k in range(K):
            w = jnp.where(valid, geo / u_ref[48 * k : 48 * k + 48, :], 0.0)
            w_ref[k, :, tile(j)] = w[16:32]
            wh, wl = split(w)
            hh, hl = split(dot3(*g2, wh, wl))
            h2h[32 * k : 32 * k + 32, inner(j)] = hh
            h2l[32 * k : 32 * k + 32, inner(j)] = hl

    zrow = pl.ds(pl.multiple_of(jnp.where(core == 0, 16, 8), 8), 8)
    qrow = pl.ds(pl.multiple_of(jnp.where(core == 0, 40, 48), 8), 8)

    @pl.loop(0, tiles)
    def _(j):
        u_ref[0 : 32 * K, :] = dot3(h2h[:, wide(j)], h2l[:, wide(j)], bh[...], bl[...])
        valid = cv[0:1, tile(j)] > 0.0
        for k in range(K):
            n = jnp.concatenate([n_ref[k, zrow, tile(j)], n_ref[k, 24:40, tile(j)], n_ref[k, qrow, tile(j)]], axis=0)
            d = jnp.where(valid, n / u_ref[32 * k : 32 * k + 32, :], 0.0)
            dh, dl = split(d)
            hh, hl = split(dot3(*g3, dh, dl))
            h3h[16 * k : 16 * k + 16, inner(j)] = hh
            h3l[16 * k : 16 * k + 16, inner(j)] = hl

    @pl.loop(0, tiles)
    def _(j):
        u_ref[0 : 16 * K, :] = dot3(h3h[:, wide(j)], h3l[:, wide(j)], bh[...], bl[...])
        acc = jnp.zeros((16, 256), jnp.float32)
        for k in range(K):
            acc = acc + mix[k] * jnp.log(w_ref[k, :, tile(j)] * u_ref[16 * k : 16 * k + 16, :])
        out[:, tile(j)] = acc


def relative_columns(reads):
    lane = np.arange(LANES)
    cols = [np.where(lane < 64, 4096 + lane, lane - LANES) if b == EDGE else b * LANES + lane for b in reads]
    return np.tile(np.concatenate(cols).astype(np.int32)[None], (8, 1))


def run_kernel(which, sources, height, width, scal, mix, arrays):
    reads = READS[which]
    blocks = len(reads)
    lanes = blocks * LANES
    wide = (blocks + 2) * LANES
    consts = matrices()
    smem = pl.BlockSpec(memory_space=pltpu.SMEM)
    vmem = pl.BlockSpec(memory_space=pltpu.VMEM)
    scratch = [
        pltpu.VMEM((K, 64, lanes), jnp.float32),
        pltpu.VMEM((64, 256), jnp.float32),
        pltpu.VMEM((8, lanes), jnp.float32),
        pltpu.VMEM((8, lanes), jnp.float32),
    ]
    for rows in (48, 32, 16):
        scratch += [pltpu.VMEM((rows * K, wide), jnp.bfloat16)] * 2
    scratch += [pltpu.VMEM((48 * K, 256), jnp.float32), pltpu.VMEM((K, 16, lanes), jnp.float32)]
    return pl.pallas_call(
        functools.partial(kernel, reads, sources, height, width),
        out_shape=jax.ShapeDtypeStruct((16, lanes), jnp.float32),
        in_specs=[smem, smem] + [vmem] * (1 + len(arrays) + len(consts)),
        out_specs=vmem,
        scratch_shapes=scratch,
        name=f"barycenter_{which}",
    )(scal, mix, jnp.asarray(relative_columns(reads)), *arrays, *[jnp.asarray(c) for c in consts])


def blocks_of(x, ids):
    runs, start = [], 0
    for i in range(1, len(ids) + 1):
        if i == len(ids) or ids[i] != ids[i - 1] + 1:
            runs.append(x[..., ids[start] * LANES : (ids[i - 1] + 1) * LANES])
            start = i
    return runs[0] if len(runs) == 1 else jnp.concatenate(runs, axis=-1)


def on_device(counts, weights):
    n_rows, n_cols = lax.axis_size("rows"), lax.axis_size("maps")
    height, width = n_rows * counts.shape[1], n_cols * counts.shape[2]
    r, m = lax.axis_index("rows"), lax.axis_index("maps")
    core = r % 2
    outer = ((r == 0) | (r == n_rows - 1)).astype(jnp.int32)
    scal = jnp.stack([core, outer, r * counts.shape[1], m * counts.shape[2]]).astype(jnp.int32)
    mix = weights / jnp.sum(weights)

    swap = [(i, i ^ 1) for i in range(n_rows)]
    hop = [(i, i + 2) for i in range(0, n_rows - 2, 2)] + [(i, i - 2) for i in range(3, n_rows, 2)]
    to_right = [(i, i + 1) for i in range(n_cols - 1)]
    to_left = [(i + 1, i) for i in range(n_cols - 1)]

    n = counts.astype(jnp.float32) + 1.0
    zo = lax.ppermute(jnp.where(core == 0, n[:, 8:], n[:, :8]), "rows", hop)
    own = [blocks_of(n, ids) for ids in CHUNKS]
    q = [lax.ppermute(x, "rows", swap) for x in own]
    zq = [lax.ppermute(x, "rows", hop) for x in q]
    f = [lax.ppermute(x, "rows", swap) for x in zq]

    sums = jnp.sum(n, axis=(1, 2))
    for axis, size in (("rows", n_rows), ("maps", n_cols)):
        bit = 1
        while bit < size:
            sums = sums + lax.ppermute(sums, axis, [(i, i ^ bit) for i in range(size)])
            bit *= 2
    log_scale = jnp.sum(mix * jnp.log(float(height * width) / sums))

    def column(b):
        i = CHUNKS[0].index(b)
        cols = slice(i * LANES, (i + 1) * LANES)
        return jnp.concatenate(
            [zo[..., b * LANES : (b + 1) * LANES]] + [x[0][..., cols] for x in (zq, own, q, f)], axis=1
        )

    left = lax.ppermute(column(31), "maps", to_right)
    right = lax.ppermute(column(0), "maps", to_left)

    outs = []
    for which, sources in enumerate(((0,), (0, 1), (0, 1, 2))):
        arrays = [zo]
        for c in sources:
            arrays += [own[c], q[c], zq[c], f[c]]
        if EDGE in READS[which]:
            arrays += [left, right]
        outs.append(run_kernel(which, sources, height, width, scal, mix, arrays))
    last = 32 - (SPLIT_B - 2)
    pieces = [
        outs[2][:, (last + 1) * LANES : (last + 2) * LANES],
        outs[0][:, LANES : (SPLIT_A - 1) * LANES],
        outs[1][:, LANES : -LANES],
        outs[2][:, LANES : last * LANES],
    ]
    return jnp.exp(jnp.concatenate(pieces, axis=1) + log_scale)


def solution(mesh):
    return jax.shard_map(
        on_device, mesh=mesh, in_specs=(P(None, "rows", "maps"), P()), out_specs=P("rows", "maps"), check_vma=False
    )
```

profile of v0, /device:TPU:16, one launch (start us, length us, event | category | flops | bytes accessed | tf_op | source)
XLA Modules:
  0.0 249.6 jit_solution(2771390351378753963)
XLA Ops:
  0.0 1.9 convert_add_fusion
  2.1 1.9 collective-permute-start.1
  5.0 2.5 %collective-permute-start.4 = (f32[8,16,1280]{2,1,0:T(8,128)}, f32[8,16,1280]{2,1,0:T(8,128)}, u32[]{:S(2)}, u32[]{:S(2)}) collective-permute-start(f32[8,16,1280]{2,1,0:T(8,128)} %slice.81.refs_5_), channel_id=1, source_target_pairs={{0,8},{8,0},{16,24},{24,16},{32,40},{40,32},{48,56},{56,48},{64,72... | collective-permute-start | bytes 1966088 | tf_op jit(solution)/shard_map/ppermute | solution.py:269
  7.5 3.8 %collective-permute-start.2 = (f32[8,16,1920]{2,1,0:T(8,128)}, f32[8,16,1920]{2,1,0:T(8,128)}, u32[]{:S(2)}, u32[]{:S(2)}) collective-permute-start(f32[8,16,1920]{2,1,0:T(8,128)} %collective-permute-done.1.refs_2_), channel_id=1, source_target_pairs={{0,16},{16,32},{32,48},{48,64},{64,80},{80,96},{96,112},{112,128},... | collective-permute-start | bytes 2949128 | tf_op jit(solution)/shard_map/ppermute | solution.py:270
  12.4 3.8 %collective-permute-start = (f32[8,8,4096]{2,1,0:T(8,128)}, f32[8,8,4096]{2,1,0:T(8,128)}, u32[]{:S(2)}, u32[]{:S(2)}) collective-permute-start(f32[8,8,4096]{2,1,0:T(8,128)} %slice_select_fusion), channel_id=1, source_target_pairs={{0,16},{16,32},{32,48},{48,64},{64,80},{80,96},{96,112},{112,128},... | collective-permute-start | bytes 3145736 | tf_op jit(solution)/shard_map/ppermute | solution.py:267
  16.3 9.0 %collective-permute-start.7 = (f32[8,16,896]{2,1,0:T(8,128)S(1)}, f32[8,16,896]{2,1,0:T(8,128)}, u32[]{:S(2)}, u32[]{:S(2)}) collective-permute-start(f32[8,16,896]{2,1,0:T(8,128)S(1)} %slice.82.refs_9_), channel_id=1, source_target_pairs={{0,8},{8,0},{16,24},{24,16},{32,40},{40,32},{48,56},{56,48},{64,72... | collective-permute-start | bytes 1376264 | tf_op jit(solution)/shard_map/ppermute | solution.py:269
  26.8 3.6 %collective-permute-start.8 = (f32[8,16,896]{2,1,0:T(8,128)}, f32[8,16,896]{2,1,0:T(8,128)}, u32[]{:S(2)}, u32[]{:S(2)}) collective-permute-start(f32[8,16,896]{2,1,0:T(8,128)} %collective-permute-done.7.refs_10_), channel_id=1, source_target_pairs={{0,16},{16,32},{32,48},{48,64},{64,80},{80,96},{96,112},{112,128},... | collective-permute-start | bytes 1376264 | tf_op jit(solution)/shard_map/ppermute | solution.py:270
  32.4 11.1 %collective-permute-done.2.refs_3_ = f32[8,16,1920]{2,1,0:T(8,128)} collective-permute-done((f32[8,16,1920]{2,1,0:T(8,128)}, f32[8,16,1920]{2,1,0:T(8,128)}, u32[]{:S(2)}, u32[]{:S(2)}) %collective-permute-start.2) | collective-permute-done | bytes 983072 | tf_op jit(solution)/shard_map/ppermute | solution.py:270
  45.4 2.4 collective-permute-start.12
  48.4 27.4 %collective-permute-done.8.refs_11_ = f32[8,16,896]{2,1,0:T(8,128)} collective-permute-done((f32[8,16,896]{2,1,0:T(8,128)}, f32[8,16,896]{2,1,0:T(8,128)}, u32[]{:S(2)}, u32[]{:S(2)}) %collective-permute-start.8) | collective-permute-done | bytes 458784 | tf_op jit(solution)/shard_map/ppermute | solution.py:270
  79.1 10.0 %collective-permute-done.5.refs_7_ = f32[8,16,1280]{2,1,0:T(8,128)} collective-permute-done((f32[8,16,1280]{2,1,0:T(8,128)}, f32[8,16,1280]{2,1,0:T(8,128)}, u32[]{:S(2)}, u32[]{:S(2)}) %collective-permute-start.5) | collective-permute-done | bytes 655392 | tf_op jit(solution)/shard_map/ppermute | solution.py:270
  95.6 3.4 %collective-permute-start.10 = (f32[8,72,128]{2,1,0:T(8,128)}, f32[8,72,128]{2,1,0:T(8,128)S(1)}, u32[]{:S(2)}, u32[]{:S(2)}) collective-permute-start(f32[8,72,128]{2,1,0:T(8,128)} %get-tuple-element.14), channel_id=1, source_target_pairs={{0,1},{1,2},{2,3},{3,4},{4,5},{5,6},{6,7},{8,9},{9,10},{10,11},{11... | collective-permute-start | bytes 884744 | tf_op jit(solution)/shard_map/ppermute | solution.py:288
  102.8 3.5 %collective-permute-done.13 = f32[8]{0:T(128)S(1)} collective-permute-done((f32[8]{0:T(128)S(1)}, f32[8]{0:T(128)S(1)}, u32[]{:S(2)}, u32[]{:S(2)}) %collective-permute-start.13) | collective-permute-done | bytes 64 | tf_op jit(solution)/shard_map/ppermute | solution.py:277
  108.3 4.4 %collective-permute-done.14 = f32[8]{0:T(128)S(1)} collective-permute-done((f32[8]{0:T(128)S(1)}, f32[8]{0:T(128)S(1)}, u32[]{:S(2)}, u32[]{:S(2)}) %collective-permute-start.14) | collective-permute-done | bytes 64 | tf_op jit(solution)/shard_map/ppermute | solution.py:277
  114.6 7.4 %collective-permute-done.15 = f32[8]{0:T(128)S(1)} collective-permute-done((f32[8]{0:T(128)S(1)}, f32[8]{0:T(128)S(1)}, u32[]{:S(2)}, u32[]{:S(2)}) %collective-permute-start.15) | collective-permute-done | bytes 64 | tf_op jit(solution)/shard_map/ppermute | solution.py:277
  122.1 3.5 %collective-permute-start.16 = (f32[8]{0:T(128)S(1)}, f32[8]{0:T(128)S(1)}, u32[]{:S(2)}, u32[]{:S(2)}) collective-permute-start(f32[8]{0:T(128)S(1)} %add.49), channel_id=1, source_target_pairs={{0,128},{8,136},{16,144},{24,152},{32,160},{40,168},{48,176},{56,1... | collective-permute-start | bytes 104 | tf_op jit(solution)/shard_map/ppermute | solution.py:277
  125.5 2.0 collective-permute-done.16
  129.4 5.0 %collective-permute-done.17 = f32[8]{0:T(128)S(1)} collective-permute-done((f32[8]{0:T(128)S(1)}, f32[8]{0:T(128)S(1)}, u32[]{:S(2)}, u32[]{:S(2)}) %collective-permute-start.17) | collective-permute-done | bytes 64 | tf_op jit(solution)/shard_map/ppermute | solution.py:277
  134.5 4.5 %collective-permute-start.18 = (f32[8]{0:T(128)S(1)}, f32[8]{0:T(128)S(1)}, u32[]{:S(2)}, u32[]{:S(2)}) collective-permute-start(f32[8]{0:T(128)S(1)} %add.51), channel_id=1, source_target_pairs={{0,1},{1,0},{2,3},{3,2},{4,5},{5,4},{6,7},{7,6},{8,9},{9,8},{10,11... | collective-permute-start | bytes 104 | tf_op jit(solution)/shard_map/ppermute | solution.py:277
  140.6 24.6 %collective-permute-start.19 = (f32[8]{0:T(128)S(1)}, f32[8]{0:T(128)S(1)}, u32[]{:S(2)}, u32[]{:S(2)}) collective-permute-start(f32[8]{0:T(128)S(1)} %add.52), channel_id=1, source_target_pairs={{0,2},{1,3},{2,0},{3,1},{4,6},{5,7},{6,4},{7,5},{8,10},{9,11},{10,... | collective-permute-start | bytes 104 | tf_op jit(solution)/shard_map/ppermute | solution.py:277
  166.7 17.8 %collective-permute-start.20 = (f32[8]{0:T(128)S(1)}, f32[8]{0:T(128)S(1)}, u32[]{:S(2)}, u32[]{:S(2)}) collective-permute-start(f32[8]{0:T(128)S(1)} %add.53), channel_id=1, source_target_pairs={{0,4},{1,5},{2,6},{3,7},{4,0},{5,1},{6,2},{7,3},{8,12},{9,13},{10,... | collective-permute-start | bytes 104 | tf_op jit(solution)/shard_map/ppermute | solution.py:277
  187.8 19.2 %barycenter_0.1 = f32[16,1792]{1,0:T(8,128)} custom-call(s32[4]{0:T(128)} %pad_add_fusion.scal, f32[8]{0:T(128)} %get-tuple-element.6.mix, s32[8,1792]{1,0:T(8,128)} %constant.57.clone.relcol, f32[8,8,4096]{2,1,0:T(8,128)} %collective-permute-done.refs_0_, f32[8,16,1920]{2,1,0:T(8,128)} %copy-done, f32[8,16,1920]{2,1,0:T(8,128)} %collective-permute-done.1.refs_2_, ...), custom_call_target="tpu_custom_call" | custom-call | tf_op jit(solution)/shard_map/barycenter_0/pallas_call | solution.py:233
  207.0 17.6 %barycenter_1.1 = f32[16,1536]{1,0:T(8,128)} custom-call(s32[4]{0:T(128)} %pad_add_fusion.scal, f32[8]{0:T(128)} %get-tuple-element.6.mix, s32[8,1536]{1,0:T(8,128)} %constant.66.clone.relcol, f32[8,8,4096]{2,1,0:T(8,128)} %collective-permute-done.refs_0_, f32[8,16,1920]{2,1,0:T(8,128)} %copy-done, f32[8,16,1920]{2,1,0:T(8,128)} %collective-permute-done.1.refs_2_, ...), custom_call_target="tpu_custom_call" | custom-call | tf_op jit(solution)/shard_map/barycenter_1/pallas_call | solution.py:233
  226.0 20.6 %barycenter_2.1 = f32[16,1792]{1,0:T(8,128)} custom-call(s32[4]{0:T(128)} %pad_add_fusion.scal, f32[8]{0:T(128)} %get-tuple-element.6.mix, s32[8,1792]{1,0:T(8,128)} %constant.67.clone.relcol, f32[8,8,4096]{2,1,0:T(8,128)} %collective-permute-done.refs_0_, f32[8,16,1920]{2,1,0:T(8,128)} %copy-done, f32[8,16,1920]{2,1,0:T(8,128)} %collective-permute-done.1.refs_2_, ...), custom_call_target="tpu_custom_call" | custom-call | tf_op jit(solution)/shard_map/barycenter_2/pallas_call | solution.py:233
  (63 shorter events, 38.2 us)
Async XLA Ops:
  2.1 5.4 %collective-permute-start.1 = (f32[8,16,1920]{2,1,0:T(8,128)S(1)}, f32[8,16,1920]{2,1,0:T(8,128)}, u32[]{:S(2)}, u32[]{:S(2)}) collective-permute-start(f32[8,16,1920]{2,1,0:T(8,128)S(1)} %pad_maximum_fusion.refs_1_), channel_id=1, source_target_pairs={{0,8},{8,0},{16,24},{24,16},{32,40},{40,32},{48,56},{56,48},{64,72... | collective-permute-start | bytes 2949128 | tf_op jit(solution)/shard_map/ppermute | solution.py:269
  5.0 42.9 %copy-start.5 = (f32[8]{0:T(128)S(1)}, f32[8]{0:T(128)}, u32[]{:S(2)}) copy-start(f32[8]{0:T(128)} %param.30) | copy-start | bytes 100
  5.0 25.5 %collective-permute-start.4 = (f32[8,16,1280]{2,1,0:T(8,128)}, f32[8,16,1280]{2,1,0:T(8,128)}, u32[]{:S(2)}, u32[]{:S(2)}) collective-permute-start(f32[8,16,1280]{2,1,0:T(8,128)} %slice.81.refs_5_), channel_id=1, source_target_pairs={{0,8},{8,0},{16,24},{24,16},{32,40},{40,32},{48,56},{56,48},{64,72... | collective-permute-start | bytes 1966088 | tf_op jit(solution)/shard_map/ppermute | solution.py:269
  7.5 36.0 %collective-permute-start.2 = (f32[8,16,1920]{2,1,0:T(8,128)}, f32[8,16,1920]{2,1,0:T(8,128)}, u32[]{:S(2)}, u32[]{:S(2)}) collective-permute-start(f32[8,16,1920]{2,1,0:T(8,128)} %collective-permute-done.1.refs_2_), channel_id=1, source_target_pairs={{0,16},{16,32},{32,48},{48,64},{64,80},{80,96},{96,112},{112,128},... | collective-permute-start | bytes 2949128 | tf_op jit(solution)/shard_map/ppermute | solution.py:270
  12.4 65.3 %collective-permute-start = (f32[8,8,4096]{2,1,0:T(8,128)}, f32[8,8,4096]{2,1,0:T(8,128)}, u32[]{:S(2)}, u32[]{:S(2)}) collective-permute-start(f32[8,8,4096]{2,1,0:T(8,128)} %slice_select_fusion), channel_id=1, source_target_pairs={{0,16},{16,32},{32,48},{48,64},{64,80},{80,96},{96,112},{112,128},... | collective-permute-start | bytes 3145736 | tf_op jit(solution)/shard_map/ppermute | solution.py:267
  16.3 190.7 %copy-start.2 = (f32[8,16,896]{2,1,0:T(8,128)}, f32[8,16,896]{2,1,0:T(8,128)S(1)}, u32[]{:S(2)}) copy-start(f32[8,16,896]{2,1,0:T(8,128)S(1)} %slice.82.refs_9_) | copy-start | bytes 1376260
  16.3 10.5 %collective-permute-start.7 = (f32[8,16,896]{2,1,0:T(8,128)S(1)}, f32[8,16,896]{2,1,0:T(8,128)}, u32[]{:S(2)}, u32[]{:S(2)}) collective-permute-start(f32[8,16,896]{2,1,0:T(8,128)S(1)} %slice.82.refs_9_), channel_id=1, source_target_pairs={{0,8},{8,0},{16,24},{24,16},{32,40},{40,32},{48,56},{56,48},{64,72... | collective-permute-start | bytes 1376264 | tf_op jit(solution)/shard_map/ppermute | solution.py:269
  26.8 49.0 %collective-permute-start.8 = (f32[8,16,896]{2,1,0:T(8,128)}, f32[8,16,896]{2,1,0:T(8,128)}, u32[]{:S(2)}, u32[]{:S(2)}) collective-permute-start(f32[8,16,896]{2,1,0:T(8,128)} %collective-permute-done.7.refs_10_), channel_id=1, source_target_pairs={{0,16},{16,32},{32,48},{48,64},{64,80},{80,96},{96,112},{112,128},... | collective-permute-start | bytes 1376264 | tf_op jit(solution)/shard_map/ppermute | solution.py:270
  30.5 58.7 %collective-permute-start.5 = (f32[8,16,1280]{2,1,0:T(8,128)}, f32[8,16,1280]{2,1,0:T(8,128)}, u32[]{:S(2)}, u32[]{:S(2)}) collective-permute-start(f32[8,16,1280]{2,1,0:T(8,128)} %collective-permute-done.4.refs_6_), channel_id=1, source_target_pairs={{0,16},{16,32},{32,48},{48,64},{64,80},{80,96},{96,112},{112,128},... | collective-permute-start | bytes 1966088 | tf_op jit(solution)/shard_map/ppermute | solution.py:270
  43.5 51.4 %collective-permute-start.3 = (f32[8,16,1920]{2,1,0:T(8,128)}, f32[8,16,1920]{2,1,0:T(8,128)S(1)}, u32[]{:S(2)}, u32[]{:S(2)}) collective-permute-start(f32[8,16,1920]{2,1,0:T(8,128)} %collective-permute-done.2.refs_3_), channel_id=1, source_target_pairs={{0,8},{8,0},{16,24},{24,16},{32,40},{40,32},{48,56},{56,48},{64,72... | collective-permute-start | bytes 2949128 | tf_op jit(solution)/shard_map/ppermute | solution.py:271
  45.4 55.5 %collective-permute-start.12 = (f32[8]{0:T(128)S(1)}, f32[8]{0:T(128)S(1)}, u32[]{:S(2)}, u32[]{:S(2)}) collective-permute-start(f32[8]{0:T(128)S(1)} %get-tuple-element.10), channel_id=1, source_target_pairs={{0,8},{8,0},{16,24},{24,16},{32,40},{40,32},{48,56},{56,48},{64,72... | collective-permute-start | bytes 104 | tf_op jit(solution)/shard_map/ppermute | solution.py:277
  75.8 148.8 %collective-permute-start.9 = (f32[8,16,896]{2,1,0:T(8,128)}, f32[8,16,896]{2,1,0:T(8,128)}, u32[]{:S(2)}, u32[]{:S(2)}) collective-permute-start(f32[8,16,896]{2,1,0:T(8,128)} %collective-permute-done.8.refs_11_), channel_id=1, source_target_pairs={{0,8},{8,0},{16,24},{24,16},{32,40},{40,32},{48,56},{56,48},{64,72... | collective-permute-start | bytes 1376264 | tf_op jit(solution)/shard_map/ppermute | solution.py:271
  89.1 117.8 %collective-permute-start.6 = (f32[8,16,1280]{2,1,0:T(8,128)}, f32[8,16,1280]{2,1,0:T(8,128)}, u32[]{:S(2)}, u32[]{:S(2)}) collective-permute-start(f32[8,16,1280]{2,1,0:T(8,128)} %collective-permute-done.5.refs_7_), channel_id=1, source_target_pairs={{0,8},{8,0},{16,24},{24,16},{32,40},{40,32},{48,56},{56,48},{64,72... | collective-permute-start | bytes 1966088 | tf_op jit(solution)/shard_map/ppermute | solution.py:271
  94.8 92.9 %copy-start.1 = (f32[8,16,1920]{2,1,0:T(8,128)}, f32[8,16,1920]{2,1,0:T(8,128)S(1)}, u32[]{:S(2)}) copy-start(f32[8,16,1920]{2,1,0:T(8,128)S(1)} %collective-permute-done.3.refs_4_) | copy-start | bytes 2949124
  95.6 129.0 %collective-permute-start.10 = (f32[8,72,128]{2,1,0:T(8,128)}, f32[8,72,128]{2,1,0:T(8,128)S(1)}, u32[]{:S(2)}, u32[]{:S(2)}) collective-permute-start(f32[8,72,128]{2,1,0:T(8,128)} %get-tuple-element.14), channel_id=1, source_target_pairs={{0,1},{1,2},{2,3},{3,4},{4,5},{5,6},{6,7},{8,9},{9,10},{10,11},{11... | collective-permute-start | bytes 884744 | tf_op jit(solution)/shard_map/ppermute | solution.py:288
  99.0 125.6 %collective-permute-start.11 = (f32[8,72,128]{2,1,0:T(8,128)}, f32[8,72,128]{2,1,0:T(8,128)S(1)}, u32[]{:S(2)}, u32[]{:S(2)}) collective-permute-start(f32[8,72,128]{2,1,0:T(8,128)} %get-tuple-element.13), channel_id=1, source_target_pairs={{1,0},{2,1},{3,2},{4,3},{5,4},{6,5},{7,6},{9,8},{10,9},{11,10},{12... | collective-permute-start | bytes 884744 | tf_op jit(solution)/shard_map/ppermute | solution.py:289
  100.9 5.5 %collective-permute-start.13 = (f32[8]{0:T(128)S(1)}, f32[8]{0:T(128)S(1)}, u32[]{:S(2)}, u32[]{:S(2)}) collective-permute-start(f32[8]{0:T(128)S(1)} %add.46), channel_id=1, source_target_pairs={{0,16},{8,24},{16,0},{24,8},{32,48},{40,56},{48,32},{56,40},{64,80... | collective-permute-start | bytes 104 | tf_op jit(solution)/shard_map/ppermute | solution.py:277
  106.3 6.3 %collective-permute-start.14 = (f32[8]{0:T(128)S(1)}, f32[8]{0:T(128)S(1)}, u32[]{:S(2)}, u32[]{:S(2)}) collective-permute-start(f32[8]{0:T(128)S(1)} %add.47), channel_id=1, source_target_pairs={{0,32},{8,40},{16,48},{24,56},{32,0},{40,8},{48,16},{56,24},{64,96... | collective-permute-start | bytes 104 | tf_op jit(solution)/shard_map/ppermute | solution.py:277
  112.7 9.4 %collective-permute-start.15 = (f32[8]{0:T(128)S(1)}, f32[8]{0:T(128)S(1)}, u32[]{:S(2)}, u32[]{:S(2)}) collective-permute-start(f32[8]{0:T(128)S(1)} %add.48), channel_id=1, source_target_pairs={{0,64},{8,72},{16,80},{24,88},{32,96},{40,104},{48,112},{56,120},{... | collective-permute-start | bytes 104 | tf_op jit(solution)/shard_map/ppermute | solution.py:277
  122.1 5.5 %collective-permute-start.16 = (f32[8]{0:T(128)S(1)}, f32[8]{0:T(128)S(1)}, u32[]{:S(2)}, u32[]{:S(2)}) collective-permute-start(f32[8]{0:T(128)S(1)} %add.49), channel_id=1, source_target_pairs={{0,128},{8,136},{16,144},{24,152},{32,160},{40,168},{48,176},{56,1... | collective-permute-start | bytes 104 | tf_op jit(solution)/shard_map/ppermute | solution.py:277
  127.5 7.0 %collective-permute-start.17 = (f32[8]{0:T(128)S(1)}, f32[8]{0:T(128)S(1)}, u32[]{:S(2)}, u32[]{:S(2)}) collective-permute-start(f32[8]{0:T(128)S(1)} %add.50), channel_id=1, source_target_pairs={{0,256},{8,264},{16,272},{24,280},{32,288},{40,296},{48,304},{56,3... | collective-permute-start | bytes 104 | tf_op jit(solution)/shard_map/ppermute | solution.py:277
  134.5 6.1 %collective-permute-start.18 = (f32[8]{0:T(128)S(1)}, f32[8]{0:T(128)S(1)}, u32[]{:S(2)}, u32[]{:S(2)}) collective-permute-start(f32[8]{0:T(128)S(1)} %add.51), channel_id=1, source_target_pairs={{0,1},{1,0},{2,3},{3,2},{4,5},{5,4},{6,7},{7,6},{8,9},{9,8},{10,11... | collective-permute-start | bytes 104 | tf_op jit(solution)/shard_map/ppermute | solution.py:277
  140.6 26.2 %collective-permute-start.19 = (f32[8]{0:T(128)S(1)}, f32[8]{0:T(128)S(1)}, u32[]{:S(2)}, u32[]{:S(2)}) collective-permute-start(f32[8]{0:T(128)S(1)} %add.52), channel_id=1, source_target_pairs={{0,2},{1,3},{2,0},{3,1},{4,6},{5,7},{6,4},{7,5},{8,10},{9,11},{10,... | collective-permute-start | bytes 104 | tf_op jit(solution)/shard_map/ppermute | solution.py:277
  166.7 19.3 %collective-permute-start.20 = (f32[8]{0:T(128)S(1)}, f32[8]{0:T(128)S(1)}, u32[]{:S(2)}, u32[]{:S(2)}) collective-permute-start(f32[8]{0:T(128)S(1)} %add.53), channel_id=1, source_target_pairs={{0,4},{1,5},{2,6},{3,7},{4,0},{5,1},{6,2},{7,3},{8,12},{9,13},{10,... | collective-permute-start | bytes 104 | tf_op jit(solution)/shard_map/ppermute | solution.py:277
  (5 other events, 59.1 us)
where the time goes:
time: 251 us; the launch traced here: 250 us
  starting transfers between devices  97.5 us (39%)
  waiting for transfers between devices  77 us (31%)
  Pallas kernels  57.4 us (23%)
  local copies, waits for them, and re-layouts  9.97 us (4%)
  other arithmetic  7.4 us (3%)
    ppermute x9, starting transfers between devices, on_device(): sums = sums + lax.ppermute(sums, axis, [(i, i ^ bit) for i in range(size)])  60.4 us
    pallas_call x3, Pallas kernels, run_kernel(): pl.pallas_call(functools.partial(kernel, reads, sources, height, width),...  57.4 us
    ppermute x3, waiting for transfers between devices, on_device(): zq = [lax.ppermute(x, 'rows', hop) for x in q]  48.4 us
    ppermute x9, waiting for transfers between devices, on_device(): sums = sums + lax.ppermute(sums, axis, [(i, i ^ bit) for i in range(size)])  27 us
    ppermute x3, starting transfers between devices, on_device(): q = [lax.ppermute(x, 'rows', swap) for x in own]  13.4 us
    ppermute x3, starting transfers between devices, on_device(): zq = [lax.ppermute(x, 'rows', hop) for x in q]  9.38 us
    unnamed x16, local copies, waits for them, and re-layouts  6.63 us
    ppermute x3, starting transfers between devices, on_device(): f = [lax.ppermute(x, 'rows', swap) for x in zq]  5.73 us
  transfers between devices with their start and end apart: 21, of which 12 were waited for; matrix products, arithmetic and copies ran while one was open for 4% of the time, Pallas kernels for 15%

commit v1 on v0

v1 whole, which is shorter than its diff:
```python
import functools

import jax
import jax.numpy as jnp
import numpy as np
from jax import lax
from jax.experimental import pallas as pl
from jax.experimental.pallas import tpu as pltpu
from jax.sharding import PartitionSpec as P


HALF = 8
K = 8
LANES = 128
EDGE = -1

FIRST, SECOND = 12, 23
CHUNKS = (
    (29, 30, 31) + tuple(range(FIRST)),
    tuple(range(FIRST, SECOND)),
    tuple(range(SECOND, 29)),
)
KERNELS = (
    (tuple(range(FIRST)), (0,)),
    ((29, 30, 31, EDGE, 0, 1), (0,)),
    (tuple(range(FIRST - 3, SECOND)), (0, 1)),
    (tuple(range(SECOND - 2, 31)), (0, 1, 2)),
)
KEPT = (
    ((1, FIRST - 2),),
    ((30, 31), (0, 0)),
    ((FIRST - 1, SECOND - 2),),
    ((SECOND - 1, 29),),
)


def taps():
    spread = 0.45 * HALF
    a = np.arange(-HALF, HALF + 1, dtype=np.float64)
    g = np.exp(-a * a / (2.0 * spread * spread))
    return g / g.sum()


def band(out_pos, in_pos):
    g = taps()
    d = np.asarray(in_pos)[None, :] - np.asarray(out_pos)[:, None]
    return np.where(np.abs(d) <= HALF, g[np.clip(d + HALF, 0, 2 * HALF)], 0.0)


def split_np(x):
    x = np.asarray(x, np.float32)
    hi = x.astype(jnp.bfloat16)
    lo = (x - hi.astype(np.float32)).astype(jnp.bfloat16)
    return hi, lo


def positions(core):
    own = np.arange(16)
    if core == 0:
        zo, zq, q, f = np.arange(-24, -16), np.arange(-16, 0), np.arange(16, 32), np.arange(32, 40)
        z8, q8 = np.arange(-8, 0), np.arange(16, 24)
    else:
        zo, zq, q, f = np.arange(32, 40), np.arange(16, 32), np.arange(-16, 0), np.arange(-24, -16)
        z8, q8 = np.arange(16, 24), np.arange(-8, 0)
    return np.concatenate([zo, zq, own, q, f]), np.concatenate([zq, own, q]), np.concatenate([z8, own, q8]), own


def matrices():
    out = []
    for s in range(3):
        both = [split_np(band(positions(c)[s + 1], positions(c)[s])) for c in (0, 1)]
        out.append(np.stack([np.concatenate([h, l, h], axis=1) for h, l in both]))
    near = split_np(band(np.arange(256), np.arange(256)).T)
    lane = np.arange(LANES)
    far = split_np(band(np.arange(256), np.where(lane < 64, 256 + lane, lane - LANES)).T)
    out.append(np.concatenate([near[0], near[0], near[1], far[0], far[0], far[1]], axis=0))
    return out


def split(x):
    hi = x.astype(jnp.bfloat16)
    lo = (x - hi.astype(jnp.float32)).astype(jnp.bfloat16)
    return hi, lo


def dot(a, b):
    return jnp.dot(a, b, preferred_element_type=jnp.float32)


def row_pass(g, x):
    hi, lo = split(x)
    return split(dot(g, jnp.concatenate([hi, hi, lo], axis=0)))


def window_sum(pos, size):
    g = taps()
    total = jnp.zeros(pos.shape, jnp.float32)
    for i, a in enumerate(range(-HALF, HALF + 1)):
        total = total + jnp.where((pos + a >= 0) & (pos + a < size), np.float32(g[i]), np.float32(0.0))
    return total


def copies(reads, foff, zo, parts, n_ref):
    where = {b: (c, i) for c, ids in enumerate(CHUNKS) for i, b in enumerate(ids)}
    out = []
    at = 0
    while at < len(reads):
        if reads[at] == EDGE:
            at += 1
            continue
        c, i = where[reads[at]]
        run = 1
        while at + run < len(reads) and reads[at + run] == reads[at] + run and where[reads[at + run]] == (c, i + run):
            run += 1
        own, q, zq, f = parts[c]
        dst = pl.ds(at * LANES, run * LANES)
        src = pl.ds(i * LANES, run * LANES)
        out += [
            (zo.at[:, :, pl.ds(reads[at] * LANES, run * LANES)], n_ref.at[:, pl.ds(0, 8), dst]),
            (zq.at[:, :, src], n_ref.at[:, pl.ds(8, 16), dst]),
            (own.at[:, :, src], n_ref.at[:, pl.ds(24, 16), dst]),
            (q.at[:, :, src], n_ref.at[:, pl.ds(40, 16), dst]),
            (f.at[:, pl.ds(foff, 8), src], n_ref.at[:, pl.ds(56, 8), dst]),
        ]
        at += run
    return out


def count_copies(reads, sources):
    class Fake:
        at = property(lambda self: self)

        def __getitem__(self, _):
            return self

    x = Fake()
    return len(copies(reads, 0, x, {c: (x,) * 4 for c in sources}, x))


def kernel(reads, sources, joins, height, width, scal, mix, relcol, *refs):
    n_in = 1 + 4 * len(sources) + (2 if EDGE in reads else 0)
    zo = refs[0]
    parts = {c: refs[1 + 4 * i : 5 + 4 * i] for i, c in enumerate(sources)}
    halo = refs[1 + 4 * len(sources) : n_in]
    g1, g2, g3, bm = refs[n_in : n_in + 4]
    n_in += 4
    if joins:
        log_scale, earlier = refs[n_in], refs[n_in + 1 : n_in + len(joins)]
        n_in += len(joins)
    out = refs[n_in]
    n_ref, rr, rc, cv, h1h, h1l, h2h, h2l, h3h, h3l, u_ref, w_ref, sems = refs[n_in + 1 :][:13]
    acc_ref = refs[-1] if joins else out
    blocks = len(reads)
    tiles = blocks // 2
    core, outer, row0, col0 = scal[0], scal[1], scal[2], scal[3]
    foff = pl.multiple_of(core * 8, 8)

    moves = [
        pltpu.make_async_copy(src, dst, sems.at[i])
        for i, (src, dst) in enumerate(copies(reads, foff, zo, parts, n_ref))
    ]
    for move in moves:
        move.start()

    i = lax.broadcasted_iota(jnp.int32, (64, 256), 0)
    flipped = jnp.where(i < 8, i + 32, jnp.where(i < 24, i + 8, jnp.where(i < 40, i - 24, jnp.where(i < 56, i - 56, i - 80))))
    row = row0 + jnp.where(core == 0, i - 24, flipped)
    total = window_sum(row, height)
    rr[...] = jnp.where(total > 0.0, 1.0 / jnp.where(total > 0.0, total, 1.0), 0.0)
    col = col0 + relcol[...]
    total = window_sum(col, width)
    rc[...] = jnp.where(total > 0.0, 1.0 / jnp.where(total > 0.0, total, 1.0), 0.0)
    cv[...] = jnp.where((col >= 0) & (col < width), 1.0, 0.0)

    for ref in (h1h, h1l, h2h, h2l, h3h, h3l):
        rows = ref.shape[0]
        ref[:, 0:LANES] = jnp.zeros((rows, LANES), jnp.bfloat16)
        ref[:, pl.ds((blocks + 1) * LANES, LANES)] = jnp.zeros((rows, LANES), jnp.bfloat16)

    if EDGE in reads:
        dst = pl.ds(reads.index(EDGE) * LANES, LANES)
        lane = lax.broadcasted_iota(jnp.int32, (K, 8, LANES), 2)
        left, right = halo
        for r in range(0, 56, 8):
            n_ref[:, r : r + 8, dst] = jnp.where(lane < 64, right[:, r : r + 8, :], left[:, r : r + 8, :])
        fr = pl.ds(56 + foff, 8)
        n_ref[:, 56:64, dst] = jnp.where(lane < 64, right[:, fr, :], left[:, fr, :])

    for move in moves:
        move.wait()

    def tile(j):
        return pl.ds(pl.multiple_of(j * 256, 256), 256)

    def at(j, shift, size):
        return pl.ds(pl.multiple_of(j * 256 + shift, LANES), size)

    def column_pass(high, low, j):
        rows = high.shape[0]
        first = lax.broadcasted_iota(jnp.int32, (rows, LANES), 1) < 64
        mh, ml = high[:, at(j, LANES, 256)], low[:, at(j, LANES, 256)]
        eh = jnp.where(first, high[:, at(j, 3 * LANES, LANES)], high[:, at(j, 0, LANES)])
        el = jnp.where(first, low[:, at(j, 3 * LANES, LANES)], low[:, at(j, 0, LANES)])
        return dot(jnp.concatenate([mh, ml, mh, eh, el, eh], axis=1), bm[...])

    @pl.loop(0, tiles)
    def _(j):
        scale = rr[...] * rc[0:1, tile(j)]
        for k in range(K):
            hh, hl = row_pass(g1[core], n_ref[k, :, tile(j)] * scale)
            h1h[48 * k : 48 * k + 48, at(j, LANES, 256)] = hh
            h1l[48 * k : 48 * k + 48, at(j, LANES, 256)] = hl

    @pl.loop(0, tiles)
    def _(j):
        u_ref[...] = column_pass(h1h, h1l, j)
        acc = jnp.zeros((48, 256), jnp.float32)
        for k in range(K):
            acc = acc + mix[k] * jnp.log(u_ref[48 * k : 48 * k + 48, :])
        valid = cv[0:1, tile(j)] > 0.0
        index = lax.broadcasted_iota(jnp.int32, (48, 256), 0)
        valid = valid & ((index >= 16) | (outer == 0))
        geo = jnp.exp(acc)
        for k in range(K):
            w = jnp.where(valid, geo / u_ref[48 * k : 48 * k + 48, :], 0.0)
            w_ref[k, :, tile(j)] = w[16:32]
            hh, hl = row_pass(g2[core], w)
            h2h[32 * k : 32 * k + 32, at(j, LANES, 256)] = hh
            h2l[32 * k : 32 * k + 32, at(j, LANES, 256)] = hl

    zrow = pl.ds(pl.multiple_of(jnp.where(core == 0, 16, 8), 8), 8)
    qrow = pl.ds(pl.multiple_of(jnp.where(core == 0, 40, 48), 8), 8)

    @pl.loop(0, tiles)
    def _(j):
        u_ref[0 : 32 * K, :] = column_pass(h2h, h2l, j)
        valid = cv[0:1, tile(j)] > 0.0
        for k in range(K):
            n = jnp.concatenate([n_ref[k, zrow, tile(j)], n_ref[k, 24:40, tile(j)], n_ref[k, qrow, tile(j)]], axis=0)
            d = jnp.where(valid, n / u_ref[32 * k : 32 * k + 32, :], 0.0)
            hh, hl = row_pass(g3[core], d)
            h3h[16 * k : 16 * k + 16, at(j, LANES, 256)] = hh
            h3l[16 * k : 16 * k + 16, at(j, LANES, 256)] = hl

    @pl.loop(0, tiles)
    def _(j):
        u_ref[0 : 16 * K, :] = column_pass(h3h, h3l, j)
        acc = jnp.zeros((16, 256), jnp.float32)
        for k in range(K):
            acc = acc + mix[k] * jnp.log(w_ref[k, :, tile(j)] * u_ref[16 * k : 16 * k + 16, :])
        acc_ref[:, tile(j)] = acc

    for i, moved in enumerate(joins):
        ref = acc_ref if i == len(joins) - 1 else earlier[i]
        for src, dst, count in moved:
            piece = ref[:, src * LANES : (src + count) * LANES] + log_scale[0]
            out[:, dst * LANES : (dst + count) * LANES] = jnp.exp(piece)


def relative_columns(reads):
    lane = np.arange(LANES)
    cols = [np.where(lane < 64, 4096 + lane, lane - LANES) if b == EDGE else b * LANES + lane for b in reads]
    return np.tile(np.concatenate(cols).astype(np.int32)[None], (8, 1))


def run_kernel(which, height, width, scal, mix, arrays, earlier, log_scale):
    reads, sources = KERNELS[which]
    blocks = len(reads)
    lanes = blocks * LANES
    wide = (blocks + 2) * LANES
    consts = matrices()
    smem = pl.BlockSpec(memory_space=pltpu.SMEM)
    vmem = pl.BlockSpec(memory_space=pltpu.VMEM)
    anywhere = pl.BlockSpec(memory_space=pl.ANY)
    halos = 2 if EDGE in reads else 0
    scratch = [
        pltpu.VMEM((K, 64, lanes), jnp.float32),
        pltpu.VMEM((64, 256), jnp.float32),
        pltpu.VMEM((8, lanes), jnp.float32),
        pltpu.VMEM((8, lanes), jnp.float32),
    ]
    for rows in (48, 32, 16):
        scratch += [pltpu.VMEM((rows * K, wide), jnp.bfloat16)] * 2
    scratch += [
        pltpu.VMEM((48 * K, 256), jnp.float32),
        pltpu.VMEM((K, 16, lanes), jnp.float32),
        pltpu.SemaphoreType.DMA((count_copies(reads, sources),)),
    ]
    in_specs = [smem, smem, vmem] + [anywhere] * (len(arrays) - halos) + [vmem] * (halos + len(consts))
    args = [scal, mix, jnp.asarray(relative_columns(reads)), *arrays, *[jnp.asarray(c) for c in consts]]
    joins = ()
    if earlier:
        joins = tuple(
            tuple((KERNELS[i][0].index(lo), lo, hi - lo + 1) for lo, hi in kept) for i, kept in enumerate(KEPT)
        )
        in_specs += [smem] + [vmem] * len(earlier)
        args += [log_scale.reshape(1), *earlier]
        scratch.append(pltpu.VMEM((16, lanes), jnp.float32))
    return pl.pallas_call(
        functools.partial(kernel, reads, sources, joins, height, width),
        out_shape=jax.ShapeDtypeStruct((16, 32 * LANES if earlier else lanes), jnp.float32),
        in_specs=in_specs,
        out_specs=vmem,
        scratch_shapes=scratch,
    )(*args)


def blocks_of(x, ids):
    runs, start = [], 0
    for i in range(1, len(ids) + 1):
        if i == len(ids) or ids[i] != ids[i - 1] + 1:
            runs.append(x[..., ids[start] * LANES : (ids[i - 1] + 1) * LANES])
            start = i
    return runs[0] if len(runs) == 1 else jnp.concatenate(runs, axis=-1)


def on_device(counts, weights):
    n_rows, n_cols = lax.axis_size("rows"), lax.axis_size("maps")
    height, width = n_rows * counts.shape[1], n_cols * counts.shape[2]
    r, m = lax.axis_index("rows"), lax.axis_index("maps")
    core = r % 2
    outer = ((r == 0) | (r == n_rows - 1)).astype(jnp.int32)
    scal = jnp.stack([core, outer, r * counts.shape[1], m * counts.shape[2]]).astype(jnp.int32)
    mix = weights / jnp.sum(weights)

    swap = [(i, i ^ 1) for i in range(n_rows)]
    hop = [(i, i + 2) for i in range(0, n_rows - 2, 2)] + [(i, i - 2) for i in range(3, n_rows, 2)]
    to_right = [(i, i + 1) for i in range(n_cols - 1)]
    to_left = [(i + 1, i) for i in range(n_cols - 1)]

    def after(x, *deps):
        return lax.optimization_barrier((x,) + deps)[0]

    def to_float(x):
        return x.astype(jnp.float32) + 1.0

    zo_own = to_float(lax.dynamic_slice_in_dim(counts, (1 - core) * 8, 8, axis=1))
    zo = lax.ppermute(zo_own, "rows", hop)
    n = to_float(after(counts, zo_own))
    own = [blocks_of(n, ids) for ids in CHUNKS]
    q = [lax.ppermute(x, "rows", swap) for x in own]
    zq = [lax.ppermute(x, "rows", hop) for x in q]

    sums = jnp.sum(n, axis=(1, 2))
    step = 0
    for axis, size in (("rows", n_rows), ("maps", n_cols)):
        bit = 1
        while bit < size:
            sums = sums + lax.ppermute(sums, axis, [(i, i ^ bit) for i in range(size)])
            bit, step = bit * 2, step + 1
    log_scale = jnp.sum(mix * jnp.log(float(height * width) / sums))

    f = [lax.ppermute(x, "rows", swap) for x in zq]

    def column(b):
        i = CHUNKS[0].index(b)
        cols = slice(i * LANES, (i + 1) * LANES)
        return jnp.concatenate(
            [zo[..., b * LANES : (b + 1) * LANES]] + [x[0][..., cols] for x in (zq, own, q, f)], axis=1
        )

    left = lax.ppermute(column(31), "maps", to_right)
    right = lax.ppermute(column(0), "maps", to_left)

    outs = []
    for which in range(len(KERNELS)):
        arrays = [zo]
        for c in KERNELS[which][1]:
            arrays += [own[c], q[c], zq[c], f[c]]
        if EDGE in KERNELS[which][0]:
            arrays += [left, right]
        earlier = outs if which == len(KERNELS) - 1 else []
        outs.append(run_kernel(which, height, width, scal, mix, arrays, earlier, log_scale))
    return outs[-1]


def solution(mesh):
    return jax.shard_map(
        on_device, mesh=mesh, in_specs=(P(None, "rows", "maps"), P()), out_specs=P("rows", "maps"), check_vma=False
    )
```

time: 251 us -> 249 us (level)
  the two profiles are of different devices: /device:TPU:16 before, /device:TPU:8 now
where the time goes in v1:
time: 249 us; the launch traced here: 248 us
  starting transfers between devices  98.1 us (39%)
  waiting for transfers between devices  80.3 us (32%)
  Pallas kernels  56.7 us (23%)
  local copies, waits for them, and re-layouts  6.24 us (3%)
  other arithmetic  6.07 us (2%)
    ppermute x9, starting transfers between devices, on_device(): sums = sums + lax.ppermute(sums, axis, [(i, i ^ bit) for i in range(size)])  59.9 us
    pallas_call x4, Pallas kernels, run_kernel(): pl.pallas_call(functools.partial(kernel, reads, sources, joins, height, w...  56.7 us
    ppermute x3, waiting for transfers between devices, on_device(): zq = [lax.ppermute(x, 'rows', hop) for x in q]  54.1 us
    ppermute x9, waiting for transfers between devices, on_device(): sums = sums + lax.ppermute(sums, axis, [(i, i ^ bit) for i in range(size)])  26.1 us
    ppermute x3, starting transfers between devices, on_device(): q = [lax.ppermute(x, 'rows', swap) for x in own]  13.4 us
    ppermute x3, starting transfers between devices, on_device(): zq = [lax.ppermute(x, 'rows', hop) for x in q]  9.38 us
    ppermute x3, starting transfers between devices, on_device(): f = [lax.ppermute(x, 'rows', swap) for x in zq]  6.22 us
  transfers between devices with their start and end apart: 21, of which 10 were waited for; matrix products, arithmetic and copies ran while one was open for 4% of the time, Pallas kernels for 17%

profile of v1, /device:TPU:8, one launch (start us, length us, event | category | flops | bytes accessed | tf_op | source)
XLA Modules:
  0.0 247.8 jit_solution(6958682350054146405)
XLA Ops:
  0.0 2.5 convert_add_fusion.1
  5.1 2.4 collective-permute-start.4
  7.5 3.8 %collective-permute-start.2 = (f32[8,16,1920]{2,1,0:T(8,128)S(1)}, f32[8,16,1920]{2,1,0:T(8,128)}, u32[]{:S(2)}, u32[]{:S(2)}) collective-permute-start(f32[8,16,1920]{2,1,0:T(8,128)S(1)} %collective-permute-done.1.refs_2_), channel_id=1, source_target_pairs={{0,16},{16,32},{32,48},{48,64},{64,80},{80,96},{96,112},{112,128},... | collective-permute-start | bytes 2949128 | tf_op jit(solution)/shard_map/ppermute | solution.py:342
  11.3 3.8 %collective-permute-start = (f32[8,8,4096]{2,1,0:T(8,128)}, f32[8,8,4096]{2,1,0:T(8,128)S(1)}, u32[]{:S(2)}, u32[]{:S(2)}) collective-permute-start(f32[8,8,4096]{2,1,0:T(8,128)} %convert_add_fusion.1), channel_id=1, source_target_pairs={{0,16},{16,32},{32,48},{48,64},{64,80},{80,96},{96,112},{112,128},... | collective-permute-start | bytes 3145736 | tf_op jit(solution)/shard_map/ppermute | solution.py:338
  15.2 9.1 %collective-permute-start.7 = (f32[8,16,768]{2,1,0:T(8,128)S(1)}, f32[8,16,768]{2,1,0:T(8,128)}, u32[]{:S(2)}, u32[]{:S(2)}) collective-permute-start(f32[8,16,768]{2,1,0:T(8,128)S(1)} %slice.61.refs_9_), channel_id=1, source_target_pairs={{0,8},{8,0},{16,24},{24,16},{32,40},{40,32},{48,56},{56,48},{64,72... | collective-permute-start | bytes 1179656 | tf_op jit(solution)/shard_map/ppermute | solution.py:341
  24.3 3.6 %collective-permute-start.5 = (f32[8,16,1408]{2,1,0:T(8,128)}, f32[8,16,1408]{2,1,0:T(8,128)}, u32[]{:S(2)}, u32[]{:S(2)}) collective-permute-start(f32[8,16,1408]{2,1,0:T(8,128)} %collective-permute-done.4.refs_6_), channel_id=1, source_target_pairs={{0,16},{16,32},{32,48},{48,64},{64,80},{80,96},{96,112},{112,128},... | collective-permute-start | bytes 2162696 | tf_op jit(solution)/shard_map/ppermute | solution.py:342
  29.9 13.3 %collective-permute-done.2.refs_3_ = f32[8,16,1920]{2,1,0:T(8,128)} collective-permute-done((f32[8,16,1920]{2,1,0:T(8,128)S(1)}, f32[8,16,1920]{2,1,0:T(8,128)}, u32[]{:S(2)}, u32[]{:S(2)}) %collective-permute-start.2) | collective-permute-done | bytes 983072 | tf_op jit(solution)/shard_map/ppermute | solution.py:342
  45.2 2.4 collective-permute-start.10
  48.3 40.8 %collective-permute-done.8.refs_11_ = f32[8,16,768]{2,1,0:T(8,128)} collective-permute-done((f32[8,16,768]{2,1,0:T(8,128)}, f32[8,16,768]{2,1,0:T(8,128)}, u32[]{:S(2)}, u32[]{:S(2)}) %collective-permute-start.8) | collective-permute-done | bytes 393248 | tf_op jit(solution)/shard_map/ppermute | solution.py:342
  91.7 2.4 collective-permute-start.6
  99.5 4.1 %collective-permute-start.19 = (f32[8,72,128]{2,1,0:T(8,128)}, f32[8,72,128]{2,1,0:T(8,128)}, u32[]{:S(2)}, u32[]{:S(2)}) collective-permute-start(f32[8,72,128]{2,1,0:T(8,128)} %get-tuple-element.16), channel_id=1, source_target_pairs={{0,1},{1,2},{2,3},{3,4},{4,5},{5,6},{6,7},{8,9},{9,10},{10,11},{11... | collective-permute-start | bytes 884744 | tf_op jit(solution)/shard_map/ppermute | solution.py:362
  107.4 3.5 %collective-permute-done.11 = f32[8]{0:T(128)S(1)} collective-permute-done((f32[8]{0:T(128)S(1)}, f32[8]{0:T(128)S(1)}, u32[]{:S(2)}, u32[]{:S(2)}) %collective-permute-start.11) | collective-permute-done | bytes 64 | tf_op jit(solution)/shard_map/ppermute | solution.py:349
  112.8 4.4 %collective-permute-done.12 = f32[8]{0:T(128)S(1)} collective-permute-done((f32[8]{0:T(128)S(1)}, f32[8]{0:T(128)S(1)}, u32[]{:S(2)}, u32[]{:S(2)}) %collective-permute-start.12) | collective-permute-done | bytes 64 | tf_op jit(solution)/shard_map/ppermute | solution.py:349
  119.2 7.5 %collective-permute-done.13 = f32[8]{0:T(128)S(1)} collective-permute-done((f32[8]{0:T(128)S(1)}, f32[8]{0:T(128)S(1)}, u32[]{:S(2)}, u32[]{:S(2)}) %collective-permute-start.13) | collective-permute-done | bytes 64 | tf_op jit(solution)/shard_map/ppermute | solution.py:349
  128.6 3.5 %collective-permute-done.14 = f32[8]{0:T(128)S(1)} collective-permute-done((f32[8]{0:T(128)S(1)}, f32[8]{0:T(128)S(1)}, u32[]{:S(2)}, u32[]{:S(2)}) %collective-permute-start.14) | collective-permute-done | bytes 64 | tf_op jit(solution)/shard_map/ppermute | solution.py:349
  132.2 4.4 %collective-permute-start.15 = (f32[8]{0:T(128)S(1)}, f32[8]{0:T(128)S(1)}, u32[]{:S(2)}, u32[]{:S(2)}) collective-permute-start(f32[8]{0:T(128)S(1)} %add.56), channel_id=1, source_target_pairs={{0,256},{8,264},{16,272},{24,280},{32,288},{40,296},{48,304},{56,3... | collective-permute-start | bytes 104 | tf_op jit(solution)/shard_map/ppermute | solution.py:349
  136.6 2.5 %collective-permute-done.15 = f32[8]{0:T(128)S(1)} collective-permute-done((f32[8]{0:T(128)S(1)}, f32[8]{0:T(128)S(1)}, u32[]{:S(2)}, u32[]{:S(2)}) %collective-permute-start.15) | collective-permute-done | bytes 64 | tf_op jit(solution)/shard_map/ppermute | solution.py:349
  139.1 4.5 %collective-permute-start.16 = (f32[8]{0:T(128)S(1)}, f32[8]{0:T(128)S(1)}, u32[]{:S(2)}, u32[]{:S(2)}) collective-permute-start(f32[8]{0:T(128)S(1)} %add.57), channel_id=1, source_target_pairs={{0,1},{1,0},{2,3},{3,2},{4,5},{5,4},{6,7},{7,6},{8,9},{9,8},{10,11... | collective-permute-start | bytes 104 | tf_op jit(solution)/shard_map/ppermute | solution.py:349
  145.1 23.2 %collective-permute-start.17 = (f32[8]{0:T(128)S(1)}, f32[8]{0:T(128)S(1)}, u32[]{:S(2)}, u32[]{:S(2)}) collective-permute-start(f32[8]{0:T(128)S(1)} %add.58), channel_id=1, source_target_pairs={{0,2},{1,3},{2,0},{3,1},{4,6},{5,7},{6,4},{7,5},{8,10},{9,11},{10,... | collective-permute-start | bytes 104 | tf_op jit(solution)/shard_map/ppermute | solution.py:349
  169.9 17.8 %collective-permute-start.18 = (f32[8]{0:T(128)S(1)}, f32[8]{0:T(128)S(1)}, u32[]{:S(2)}, u32[]{:S(2)}) collective-permute-start(f32[8]{0:T(128)S(1)} %add.59), channel_id=1, source_target_pairs={{0,4},{1,5},{2,6},{3,7},{4,0},{5,1},{6,2},{7,3},{8,12},{9,13},{10,... | collective-permute-start | bytes 104 | tf_op jit(solution)/shard_map/ppermute | solution.py:349
  191.0 15.4 %shard_map.208.refs_18_ = f32[16,1536]{1,0:T(8,128)} custom-call(s32[4]{0:T(128)} %pad_add_fusion.scal, f32[8]{0:T(128)} %get-tuple-element.8.mix, s32[8,1536]{1,0:T(8,128)} %constant.55.clone.relcol, f32[8,8,4096]{2,1,0:T(8,128)} %copy-done.1, f32[8,16,1920]{2,1,0:T(8,128)} %copy-done, f32[8,16,1920]{2,1,0:T(8,128)} %copy-done.2, ...), custom_call_target="tpu_custom_call" | custom-call | tf_op jit(solution)/shard_map/pallas_call | solution.py:299
  206.4 17.8 %shard_map.210.refs_20_ = f32[16,1792]{1,0:T(8,128)} custom-call(s32[4]{0:T(128)} %pad_add_fusion.scal, f32[8]{0:T(128)} %get-tuple-element.8.mix, s32[8,1792]{1,0:T(8,128)} %constant.61.clone.relcol, f32[8,8,4096]{2,1,0:T(8,128)} %copy-done.1, f32[8,16,1920]{2,1,0:T(8,128)} %copy-done, f32[8,16,1920]{2,1,0:T(8,128)} %copy-done.2, ...), custom_call_target="tpu_custom_call" | custom-call | tf_op jit(solution)/shard_map/pallas_call | solution.py:299
  224.2 9.3 %shard_map.209.refs_19_ = f32[16,768]{1,0:T(8,128)} custom-call(s32[4]{0:T(128)} %pad_add_fusion.scal, f32[8]{0:T(128)} %get-tuple-element.8.mix, s32[8,768]{1,0:T(8,128)} %constant.60.clone.relcol, f32[8,8,4096]{2,1,0:T(8,128)} %copy-done.1, f32[8,16,1920]{2,1,0:T(8,128)} %copy-done, f32[8,16,1920]{2,1,0:T(8,128)} %copy-done.2, ...), custom_call_target="tpu_custom_call" | custom-call | tf_op jit(solution)/shard_map/pallas_call | solution.py:299
  233.6 14.3 %shard_map.211 = f32[16,4096]{1,0:T(8,128)} custom-call(s32[4]{0:T(128)} %pad_add_fusion.scal, f32[8]{0:T(128)} %get-tuple-element.8.mix, s32[8,1280]{1,0:T(8,128)} %constant.62.clone.relcol, f32[8,8,4096]{2,1,0:T(8,128)} %copy-done.1, f32[8,16,1920]{2,1,0:T(8,128)} %copy-done, f32[8,16,1920]{2,1,0:T(8,128)} %copy-done.2, ...), custom_call_target="tpu_custom_call" | custom-call | tf_op jit(solution)/shard_map/pallas_call | solution.py:299
  (61 shorter events, 31.1 us)
Async XLA Ops:
  3.0 188.0 %copy-start = (f32[8,16,1920]{2,1,0:T(8,128)}, f32[8,16,1920]{2,1,0:T(8,128)S(1)}, u32[]{:S(2)}) copy-start(f32[8,16,1920]{2,1,0:T(8,128)S(1)} %pad_maximum_fusion.refs_1_) | copy-start | bytes 2949124
  3.1 4.5 %collective-permute-start.1 = (f32[8,16,1920]{2,1,0:T(8,128)S(1)}, f32[8,16,1920]{2,1,0:T(8,128)S(1)}, u32[]{:S(2)}, u32[]{:S(2)}) collective-permute-start(f32[8,16,1920]{2,1,0:T(8,128)S(1)} %pad_maximum_fusion.refs_1_), channel_id=1, source_target_pairs={{0,8},{8,0},{16,24},{24,16},{32,40},{40,32},{48,56},{56,48},{64,72... | collective-permute-start | bytes 2949128 | tf_op jit(solution)/shard_map/ppermute | solution.py:341
  5.1 19.3 %collective-permute-start.4 = (f32[8,16,1408]{2,1,0:T(8,128)S(1)}, f32[8,16,1408]{2,1,0:T(8,128)}, u32[]{:S(2)}, u32[]{:S(2)}) collective-permute-start(f32[8,16,1408]{2,1,0:T(8,128)S(1)} %slice.60.refs_5_), channel_id=1, source_target_pairs={{0,8},{8,0},{16,24},{24,16},{32,40},{40,32},{48,56},{56,48},{64,72... | collective-permute-start | bytes 2162696 | tf_op jit(solution)/shard_map/ppermute | solution.py:341
  7.5 183.5 %copy-start.2 = (f32[8,16,1920]{2,1,0:T(8,128)}, f32[8,16,1920]{2,1,0:T(8,128)S(1)}, u32[]{:S(2)}) copy-start(f32[8,16,1920]{2,1,0:T(8,128)S(1)} %collective-permute-done.1.refs_2_) | copy-start | bytes 2949124
  7.5 35.7 %collective-permute-start.2 = (f32[8,16,1920]{2,1,0:T(8,128)S(1)}, f32[8,16,1920]{2,1,0:T(8,128)}, u32[]{:S(2)}, u32[]{:S(2)}) collective-permute-start(f32[8,16,1920]{2,1,0:T(8,128)S(1)} %collective-permute-done.1.refs_2_), channel_id=1, source_target_pairs={{0,16},{16,32},{32,48},{48,64},{64,80},{80,96},{96,112},{112,128},... | collective-permute-start | bytes 2949128 | tf_op jit(solution)/shard_map/ppermute | solution.py:342
  11.3 79.6 %collective-permute-start = (f32[8,8,4096]{2,1,0:T(8,128)}, f32[8,8,4096]{2,1,0:T(8,128)S(1)}, u32[]{:S(2)}, u32[]{:S(2)}) collective-permute-start(f32[8,8,4096]{2,1,0:T(8,128)} %convert_add_fusion.1), channel_id=1, source_target_pairs={{0,16},{16,32},{32,48},{48,64},{64,80},{80,96},{96,112},{112,128},... | collective-permute-start | bytes 3145736 | tf_op jit(solution)/shard_map/ppermute | solution.py:338
  15.2 209.0 %copy-start.6 = (f32[8,16,768]{2,1,0:T(8,128)}, f32[8,16,768]{2,1,0:T(8,128)S(1)}, u32[]{:S(2)}) copy-start(f32[8,16,768]{2,1,0:T(8,128)S(1)} %slice.61.refs_9_) | copy-start | bytes 1179652
  15.2 12.8 %collective-permute-start.7 = (f32[8,16,768]{2,1,0:T(8,128)S(1)}, f32[8,16,768]{2,1,0:T(8,128)}, u32[]{:S(2)}, u32[]{:S(2)}) collective-permute-start(f32[8,16,768]{2,1,0:T(8,128)S(1)} %slice.61.refs_9_), channel_id=1, source_target_pairs={{0,8},{8,0},{16,24},{24,16},{32,40},{40,32},{48,56},{56,48},{64,72... | collective-permute-start | bytes 1179656 | tf_op jit(solution)/shard_map/ppermute | solution.py:341
  24.3 67.3 %collective-permute-start.5 = (f32[8,16,1408]{2,1,0:T(8,128)}, f32[8,16,1408]{2,1,0:T(8,128)}, u32[]{:S(2)}, u32[]{:S(2)}) collective-permute-start(f32[8,16,1408]{2,1,0:T(8,128)} %collective-permute-done.4.refs_6_), channel_id=1, source_target_pairs={{0,16},{16,32},{32,48},{48,64},{64,80},{80,96},{96,112},{112,128},... | collective-permute-start | bytes 2162696 | tf_op jit(solution)/shard_map/ppermute | solution.py:342
  28.0 61.1 %collective-permute-start.8 = (f32[8,16,768]{2,1,0:T(8,128)}, f32[8,16,768]{2,1,0:T(8,128)}, u32[]{:S(2)}, u32[]{:S(2)}) collective-permute-start(f32[8,16,768]{2,1,0:T(8,128)} %collective-permute-done.7.refs_10_), channel_id=1, source_target_pairs={{0,16},{16,32},{32,48},{48,64},{64,80},{80,96},{96,112},{112,128},... | collective-permute-start | bytes 1179656 | tf_op jit(solution)/shard_map/ppermute | solution.py:342
  43.3 54.6 %collective-permute-start.3 = (f32[8,16,1920]{2,1,0:T(8,128)}, f32[8,16,1920]{2,1,0:T(8,128)}, u32[]{:S(2)}, u32[]{:S(2)}) collective-permute-start(f32[8,16,1920]{2,1,0:T(8,128)} %collective-permute-done.2.refs_3_), channel_id=1, source_target_pairs={{0,8},{8,0},{16,24},{24,16},{32,40},{40,32},{48,56},{56,48},{64,72... | collective-permute-start | bytes 2949128 | tf_op jit(solution)/shard_map/ppermute | solution.py:353
  45.2 60.3 %collective-permute-start.10 = (f32[8]{0:T(128)S(1)}, f32[8]{0:T(128)S(1)}, u32[]{:S(2)}, u32[]{:S(2)}) collective-permute-start(f32[8]{0:T(128)S(1)} %get-tuple-element.12), channel_id=1, source_target_pairs={{0,8},{8,0},{16,24},{24,16},{32,40},{40,32},{48,56},{56,48},{64,72... | collective-permute-start | bytes 104 | tf_op jit(solution)/shard_map/ppermute | solution.py:349
  89.1 144.5 %collective-permute-start.9 = (f32[8,16,768]{2,1,0:T(8,128)}, f32[8,16,768]{2,1,0:T(8,128)}, u32[]{:S(2)}, u32[]{:S(2)}) collective-permute-start(f32[8,16,768]{2,1,0:T(8,128)} %collective-permute-done.8.refs_11_), channel_id=1, source_target_pairs={{0,8},{8,0},{16,24},{24,16},{32,40},{40,32},{48,56},{56,48},{64,72... | collective-permute-start | bytes 1179656 | tf_op jit(solution)/shard_map/ppermute | solution.py:353
  91.7 114.8 %collective-permute-start.6 = (f32[8,16,1408]{2,1,0:T(8,128)}, f32[8,16,1408]{2,1,0:T(8,128)}, u32[]{:S(2)}, u32[]{:S(2)}) collective-permute-start(f32[8,16,1408]{2,1,0:T(8,128)} %collective-permute-done.5.refs_7_), channel_id=1, source_target_pairs={{0,8},{8,0},{16,24},{24,16},{32,40},{40,32},{48,56},{56,48},{64,72... | collective-permute-start | bytes 2162696 | tf_op jit(solution)/shard_map/ppermute | solution.py:353
  99.5 124.8 %collective-permute-start.19 = (f32[8,72,128]{2,1,0:T(8,128)}, f32[8,72,128]{2,1,0:T(8,128)}, u32[]{:S(2)}, u32[]{:S(2)}) collective-permute-start(f32[8,72,128]{2,1,0:T(8,128)} %get-tuple-element.16), channel_id=1, source_target_pairs={{0,1},{1,2},{2,3},{3,4},{4,5},{5,6},{6,7},{8,9},{9,10},{10,11},{11... | collective-permute-start | bytes 884744 | tf_op jit(solution)/shard_map/ppermute | solution.py:362
  103.6 120.7 %collective-permute-start.20 = (f32[8,72,128]{2,1,0:T(8,128)}, f32[8,72,128]{2,1,0:T(8,128)}, u32[]{:S(2)}, u32[]{:S(2)}) collective-permute-start(f32[8,72,128]{2,1,0:T(8,128)} %get-tuple-element.15), channel_id=1, source_target_pairs={{1,0},{2,1},{3,2},{4,3},{5,4},{6,5},{7,6},{9,8},{10,9},{11,10},{12... | collective-permute-start | bytes 884744 | tf_op jit(solution)/shard_map/ppermute | solution.py:363
  105.5 5.5 %collective-permute-start.11 = (f32[8]{0:T(128)S(1)}, f32[8]{0:T(128)S(1)}, u32[]{:S(2)}, u32[]{:S(2)}) collective-permute-start(f32[8]{0:T(128)S(1)} %add.52), channel_id=1, source_target_pairs={{0,16},{8,24},{16,0},{24,8},{32,48},{40,56},{48,32},{56,40},{64,80... | collective-permute-start | bytes 104 | tf_op jit(solution)/shard_map/ppermute | solution.py:349
  110.9 6.3 %collective-permute-start.12 = (f32[8]{0:T(128)S(1)}, f32[8]{0:T(128)S(1)}, u32[]{:S(2)}, u32[]{:S(2)}) collective-permute-start(f32[8]{0:T(128)S(1)} %add.53), channel_id=1, source_target_pairs={{0,32},{8,40},{16,48},{24,56},{32,0},{40,8},{48,16},{56,24},{64,96... | collective-permute-start | bytes 104 | tf_op jit(solution)/shard_map/ppermute | solution.py:349
  117.3 9.4 %collective-permute-start.13 = (f32[8]{0:T(128)S(1)}, f32[8]{0:T(128)S(1)}, u32[]{:S(2)}, u32[]{:S(2)}) collective-permute-start(f32[8]{0:T(128)S(1)} %add.54), channel_id=1, source_target_pairs={{0,64},{8,72},{16,80},{24,88},{32,96},{40,104},{48,112},{56,120},{... | collective-permute-start | bytes 104 | tf_op jit(solution)/shard_map/ppermute | solution.py:349
  126.7 5.5 %collective-permute-start.14 = (f32[8]{0:T(128)S(1)}, f32[8]{0:T(128)S(1)}, u32[]{:S(2)}, u32[]{:S(2)}) collective-permute-start(f32[8]{0:T(128)S(1)} %add.55), channel_id=1, source_target_pairs={{0,128},{8,136},{16,144},{24,152},{32,160},{40,168},{48,176},{56,1... | collective-permute-start | bytes 104 | tf_op jit(solution)/shard_map/ppermute | solution.py:349
  132.2 7.0 %collective-permute-start.15 = (f32[8]{0:T(128)S(1)}, f32[8]{0:T(128)S(1)}, u32[]{:S(2)}, u32[]{:S(2)}) collective-permute-start(f32[8]{0:T(128)S(1)} %add.56), channel_id=1, source_target_pairs={{0,256},{8,264},{16,272},{24,280},{32,288},{40,296},{48,304},{56,3... | collective-permute-start | bytes 104 | tf_op jit(solution)/shard_map/ppermute | solution.py:349
  139.1 6.0 %collective-permute-start.16 = (f32[8]{0:T(128)S(1)}, f32[8]{0:T(128)S(1)}, u32[]{:S(2)}, u32[]{:S(2)}) collective-permute-start(f32[8]{0:T(128)S(1)} %add.57), channel_id=1, source_target_pairs={{0,1},{1,0},{2,3},{3,2},{4,5},{5,4},{6,7},{7,6},{8,9},{9,8},{10,11... | collective-permute-start | bytes 104 | tf_op jit(solution)/shard_map/ppermute | solution.py:349
  145.1 24.7 %collective-permute-start.17 = (f32[8]{0:T(128)S(1)}, f32[8]{0:T(128)S(1)}, u32[]{:S(2)}, u32[]{:S(2)}) collective-permute-start(f32[8]{0:T(128)S(1)} %add.58), channel_id=1, source_target_pairs={{0,2},{1,3},{2,0},{3,1},{4,6},{5,7},{6,4},{7,5},{8,10},{9,11},{10,... | collective-permute-start | bytes 104 | tf_op jit(solution)/shard_map/ppermute | solution.py:349
  169.9 19.3 %collective-permute-start.18 = (f32[8]{0:T(128)S(1)}, f32[8]{0:T(128)S(1)}, u32[]{:S(2)}, u32[]{:S(2)}) collective-permute-start(f32[8]{0:T(128)S(1)} %add.59), channel_id=1, source_target_pairs={{0,4},{1,5},{2,6},{3,7},{4,0},{5,1},{6,2},{7,3},{8,12},{9,13},{10,... | collective-permute-start | bytes 104 | tf_op jit(solution)/shard_map/ppermute | solution.py:349
  (5 other events, 197.7 us)

commit v2 on v1

--- a/solution.py
+++ b/solution.py
@@ -100,41 +100,66 @@
     return total
 
 
-def copies(reads, foff, zo, parts, n_ref):
+def copies(reads, foff, zo, parts, halo, n_ref):
     where = {b: (c, i) for c, ids in enumerate(CHUNKS) for i, b in enumerate(ids)}
     out = []
-    at = 0
-    while at < len(reads):
-        if reads[at] == EDGE:
-            at += 1
-            continue
-        c, i = where[reads[at]]
-        run = 1
-        while at + run < len(reads) and reads[at + run] == reads[at] + run and where[reads[at + run]] == (c, i + run):
-            run += 1
-        own, q, zq, f = parts[c]
-        dst = pl.ds(at * LANES, run * LANES)
-        src = pl.ds(i * LANES, run * LANES)
-        out += [
-            (zo.at[:, :, pl.ds(reads[at] * LANES, run * LANES)], n_ref.at[:, pl.ds(0, 8), dst]),
-            (zq.at[:, :, src], n_ref.at[:, pl.ds(8, 16), dst]),
-            (own.at[:, :, src], n_ref.at[:, pl.ds(24, 16), dst]),
-            (q.at[:, :, src], n_ref.at[:, pl.ds(40, 16), dst]),
-            (f.at[:, pl.ds(foff, 8), src], n_ref.at[:, pl.ds(56, 8), dst]),
+    for at in range(0, len(reads), 2):
+        pair = reads[at : at + 2]
+        joined = EDGE not in pair and pair[1] == pair[0] + 1 and where[pair[1]] == (where[pair[0]][0], where[pair[0]][1] + 1)
+        tile = []
+        for i, b in enumerate(pair[:1] if joined else pair):
+            size = (2 if joined else 1) * LANES
+            dst = pl.ds((at + i) * LANES, size)
+            if b == EDGE:
+                tile.append((halo[1], n_ref.at[:, :, dst]))
+                continue
+            c, place = where[b]
+            own, q, zq, f = parts[c]
+            src = pl.ds(place * LANES, size)
+            tile += [
+                (zo.at[:, :, pl.ds(b * LANES, size)], n_ref.at[:, pl.ds(0, 8), dst]),
+                (zq.at[:, :, src], n_ref.at[:, pl.ds(8, 16), dst]),
+                (own.at[:, :, src], n_ref.at[:, pl.ds(24, 16), dst]),
+                (q.at[:, :, src], n_ref.at[:, pl.ds(40, 16), dst]),
+                (f.at[:, pl.ds(foff, 8), src], n_ref.at[:, pl.ds(56, 8), dst]),
+            ]
+        out.append(tile)
+    return out
+
+
+def edge_kernel(places, scal, zo, own, q, zq, f, left, right, sems):
+    foff = pl.multiple_of(scal[0] * 8, 8)
+    moves = []
+    for (b, place), out in zip(places, (left, right)):
+        src = pl.ds(place * LANES, LANES)
+        moves += [
+            (zo.at[:, :, pl.ds(b * LANES, LANES)], out.at[:, pl.ds(0, 8), :]),
+            (zq.at[:, :, src], out.at[:, pl.ds(8, 16), :]),
+            (own.at[:, :, src], out.at[:, pl.ds(24, 16), :]),
+            (q.at[:, :, src], out.at[:, pl.ds(40, 16), :]),
+            (f.at[:, pl.ds(foff, 8), src], out.at[:, pl.ds(56, 8), :]),
         ]
-        at += run
-    return out
-
-
-def count_copies(reads, sources):
-    class Fake:
-        at = property(lambda self: self)
-
-        def __getitem__(self, _):
-            return self
-
-    x = Fake()
-    return len(copies(reads, 0, x, {c: (x,) * 4 for c in sources}, x))
+    moves = [pltpu.make_async_copy(src, dst, sems.at[i]) for i, (src, dst) in enumerate(moves)]
+    for move in moves:
+        move.start()
+    for move in moves:
+        move.wait()
+
+
+def edge_columns(scal, *arrays):
+    smem = pl.BlockSpec(memory_space=pltpu.SMEM)
+    anywhere = pl.BlockSpec(memory_space=pl.ANY)
+    vmem = pl.BlockSpec(memory_space=pltpu.VMEM)
+    shape = jax.ShapeDtypeStruct((K, 64, LANES), jnp.float32)
+    places = tuple((b, CHUNKS[0].index(b)) for b in (31, 0))
+    return pl.pallas_call(
+        functools.partial(edge_kernel, places),
+        out_shape=(shape, shape),
+        in_specs=[smem] + [anywhere] * len(arrays),
+        out_specs=(vmem, vmem),
+        scratch_shapes=[pltpu.SemaphoreType.DMA((10,))],
+        name="edge_columns",
+    )(scal, *arrays)
 
 
 def kernel(reads, sources, joins, height, width, scal, mix, relcol, *refs):
@@ -155,12 +180,9 @@
     core, outer, row0, col0 = scal[0], scal[1], scal[2], scal[3]
     foff = pl.multiple_of(core * 8, 8)
 
-    moves = [
-        pltpu.make_async_copy(src, dst, sems.at[i])
-        for i, (src, dst) in enumerate(copies(reads, foff, zo, parts, n_ref))
-    ]
-    for move in moves:
-        move.start()
+    for i, moves in enumerate(copies(reads, foff, zo, parts, halo, n_ref)):
+        for src, dst in moves:
+            pltpu.make_async_copy(src, dst, sems.at[i]).start()
 
     i = lax.broadcasted_iota(jnp.int32, (64, 256), 0)
     flipped = jnp.where(i < 8, i + 32, jnp.where(i < 24, i + 8, jnp.where(i < 40, i - 24, jnp.where(i < 56, i - 56, i - 80))))
@@ -177,18 +199,6 @@
         ref[:, 0:LANES] = jnp.zeros((rows, LANES), jnp.bfloat16)
         ref[:, pl.ds((blocks + 1) * LANES, LANES)] = jnp.zeros((rows, LANES), jnp.bfloat16)
 
-    if EDGE in reads:
-        dst = pl.ds(reads.index(EDGE) * LANES, LANES)
-        lane = lax.broadcasted_iota(jnp.int32, (K, 8, LANES), 2)
-        left, right = halo
-        for r in range(0, 56, 8):
-            n_ref[:, r : r + 8, dst] = jnp.where(lane < 64, right[:, r : r + 8, :], left[:, r : r + 8, :])
-        fr = pl.ds(56 + foff, 8)
-        n_ref[:, 56:64, dst] = jnp.where(lane < 64, right[:, fr, :], left[:, fr, :])
-
-    for move in moves:
-        move.wait()
-
     def tile(j):
         return pl.ds(pl.multiple_of(j * 256, 256), 256)
 
@@ -203,8 +213,19 @@
         el = jnp.where(first, low[:, at(j, 3 * LANES, LANES)], low[:, at(j, 0, LANES)])
         return dot(jnp.concatenate([mh, ml, mh, eh, el, eh], axis=1), bm[...])
 
-    @pl.loop(0, tiles)
-    def _(j):
+    def arrived(j):
+        window = n_ref.at[:, :, tile(j)]
+        pltpu.make_async_copy(window, window, sems.at[j]).wait()
+
+    if halo:
+        for j in range(tiles):
+            arrived(j)
+        dst = pl.ds(reads.index(EDGE) * LANES, LANES)
+        lane = lax.broadcasted_iota(jnp.int32, (K, 8, LANES), 2)
+        for r in range(0, 64, 8):
+            n_ref[:, r : r + 8, dst] = jnp.where(lane < 64, n_ref[:, r : r + 8, dst], halo[0][:, r : r + 8, :])
+
+    def first(j):
         scale = rr[...] * rc[0:1, tile(j)]
         for k in range(K):
             hh, hl = row_pass(g1[core], n_ref[k, :, tile(j)] * scale)
@@ -213,42 +234,82 @@
 
     @pl.loop(0, tiles)
     def _(j):
-        u_ref[...] = column_pass(h1h, h1l, j)
+        if not halo:
+            arrived(j)
+        first(j)
+
+    def step(j, p):
         acc = jnp.zeros((48, 256), jnp.float32)
         for k in range(K):
-            acc = acc + mix[k] * jnp.log(u_ref[48 * k : 48 * k + 48, :])
+            acc = acc + mix[k] * jnp.log(u_ref[p, 48 * k : 48 * k + 48, :])
         valid = cv[0:1, tile(j)] > 0.0
         index = lax.broadcasted_iota(jnp.int32, (48, 256), 0)
         valid = valid & ((index >= 16) | (outer == 0))
         geo = jnp.exp(acc)
         for k in range(K):
-            w = jnp.where(valid, geo / u_ref[48 * k : 48 * k + 48, :], 0.0)
+            w = jnp.where(valid, geo / u_ref[p, 48 * k : 48 * k + 48, :], 0.0)
             w_ref[k, :, tile(j)] = w[16:32]
             hh, hl = row_pass(g2[core], w)
             h2h[32 * k : 32 * k + 32, at(j, LANES, 256)] = hh
             h2l[32 * k : 32 * k + 32, at(j, LANES, 256)] = hl
 
+    def stage(j, count):
+        for p in range(count):
+            u_ref[p] = column_pass(h1h, h1l, j + p)
+        for p in range(count):
+            step(j + p, p)
+
+    @pl.loop(0, tiles // 2)
+    def _(j):
+        stage(2 * j, 2)
+
+    if tiles % 2:
+        stage(tiles - 1, 1)
+
     zrow = pl.ds(pl.multiple_of(jnp.where(core == 0, 16, 8), 8), 8)
     qrow = pl.ds(pl.multiple_of(jnp.where(core == 0, 40, 48), 8), 8)
 
-    @pl.loop(0, tiles)
-    def _(j):
-        u_ref[0 : 32 * K, :] = column_pass(h2h, h2l, j)
+    def step(j, p):
         valid = cv[0:1, tile(j)] > 0.0
         for k in range(K):
             n = jnp.concatenate([n_ref[k, zrow, tile(j)], n_ref[k, 24:40, tile(j)], n_ref[k, qrow, tile(j)]], axis=0)
-            d = jnp.where(valid, n / u_ref[32 * k : 32 * k + 32, :], 0.0)
+            d = jnp.where(valid, n / u_ref[p, 32 * k : 32 * k + 32, :], 0.0)
             hh, hl = row_pass(g3[core], d)
             h3h[16 * k : 16 * k + 16, at(j, LANES, 256)] = hh
             h3l[16 * k : 16 * k + 16, at(j, LANES, 256)] = hl
 
-    @pl.loop(0, tiles)
+    def stage(j, count):
+        for p in range(count):
+            u_ref[p, 0 : 32 * K, :] = column_pass(h2h, h2l, j + p)
+        for p in range(count):
+            step(j + p, p)
+
+    @pl.loop(0, tiles // 2)
     def _(j):
-        u_ref[0 : 16 * K, :] = column_pass(h3h, h3l, j)
+        stage(2 * j, 2)
+
+    if tiles % 2:
+        stage(tiles - 1, 1)
+
+    def step(j, p):
         acc = jnp.zeros((16, 256), jnp.float32)
         for k in range(K):
-            acc = acc + mix[k] * jnp.log(w_ref[k, :, tile(j)] * u_ref[16 * k : 16 * k + 16, :])
+            acc = acc + mix[k] * jnp.log(w_ref[k, :, tile(j)] * u_ref[p, 16 * k : 16 * k + 16, :])
         acc_ref[:, tile(j)] = acc
+
+    def stage(j, count):
+        for p in range(count):
+            u_ref[p, 0 : 16 * K, :] = column_pass(h3h, h3l, j + p)
+        for p in range(count):
+            step(j + p, p)
+
+    @pl.loop(0, tiles // 2)
+    def _(j):
+        stage(2 * j, 2)
+
+    if tiles % 2:
+        stage(tiles - 1, 1)
+
 
     for i, moved in enumerate(joins):
         ref = acc_ref if i == len(joins) - 1 else earlier[i]
@@ -272,7 +333,6 @@
     smem = pl.BlockSpec(memory_space=pltpu.SMEM)
     vmem = pl.BlockSpec(memory_space=pltpu.VMEM)
     anywhere = pl.BlockSpec(memory_space=pl.ANY)
-    halos = 2 if EDGE in reads else 0
     scratch = [
         pltpu.VMEM((K, 64, lanes), jnp.float32),
         pltpu.VMEM((64, 256), jnp.float32),
@@ -282,11 +342,12 @@
     for rows in (48, 32, 16):
         scratch += [pltpu.VMEM((rows * K, wide), jnp.bfloat16)] * 2
     scratch += [
-        pltpu.VMEM((48 * K, 256), jnp.float32),
+        pltpu.VMEM((2, 48 * K, 256), jnp.float32),
         pltpu.VMEM((K, 16, lanes), jnp.float32),
-        pltpu.SemaphoreType.DMA((count_copies(reads, sources),)),
+        pltpu.SemaphoreType.DMA((blocks // 2,)),
     ]
-    in_specs = [smem, smem, vmem] + [anywhere] * (len(arrays) - halos) + [vmem] * (halos + len(consts))
+    halo_specs = [vmem, anywhere] if EDGE in reads else []
+    in_specs = [smem, smem, vmem] + [anywhere] * (len(arrays) - len(halo_specs)) + halo_specs + [vmem] * len(consts)
     args = [scal, mix, jnp.asarray(relative_columns(reads)), *arrays, *[jnp.asarray(c) for c in consts]]
     joins = ()
     if earlier:
@@ -321,7 +382,7 @@
     core = r % 2
     outer = ((r == 0) | (r == n_rows - 1)).astype(jnp.int32)
     scal = jnp.stack([core, outer, r * counts.shape[1], m * counts.shape[2]]).astype(jnp.int32)
-    mix = weights / jnp.sum(weights)
+    mix = lax.optimization_barrier(weights / jnp.sum(weights))
 
     swap = [(i, i ^ 1) for i in range(n_rows)]
     hop = [(i, i + 2) for i in range(0, n_rows - 2, 2)] + [(i, i - 2) for i in range(3, n_rows, 2)]
@@ -342,25 +403,16 @@
     zq = [lax.ppermute(x, "rows", hop) for x in q]
 
     sums = jnp.sum(n, axis=(1, 2))
-    step = 0
-    for axis, size in (("rows", n_rows), ("maps", n_cols)):
-        bit = 1
-        while bit < size:
-            sums = sums + lax.ppermute(sums, axis, [(i, i ^ bit) for i in range(size)])
-            bit, step = bit * 2, step + 1
+    rounds = [("rows", 1), ("maps", 1), ("maps", 2), ("rows", 16), ("rows", 32), ("rows", 2), ("rows", 4), ("rows", 8), ("maps", 4)]
+    for axis, bit in rounds:
+        sums = sums + lax.ppermute(sums, axis, [(d, d ^ bit) for d in range(lax.axis_size(axis))])
     log_scale = jnp.sum(mix * jnp.log(float(height * width) / sums))
 
     f = [lax.ppermute(x, "rows", swap) for x in zq]
 
-    def column(b):
-        i = CHUNKS[0].index(b)
-        cols = slice(i * LANES, (i + 1) * LANES)
-        return jnp.concatenate(
-            [zo[..., b * LANES : (b + 1) * LANES]] + [x[0][..., cols] for x in (zq, own, q, f)], axis=1
-        )
-
-    left = lax.ppermute(column(31), "maps", to_right)
-    right = lax.ppermute(column(0), "maps", to_left)
+    last, first = edge_columns(scal, zo, own[0], q[0], zq[0], f[0])
+    left = lax.ppermute(last, "maps", to_right)
+    right = lax.ppermute(first, "maps", to_left)
 
     outs = []
     for which in range(len(KERNELS)):

time: 249 us -> 217 us (0.87)
  the two profiles are of different devices: /device:TPU:8 before, /device:TPU:24 now
where the time goes in v2:
time: 217 us; the launch traced here: 216 us
  waiting for transfers between devices  84 us (39%)
  starting transfers between devices  77.1 us (36%)
  Pallas kernels  46.3 us (21%)
  other arithmetic  5.45 us (3%)
  local copies, waits for them, and re-layouts  2.57 us (1%)
    ppermute x3, waiting for transfers between devices, on_device(): zq = [lax.ppermute(x, 'rows', hop) for x in q]  48.9 us
    pallas_call x4, Pallas kernels, run_kernel(): pl.pallas_call(functools.partial(kernel, reads, sources, joins, height, w...  43.7 us
    ppermute x9, starting transfers between devices, on_device(): lax.ppermute(sums, axis, [(d, d ^ bit) for d in range(lax.axis_size(axis))])  41.5 us
    ppermute x9, waiting for transfers between devices, on_device(): lax.ppermute(sums, axis, [(d, d ^ bit) for d in range(lax.axis_size(axis))])  29.3 us
    ppermute x3, starting transfers between devices, on_device(): q = [lax.ppermute(x, 'rows', swap) for x in own]  15.6 us
    ppermute x3, starting transfers between devices, on_device(): zq = [lax.ppermute(x, 'rows', hop) for x in q]  7.63 us
    ppermute x3, waiting for transfers between devices, on_device(): q = [lax.ppermute(x, 'rows', swap) for x in own]  5.79 us
    ppermute x3, starting transfers between devices, on_device(): f = [lax.ppermute(x, 'rows', swap) for x in zq]  5.73 us
  transfers between devices with their start and end apart: 21, of which 14 were waited for; matrix products, arithmetic and copies ran while one was open for 1% of the time, Pallas kernels for 16%

profile of v2, /device:TPU:24, one launch (start us, length us, event | category | flops | bytes accessed | tf_op | source)
XLA Modules:
  0.0 215.9 jit_solution(18132073482807245683)
XLA Ops:
  0.0 2.5 %convert_add_fusion.1 = f32[8,8,4096]{2,1,0:T(8,128)} fusion(s32[8,16,4096]{2,1,0:T(8,128)} %param.22, s32[]{:T(128)S(6)} %select_n.11), kind=kLoop, calls=%fused_computation.1 | loop fusion | flops 524288 | bytes 2097156 | tf_op jit(solution)/shard_map/add | solution.py:396
  5.0 2.5 %collective-permute-done.1.refs_2_.q = f32[8,16,1920]{2,1,0:T(8,128)S(1)} collective-permute-done((f32[8,16,1920]{2,1,0:T(8,128)S(1)}, f32[8,16,1920]{2,1,0:T(8,128)S(1)}, u32[]{:S(2)}, u32[]{:S(2)}) %collective-permute-start.1) | collective-permute-done | bytes 983072 | tf_op jit(solution)/shard_map/ppermute | solution.py:402
  7.5 3.8 %collective-permute-start.2 = (f32[8,16,1920]{2,1,0:T(8,128)S(1)}, f32[8,16,1920]{2,1,0:T(8,128)}, u32[]{:S(2)}, u32[]{:S(2)}) collective-permute-start(f32[8,16,1920]{2,1,0:T(8,128)S(1)} %collective-permute-done.1.refs_2_.q), channel_id=1, source_target_pairs={{0,16},{16,32},{32,48},{48,64},{64,80},{80,96},{96,112},{112,128},... | collective-permute-start | bytes 2949128 | tf_op jit(solution)/shard_map/ppermute | solution.py:403
  11.4 11.3 %collective-permute-start.4 = (f32[8,16,1408]{2,1,0:T(8,128)S(1)}, f32[8,16,1408]{2,1,0:T(8,128)S(1)}, u32[]{:S(2)}, u32[]{:S(2)}) collective-permute-start(f32[8,16,1408]{2,1,0:T(8,128)S(1)} %slice.18.refs_5_), channel_id=1, source_target_pairs={{0,8},{8,0},{16,24},{24,16},{32,40},{40,32},{48,56},{56,48},{64,72... | collective-permute-start | bytes 2162696 | tf_op jit(solution)/shard_map/ppermute | solution.py:402
  28.4 15.2 %collective-permute-done.2.refs_3_.zq = f32[8,16,1920]{2,1,0:T(8,128)} collective-permute-done((f32[8,16,1920]{2,1,0:T(8,128)S(1)}, f32[8,16,1920]{2,1,0:T(8,128)}, u32[]{:S(2)}, u32[]{:S(2)}) %collective-permute-start.2) | collective-permute-done | bytes 983072 | tf_op jit(solution)/shard_map/ppermute | solution.py:403
  51.3 7.7 %collective-permute-done.5.refs_7_ = f32[8,16,1408]{2,1,0:T(8,128)} collective-permute-done((f32[8,16,1408]{2,1,0:T(8,128)S(1)}, f32[8,16,1408]{2,1,0:T(8,128)}, u32[]{:S(2)}, u32[]{:S(2)}) %collective-permute-start.5) | collective-permute-done | bytes 720928 | tf_op jit(solution)/shard_map/ppermute | solution.py:403
  63.4 26.0 %collective-permute-done.8.refs_11_ = f32[8,16,768]{2,1,0:T(8,128)} collective-permute-done((f32[8,16,768]{2,1,0:T(8,128)}, f32[8,16,768]{2,1,0:T(8,128)}, u32[]{:S(2)}, u32[]{:S(2)}) %collective-permute-start.8) | collective-permute-done | bytes 393248 | tf_op jit(solution)/shard_map/ppermute | solution.py:403
  93.5 2.6 %edge_columns.1 = (f32[8,64,128]{2,1,0:T(8,128)}, f32[8,64,128]{2,1,0:T(8,128)}) custom-call(s32[4]{0:T(128)} %pad_add_fusion.scal, f32[8,8,4096]{2,1,0:T(8,128)} %copy-done.1, f32[8,16,1920]{2,1,0:T(8,128)} %copy-done, f32[8,16,1920]{2,1,0:T(8,128)} %copy-done.2, f32[8,16,1920]{2,1,0:T(8,128)} %collective-permute-done.2.refs_3_.zq, ...), custom_call_target="tpu_custom_call" | custom-call | tf_op jit(solution)/shard_map/edge_columns/pallas_call | solution.py:155
  96.1 3.4 %collective-permute-start.19 = (f32[8,64,128]{2,1,0:T(8,128)}, f32[8,64,128]{2,1,0:T(8,128)S(1)}, u32[]{:S(2)}, u32[]{:S(2)}) collective-permute-start(f32[8,64,128]{2,1,0:T(8,128)} %get-tuple-element.9), channel_id=1, source_target_pairs={{0,1},{1,2},{2,3},{3,4},{4,5},{5,6},{6,7},{8,9},{9,10},{10,11},{11... | collective-permute-start | bytes 786440 | tf_op jit(solution)/shard_map/ppermute | solution.py:414
  101.5 4.5 %collective-permute-start.11 = (f32[8]{0:T(128)S(1)}, f32[8]{0:T(128)S(1)}, u32[]{:S(2)}, u32[]{:S(2)}) collective-permute-start(f32[8]{0:T(128)S(1)} %add.52), channel_id=1, source_target_pairs={{0,1},{1,0},{2,3},{3,2},{4,5},{5,4},{6,7},{7,6},{8,9},{9,8},{10,11... | collective-permute-start | bytes 104 | tf_op jit(solution)/shard_map/ppermute | solution.py:408
  106.1 4.1 %collective-permute-done.11 = f32[8]{0:T(128)S(1)} collective-permute-done((f32[8]{0:T(128)S(1)}, f32[8]{0:T(128)S(1)}, u32[]{:S(2)}, u32[]{:S(2)}) %collective-permute-start.11) | collective-permute-done | bytes 64 | tf_op jit(solution)/shard_map/ppermute | solution.py:408
  110.2 9.8 %collective-permute-start.12 = (f32[8]{0:T(128)S(1)}, f32[8]{0:T(128)S(1)}, u32[]{:S(2)}, u32[]{:S(2)}) collective-permute-start(f32[8]{0:T(128)S(1)} %add.53), channel_id=1, source_target_pairs={{0,2},{1,3},{2,0},{3,1},{4,6},{5,7},{6,4},{7,5},{8,10},{9,11},{10,... | collective-permute-start | bytes 104 | tf_op jit(solution)/shard_map/ppermute | solution.py:408
  123.9 3.1 %collective-permute-done.13 = f32[8]{0:T(128)S(1)} collective-permute-done((f32[8]{0:T(128)S(1)}, f32[8]{0:T(128)S(1)}, u32[]{:S(2)}, u32[]{:S(2)}) %collective-permute-start.13) | collective-permute-done | bytes 64 | tf_op jit(solution)/shard_map/ppermute | solution.py:408
  127.0 2.8 %collective-permute-start.14 = (f32[8]{0:T(128)S(1)}, f32[8]{0:T(128)S(1)}, u32[]{:S(2)}, u32[]{:S(2)}) collective-permute-start(f32[8]{0:T(128)S(1)} %add.55), channel_id=1, source_target_pairs={{0,256},{8,264},{16,272},{24,280},{32,288},{40,296},{48,304},{56,3... | collective-permute-start | bytes 104 | tf_op jit(solution)/shard_map/ppermute | solution.py:408
  129.9 4.1 %collective-permute-done.14 = f32[8]{0:T(128)S(1)} collective-permute-done((f32[8]{0:T(128)S(1)}, f32[8]{0:T(128)S(1)}, u32[]{:S(2)}, u32[]{:S(2)}) %collective-permute-start.14) | collective-permute-done | bytes 64 | tf_op jit(solution)/shard_map/ppermute | solution.py:408
  135.9 3.5 %collective-permute-done.15 = f32[8]{0:T(128)S(1)} collective-permute-done((f32[8]{0:T(128)S(1)}, f32[8]{0:T(128)S(1)}, u32[]{:S(2)}, u32[]{:S(2)}) %collective-permute-start.15) | collective-permute-done | bytes 64 | tf_op jit(solution)/shard_map/ppermute | solution.py:408
  141.3 4.4 %collective-permute-done.16 = f32[8]{0:T(128)S(1)} collective-permute-done((f32[8]{0:T(128)S(1)}, f32[8]{0:T(128)S(1)}, u32[]{:S(2)}, u32[]{:S(2)}) %collective-permute-start.16) | collective-permute-done | bytes 64 | tf_op jit(solution)/shard_map/ppermute | solution.py:408
  145.8 2.4 %collective-permute-start.17 = (f32[8]{0:T(128)S(1)}, f32[8]{0:T(128)S(1)}, u32[]{:S(2)}, u32[]{:S(2)}) collective-permute-start(f32[8]{0:T(128)S(1)} %add.58), channel_id=1, source_target_pairs={{0,64},{8,72},{16,80},{24,88},{32,96},{40,104},{48,112},{56,120},{... | collective-permute-start | bytes 104 | tf_op jit(solution)/shard_map/ppermute | solution.py:408
  148.2 6.9 %collective-permute-done.17 = f32[8]{0:T(128)S(1)} collective-permute-done((f32[8]{0:T(128)S(1)}, f32[8]{0:T(128)S(1)}, u32[]{:S(2)}, u32[]{:S(2)}) %collective-permute-start.17) | collective-permute-done | bytes 64 | tf_op jit(solution)/shard_map/ppermute | solution.py:408
  155.1 13.3 %collective-permute-start.18 = (f32[8]{0:T(128)S(1)}, f32[8]{0:T(128)S(1)}, u32[]{:S(2)}, u32[]{:S(2)}) collective-permute-start(f32[8]{0:T(128)S(1)} %add.59), channel_id=1, source_target_pairs={{0,4},{1,5},{2,6},{3,7},{4,0},{5,1},{6,2},{7,3},{8,12},{9,13},{10,... | collective-permute-start | bytes 104 | tf_op jit(solution)/shard_map/ppermute | solution.py:408
  170.6 11.3 %shard_map.208.refs_18_ = f32[16,1536]{1,0:T(8,128)} custom-call(s32[4]{0:T(128)} %pad_add_fusion.scal, f32[8]{0:T(128)} %copy-done.9, s32[8,1536]{1,0:T(8,128)} %constant.55.clone.relcol, f32[8,8,4096]{2,1,0:T(8,128)} %copy-done.1, f32[8,16,1920]{2,1,0:T(8,128)} %copy-done, f32[8,16,1920]{2,1,0:T(8,128)} %copy-done.2, ...), custom_call_target="tpu_custom_call" | custom-call | tf_op jit(solution)/shard_map/pallas_call | solution.py:360
  181.9 13.5 %shard_map.210.refs_20_ = f32[16,1792]{1,0:T(8,128)} custom-call(s32[4]{0:T(128)} %pad_add_fusion.scal, f32[8]{0:T(128)} %copy-done.9, s32[8,1792]{1,0:T(8,128)} %constant.61.clone.relcol, f32[8,8,4096]{2,1,0:T(8,128)} %copy-done.1, f32[8,16,1920]{2,1,0:T(8,128)} %copy-done, f32[8,16,1920]{2,1,0:T(8,128)} %copy-done.2, ...), custom_call_target="tpu_custom_call" | custom-call | tf_op jit(solution)/shard_map/pallas_call | solution.py:360
  196.8 7.9 %shard_map.209.refs_19_ = f32[16,768]{1,0:T(8,128)} custom-call(s32[4]{0:T(128)} %pad_add_fusion.scal, f32[8]{0:T(128)} %copy-done.9, s32[8,768]{1,0:T(8,128)} %constant.60.clone.relcol, f32[8,8,4096]{2,1,0:T(8,128)} %copy-done.1, f32[8,16,1920]{2,1,0:T(8,128)} %copy-done, f32[8,16,1920]{2,1,0:T(8,128)} %copy-done.2, ...), custom_call_target="tpu_custom_call" | custom-call | tf_op jit(solution)/shard_map/pallas_call | solution.py:360
  204.7 11.1 %shard_map.211 = f32[16,4096]{1,0:T(8,128)} custom-call(s32[4]{0:T(128)} %pad_add_fusion.scal, f32[8]{0:T(128)} %copy-done.9, s32[8,1280]{1,0:T(8,128)} %constant.62.clone.relcol, f32[8,8,4096]{2,1,0:T(8,128)} %copy-done.1, f32[8,16,1920]{2,1,0:T(8,128)} %copy-done, f32[8,16,1920]{2,1,0:T(8,128)} %copy-done.2, ...), custom_call_target="tpu_custom_call" | custom-call | tf_op jit(solution)/shard_map/pallas_call | solution.py:360
  (64 shorter events, 37.6 us)
Async XLA Ops:
  3.0 88.9 %copy-start.10 = (f32[8]{0:T(128)S(1)}, f32[8]{0:T(128)}, u32[]{:S(2)}) copy-start(f32[8]{0:T(128)} %param.23) | copy-start | bytes 100
  3.1 89.5 %copy-start = (f32[8,16,1920]{2,1,0:T(8,128)}, f32[8,16,1920]{2,1,0:T(8,128)S(1)}, u32[]{:S(2)}) copy-start(f32[8,16,1920]{2,1,0:T(8,128)S(1)} %pad_maximum_fusion.refs_1_.own) | copy-start | bytes 2949124
  3.1 4.5 %collective-permute-start.1 = (f32[8,16,1920]{2,1,0:T(8,128)S(1)}, f32[8,16,1920]{2,1,0:T(8,128)S(1)}, u32[]{:S(2)}, u32[]{:S(2)}) collective-permute-start(f32[8,16,1920]{2,1,0:T(8,128)S(1)} %pad_maximum_fusion.refs_1_.own), channel_id=1, source_target_pairs={{0,8},{8,0},{16,24},{24,16},{32,40},{40,32},{48,56},{56,48},{64,72... | collective-permute-start | bytes 2949128 | tf_op jit(solution)/shard_map/ppermute | solution.py:402
  7.5 36.0 %collective-permute-start.2 = (f32[8,16,1920]{2,1,0:T(8,128)S(1)}, f32[8,16,1920]{2,1,0:T(8,128)}, u32[]{:S(2)}, u32[]{:S(2)}) collective-permute-start(f32[8,16,1920]{2,1,0:T(8,128)S(1)} %collective-permute-done.1.refs_2_.q), channel_id=1, source_target_pairs={{0,16},{16,32},{32,48},{48,64},{64,80},{80,96},{96,112},{112,128},... | collective-permute-start | bytes 2949128 | tf_op jit(solution)/shard_map/ppermute | solution.py:403
  11.4 13.1 %collective-permute-start.4 = (f32[8,16,1408]{2,1,0:T(8,128)S(1)}, f32[8,16,1408]{2,1,0:T(8,128)S(1)}, u32[]{:S(2)}, u32[]{:S(2)}) collective-permute-start(f32[8,16,1408]{2,1,0:T(8,128)S(1)} %slice.18.refs_5_), channel_id=1, source_target_pairs={{0,8},{8,0},{16,24},{24,16},{32,40},{40,32},{48,56},{56,48},{64,72... | collective-permute-start | bytes 2162696 | tf_op jit(solution)/shard_map/ppermute | solution.py:402
  24.5 34.5 %collective-permute-start.5 = (f32[8,16,1408]{2,1,0:T(8,128)S(1)}, f32[8,16,1408]{2,1,0:T(8,128)}, u32[]{:S(2)}, u32[]{:S(2)}) collective-permute-start(f32[8,16,1408]{2,1,0:T(8,128)S(1)} %collective-permute-done.4.refs_6_), channel_id=1, source_target_pairs={{0,16},{16,32},{32,48},{48,64},{64,80},{80,96},{96,112},{112,128},... | collective-permute-start | bytes 2162696 | tf_op jit(solution)/shard_map/ppermute | solution.py:403
  26.4 66.1 %collective-permute-start = (f32[8,8,4096]{2,1,0:T(8,128)}, f32[8,8,4096]{2,1,0:T(8,128)S(1)}, u32[]{:S(2)}, u32[]{:S(2)}) collective-permute-start(f32[8,8,4096]{2,1,0:T(8,128)} %convert_add_fusion.1), channel_id=1, source_target_pairs={{0,16},{16,32},{32,48},{48,64},{64,80},{80,96},{96,112},{112,128},... | collective-permute-start | bytes 3145736 | tf_op jit(solution)/shard_map/ppermute | solution.py:399
  43.6 49.0 %collective-permute-start.3 = (f32[8,16,1920]{2,1,0:T(8,128)}, f32[8,16,1920]{2,1,0:T(8,128)}, u32[]{:S(2)}, u32[]{:S(2)}) collective-permute-start(f32[8,16,1920]{2,1,0:T(8,128)} %collective-permute-done.2.refs_3_.zq), channel_id=1, source_target_pairs={{0,8},{8,0},{16,24},{24,16},{32,40},{40,32},{48,56},{56,48},{64,72... | collective-permute-start | bytes 2949128 | tf_op jit(solution)/shard_map/ppermute | solution.py:411
  45.5 149.8 %copy-start.6 = (f32[8,16,768]{2,1,0:T(8,128)}, f32[8,16,768]{2,1,0:T(8,128)S(1)}, u32[]{:S(2)}) copy-start(f32[8,16,768]{2,1,0:T(8,128)S(1)} %slice.19.refs_9_) | copy-start | bytes 1179652
  45.6 3.9 %collective-permute-start.7 = (f32[8,16,768]{2,1,0:T(8,128)S(1)}, f32[8,16,768]{2,1,0:T(8,128)}, u32[]{:S(2)}, u32[]{:S(2)}) collective-permute-start(f32[8,16,768]{2,1,0:T(8,128)S(1)} %slice.19.refs_9_), channel_id=1, source_target_pairs={{0,8},{8,0},{16,24},{24,16},{32,40},{40,32},{48,56},{56,48},{64,72... | collective-permute-start | bytes 1179656 | tf_op jit(solution)/shard_map/ppermute | solution.py:402
  49.4 39.9 %collective-permute-start.8 = (f32[8,16,768]{2,1,0:T(8,128)}, f32[8,16,768]{2,1,0:T(8,128)}, u32[]{:S(2)}, u32[]{:S(2)}) collective-permute-start(f32[8,16,768]{2,1,0:T(8,128)} %collective-permute-done.7.refs_10_), channel_id=1, source_target_pairs={{0,16},{16,32},{32,48},{48,64},{64,80},{80,96},{96,112},{112,128},... | collective-permute-start | bytes 1179656 | tf_op jit(solution)/shard_map/ppermute | solution.py:403
  59.0 122.8 %collective-permute-start.6 = (f32[8,16,1408]{2,1,0:T(8,128)}, f32[8,16,1408]{2,1,0:T(8,128)}, u32[]{:S(2)}, u32[]{:S(2)}) collective-permute-start(f32[8,16,1408]{2,1,0:T(8,128)} %collective-permute-done.5.refs_7_), channel_id=1, source_target_pairs={{0,8},{8,0},{16,24},{24,16},{32,40},{40,32},{48,56},{56,48},{64,72... | collective-permute-start | bytes 2162696 | tf_op jit(solution)/shard_map/ppermute | solution.py:411
  60.9 40.6 %collective-permute-start.10 = (f32[8]{0:T(128)S(1)}, f32[8]{0:T(128)S(1)}, u32[]{:S(2)}, u32[]{:S(2)}) collective-permute-start(f32[8]{0:T(128)S(1)} %get-tuple-element.11), channel_id=1, source_target_pairs={{0,8},{8,0},{16,24},{24,16},{32,40},{40,32},{48,56},{56,48},{64,72... | collective-permute-start | bytes 104 | tf_op jit(solution)/shard_map/ppermute | solution.py:408
  89.4 115.3 %collective-permute-start.9 = (f32[8,16,768]{2,1,0:T(8,128)}, f32[8,16,768]{2,1,0:T(8,128)}, u32[]{:S(2)}, u32[]{:S(2)}) collective-permute-start(f32[8,16,768]{2,1,0:T(8,128)} %collective-permute-done.8.refs_11_), channel_id=1, source_target_pairs={{0,8},{8,0},{16,24},{24,16},{32,40},{40,32},{48,56},{56,48},{64,72... | collective-permute-start | bytes 1179656 | tf_op jit(solution)/shard_map/ppermute | solution.py:411
  96.1 99.2 %collective-permute-start.19 = (f32[8,64,128]{2,1,0:T(8,128)}, f32[8,64,128]{2,1,0:T(8,128)S(1)}, u32[]{:S(2)}, u32[]{:S(2)}) collective-permute-start(f32[8,64,128]{2,1,0:T(8,128)} %get-tuple-element.9), channel_id=1, source_target_pairs={{0,1},{1,2},{2,3},{3,4},{4,5},{5,6},{6,7},{8,9},{9,10},{10,11},{11... | collective-permute-start | bytes 786440 | tf_op jit(solution)/shard_map/ppermute | solution.py:414
  99.6 95.8 %collective-permute-start.20 = (f32[8,64,128]{2,1,0:T(8,128)}, f32[8,64,128]{2,1,0:T(8,128)S(1)}, u32[]{:S(2)}, u32[]{:S(2)}) collective-permute-start(f32[8,64,128]{2,1,0:T(8,128)} %get-tuple-element.10), channel_id=1, source_target_pairs={{1,0},{2,1},{3,2},{4,3},{5,4},{6,5},{7,6},{9,8},{10,9},{11,10},{12... | collective-permute-start | bytes 786440 | tf_op jit(solution)/shard_map/ppermute | solution.py:415
  101.5 8.7 %collective-permute-start.11 = (f32[8]{0:T(128)S(1)}, f32[8]{0:T(128)S(1)}, u32[]{:S(2)}, u32[]{:S(2)}) collective-permute-start(f32[8]{0:T(128)S(1)} %add.52), channel_id=1, source_target_pairs={{0,1},{1,0},{2,3},{3,2},{4,5},{5,4},{6,7},{7,6},{8,9},{9,8},{10,11... | collective-permute-start | bytes 104 | tf_op jit(solution)/shard_map/ppermute | solution.py:408
  110.2 11.4 %collective-permute-start.12 = (f32[8]{0:T(128)S(1)}, f32[8]{0:T(128)S(1)}, u32[]{:S(2)}, u32[]{:S(2)}) collective-permute-start(f32[8]{0:T(128)S(1)} %add.53), channel_id=1, source_target_pairs={{0,2},{1,3},{2,0},{3,1},{4,6},{5,7},{6,4},{7,5},{8,10},{9,11},{10,... | collective-permute-start | bytes 104 | tf_op jit(solution)/shard_map/ppermute | solution.py:408
  121.6 5.5 %collective-permute-start.13 = (f32[8]{0:T(128)S(1)}, f32[8]{0:T(128)S(1)}, u32[]{:S(2)}, u32[]{:S(2)}) collective-permute-start(f32[8]{0:T(128)S(1)} %add.54), channel_id=1, source_target_pairs={{0,128},{8,136},{16,144},{24,152},{32,160},{40,168},{48,176},{56,1... | collective-permute-start | bytes 104 | tf_op jit(solution)/shard_map/ppermute | solution.py:408
  127.0 7.0 %collective-permute-start.14 = (f32[8]{0:T(128)S(1)}, f32[8]{0:T(128)S(1)}, u32[]{:S(2)}, u32[]{:S(2)}) collective-permute-start(f32[8]{0:T(128)S(1)} %add.55), channel_id=1, source_target_pairs={{0,256},{8,264},{16,272},{24,280},{32,288},{40,296},{48,304},{56,3... | collective-permute-start | bytes 104 | tf_op jit(solution)/shard_map/ppermute | solution.py:408
  134.0 5.5 %collective-permute-start.15 = (f32[8]{0:T(128)S(1)}, f32[8]{0:T(128)S(1)}, u32[]{:S(2)}, u32[]{:S(2)}) collective-permute-start(f32[8]{0:T(128)S(1)} %add.56), channel_id=1, source_target_pairs={{0,16},{8,24},{16,0},{24,8},{32,48},{40,56},{48,32},{56,40},{64,80... | collective-permute-start | bytes 104 | tf_op jit(solution)/shard_map/ppermute | solution.py:408
  139.4 6.3 %collective-permute-start.16 = (f32[8]{0:T(128)S(1)}, f32[8]{0:T(128)S(1)}, u32[]{:S(2)}, u32[]{:S(2)}) collective-permute-start(f32[8]{0:T(128)S(1)} %add.57), channel_id=1, source_target_pairs={{0,32},{8,40},{16,48},{24,56},{32,0},{40,8},{48,16},{56,24},{64,96... | collective-permute-start | bytes 104 | tf_op jit(solution)/shard_map/ppermute | solution.py:408
  145.8 9.4 %collective-permute-start.17 = (f32[8]{0:T(128)S(1)}, f32[8]{0:T(128)S(1)}, u32[]{:S(2)}, u32[]{:S(2)}) collective-permute-start(f32[8]{0:T(128)S(1)} %add.58), channel_id=1, source_target_pairs={{0,64},{8,72},{16,80},{24,88},{32,96},{40,104},{48,112},{56,120},{... | collective-permute-start | bytes 104 | tf_op jit(solution)/shard_map/ppermute | solution.py:408
  155.1 14.8 %collective-permute-start.18 = (f32[8]{0:T(128)S(1)}, f32[8]{0:T(128)S(1)}, u32[]{:S(2)}, u32[]{:S(2)}) collective-permute-start(f32[8]{0:T(128)S(1)} %add.59), channel_id=1, source_target_pairs={{0,4},{1,5},{2,6},{3,7},{4,0},{5,1},{6,2},{7,3},{8,12},{9,13},{10,... | collective-permute-start | bytes 104 | tf_op jit(solution)/shard_map/ppermute | solution.py:408
  (8 other events, 193.1 us)

commit v3 on v2

--- a/solution.py
+++ b/solution.py
@@ -14,24 +14,13 @@
 LANES = 128
 EDGE = -1
 
-FIRST, SECOND = 12, 23
-CHUNKS = (
-    (29, 30, 31) + tuple(range(FIRST)),
-    tuple(range(FIRST, SECOND)),
-    tuple(range(SECOND, 29)),
-)
+FIRST = 22
+CHUNKS = (tuple(range(FIRST)), tuple(range(FIRST, 32)) + (EDGE,))
 KERNELS = (
     (tuple(range(FIRST)), (0,)),
-    ((29, 30, 31, EDGE, 0, 1), (0,)),
-    (tuple(range(FIRST - 3, SECOND)), (0, 1)),
-    (tuple(range(SECOND - 2, 31)), (0, 1, 2)),
+    (tuple(range(FIRST - 3, 32)) + (EDGE, 0, 1), (0, 1)),
 )
-KEPT = (
-    ((1, FIRST - 2),),
-    ((30, 31), (0, 0)),
-    ((FIRST - 1, SECOND - 2),),
-    ((SECOND - 1, 29),),
-)
+KEPT = (((1, FIRST - 2),), ((FIRST - 1, 31), (0, 0)))
 
 
 def taps():
@@ -100,24 +89,18 @@
     return total
 
 
-def copies(reads, foff, zo, parts, halo, n_ref):
+def copies(reads, foff, parts, n_ref):
     where = {b: (c, i) for c, ids in enumerate(CHUNKS) for i, b in enumerate(ids)}
     out = []
     for at in range(0, len(reads), 2):
-        pair = reads[at : at + 2]
-        joined = EDGE not in pair and pair[1] == pair[0] + 1 and where[pair[1]] == (where[pair[0]][0], where[pair[0]][1] + 1)
+        (c, i), (d, j) = [where[b] for b in reads[at : at + 2]]
         tile = []
-        for i, b in enumerate(pair[:1] if joined else pair):
-            size = (2 if joined else 1) * LANES
-            dst = pl.ds((at + i) * LANES, size)
-            if b == EDGE:
-                tile.append((halo[1], n_ref.at[:, :, dst]))
-                continue
-            c, place = where[b]
-            own, q, zq, f = parts[c]
-            src = pl.ds(place * LANES, size)
+        for c, i, blocks, to in ((c, i, 2, at),) if (d, j) == (c, i + 1) else ((c, i, 1, at), (d, j, 1, at + 1)):
+            zo, own, q, zq, f = parts[c]
+            dst = pl.ds(to * LANES, blocks * LANES)
+            src = pl.ds(i * LANES, blocks * LANES)
             tile += [
-                (zo.at[:, :, pl.ds(b * LANES, size)], n_ref.at[:, pl.ds(0, 8), dst]),
+                (zo.at[:, :, src], n_ref.at[:, pl.ds(0, 8), dst]),
                 (zq.at[:, :, src], n_ref.at[:, pl.ds(8, 16), dst]),
                 (own.at[:, :, src], n_ref.at[:, pl.ds(24, 16), dst]),
                 (q.at[:, :, src], n_ref.at[:, pl.ds(40, 16), dst]),
@@ -127,46 +110,9 @@
     return out
 
 
-def edge_kernel(places, scal, zo, own, q, zq, f, left, right, sems):
-    foff = pl.multiple_of(scal[0] * 8, 8)
-    moves = []
-    for (b, place), out in zip(places, (left, right)):
-        src = pl.ds(place * LANES, LANES)
-        moves += [
-            (zo.at[:, :, pl.ds(b * LANES, LANES)], out.at[:, pl.ds(0, 8), :]),
-            (zq.at[:, :, src], out.at[:, pl.ds(8, 16), :]),
-            (own.at[:, :, src], out.at[:, pl.ds(24, 16), :]),
-            (q.at[:, :, src], out.at[:, pl.ds(40, 16), :]),
-            (f.at[:, pl.ds(foff, 8), src], out.at[:, pl.ds(56, 8), :]),
-        ]
-    moves = [pltpu.make_async_copy(src, dst, sems.at[i]) for i, (src, dst) in enumerate(moves)]
-    for move in moves:
-        move.start()
-    for move in moves:
-        move.wait()
-
-
-def edge_columns(scal, *arrays):
-    smem = pl.BlockSpec(memory_space=pltpu.SMEM)
-    anywhere = pl.BlockSpec(memory_space=pl.ANY)
-    vmem = pl.BlockSpec(memory_space=pltpu.VMEM)
-    shape = jax.ShapeDtypeStruct((K, 64, LANES), jnp.float32)
-    places = tuple((b, CHUNKS[0].index(b)) for b in (31, 0))
-    return pl.pallas_call(
-        functools.partial(edge_kernel, places),
-        out_shape=(shape, shape),
-        in_specs=[smem] + [anywhere] * len(arrays),
-        out_specs=(vmem, vmem),
-        scratch_shapes=[pltpu.SemaphoreType.DMA((10,))],
-        name="edge_columns",
-    )(scal, *arrays)
-
-
 def kernel(reads, sources, joins, height, width, scal, mix, relcol, *refs):
-    n_in = 1 + 4 * len(sources) + (2 if EDGE in reads else 0)
-    zo = refs[0]
-    parts = {c: refs[1 + 4 * i : 5 + 4 * i] for i, c in enumerate(sources)}
-    halo = refs[1 + 4 * len(sources) : n_in]
+    n_in = 5 * len(sources)
+    parts = {c: refs[5 * i : 5 * i + 5] for i, c in enumerate(sources)}
     g1, g2, g3, bm = refs[n_in : n_in + 4]
     n_in += 4
     if joins:
@@ -180,7 +126,7 @@
     core, outer, row0, col0 = scal[0], scal[1], scal[2], scal[3]
     foff = pl.multiple_of(core * 8, 8)
 
-    for i, moves in enumerate(copies(reads, foff, zo, parts, halo, n_ref)):
+    for i, moves in enumerate(copies(reads, foff, parts, n_ref)):
         for src, dst in moves:
             pltpu.make_async_copy(src, dst, sems.at[i]).start()
 
@@ -217,14 +163,6 @@
         window = n_ref.at[:, :, tile(j)]
         pltpu.make_async_copy(window, window, sems.at[j]).wait()
 
-    if halo:
-        for j in range(tiles):
-            arrived(j)
-        dst = pl.ds(reads.index(EDGE) * LANES, LANES)
-        lane = lax.broadcasted_iota(jnp.int32, (K, 8, LANES), 2)
-        for r in range(0, 64, 8):
-            n_ref[:, r : r + 8, dst] = jnp.where(lane < 64, n_ref[:, r : r + 8, dst], halo[0][:, r : r + 8, :])
-
     def first(j):
         scale = rr[...] * rc[0:1, tile(j)]
         for k in range(K):
@@ -232,11 +170,18 @@
             h1h[48 * k : 48 * k + 48, at(j, LANES, 256)] = hh
             h1l[48 * k : 48 * k + 48, at(j, LANES, 256)] = hl
 
-    @pl.loop(0, tiles)
+    def stage(j, count):
+        for p in range(count):
+            arrived(j + p)
+        for p in range(count):
+            first(j + p)
+
+    @pl.loop(0, tiles // 2)
     def _(j):
-        if not halo:
-            arrived(j)
-        first(j)
+        stage(2 * j, 2)
+
+    if tiles % 2:
+        stage(tiles - 1, 1)
 
     def step(j, p):
         acc = jnp.zeros((48, 256), jnp.float32)
@@ -346,8 +291,7 @@
         pltpu.VMEM((K, 16, lanes), jnp.float32),
         pltpu.SemaphoreType.DMA((blocks // 2,)),
     ]
-    halo_specs = [vmem, anywhere] if EDGE in reads else []
-    in_specs = [smem, smem, vmem] + [anywhere] * (len(arrays) - len(halo_specs)) + halo_specs + [vmem] * len(consts)
+    in_specs = [smem, smem, vmem] + [anywhere] * len(arrays) + [vmem] * len(consts)
     args = [scal, mix, jnp.asarray(relative_columns(reads)), *arrays, *[jnp.asarray(c) for c in consts]]
     joins = ()
     if earlier:
@@ -366,15 +310,6 @@
     )(*args)
 
 
-def blocks_of(x, ids):
-    runs, start = [], 0
-    for i in range(1, len(ids) + 1):
-        if i == len(ids) or ids[i] != ids[i - 1] + 1:
-            runs.append(x[..., ids[start] * LANES : (ids[i - 1] + 1) * LANES])
-            start = i
-    return runs[0] if len(runs) == 1 else jnp.concatenate(runs, axis=-1)
-
-
 def on_device(counts, weights):
     n_rows, n_cols = lax.axis_size("rows"), lax.axis_size("maps")
     height, width = n_rows * counts.shape[1], n_cols * counts.shape[2]
@@ -395,32 +330,33 @@
     def to_float(x):
         return x.astype(jnp.float32) + 1.0
 
-    zo_own = to_float(lax.dynamic_slice_in_dim(counts, (1 - core) * 8, 8, axis=1))
-    zo = lax.ppermute(zo_own, "rows", hop)
+    def outward(x):
+        return lax.dynamic_slice_in_dim(x, (1 - core) * 8, 8, axis=1)
+
+    edge = FIRST * LANES
+    zo_own = to_float(outward(counts[..., :edge]))
+    zo = [lax.ppermute(zo_own, "rows", hop)]
     n = to_float(after(counts, zo_own))
-    own = [blocks_of(n, ids) for ids in CHUNKS]
+    left = lax.ppermute(n[..., -LANES:], "maps", to_right)
+    right = lax.ppermute(n[..., :LANES], "maps", to_left)
+    lane = lax.broadcasted_iota(jnp.int32, left.shape, 2)
+    own = [n[..., :edge], jnp.concatenate([n[..., edge:], jnp.where(lane < 64, right, left)], axis=-1)]
+    zo.append(lax.ppermute(outward(own[1]), "rows", hop))
     q = [lax.ppermute(x, "rows", swap) for x in own]
     zq = [lax.ppermute(x, "rows", hop) for x in q]
+    f = [lax.ppermute(x, "rows", swap) for x in zq]
 
     sums = jnp.sum(n, axis=(1, 2))
-    rounds = [("rows", 1), ("maps", 1), ("maps", 2), ("rows", 16), ("rows", 32), ("rows", 2), ("rows", 4), ("rows", 8), ("maps", 4)]
+    rounds = [("maps", 4), ("rows", 1), ("maps", 1), ("maps", 2), ("rows", 16), ("rows", 32), ("rows", 2), ("rows", 4), ("rows", 8)]
     for axis, bit in rounds:
         sums = sums + lax.ppermute(sums, axis, [(d, d ^ bit) for d in range(lax.axis_size(axis))])
     log_scale = jnp.sum(mix * jnp.log(float(height * width) / sums))
 
-    f = [lax.ppermute(x, "rows", swap) for x in zq]
-
-    last, first = edge_columns(scal, zo, own[0], q[0], zq[0], f[0])
-    left = lax.ppermute(last, "maps", to_right)
-    right = lax.ppermute(first, "maps", to_left)
-
     outs = []
     for which in range(len(KERNELS)):
-        arrays = [zo]
+        arrays = []
         for c in KERNELS[which][1]:
-            arrays += [own[c], q[c], zq[c], f[c]]
-        if EDGE in KERNELS[which][0]:
-            arrays += [left, right]
+            arrays += [zo[c], own[c], q[c], zq[c], f[c]]
         earlier = outs if which == len(KERNELS) - 1 else []
         outs.append(run_kernel(which, height, width, scal, mix, arrays, earlier, log_scale))
     return outs[-1]

time: 217 us -> 194 us (0.89)
  the two profiles are of different devices: /device:TPU:24 before, /device:TPU:56 now
where the time goes in v3:
time: 194 us; the launch traced here: 193 us
  starting transfers between devices  79.9 us (41%)
  waiting for transfers between devices  70.8 us (36%)
  Pallas kernels  33.4 us (17%)
  other arithmetic  5.6 us (3%)
  local copies, waits for them, and re-layouts  3.15 us (2%)
    ppermute x9, starting transfers between devices, on_device(): lax.ppermute(sums, axis, [(d, d ^ bit) for d in range(lax.axis_size(axis))])  50.9 us
    ppermute x2, waiting for transfers between devices, on_device(): zq = [lax.ppermute(x, 'rows', hop) for x in q]  43.7 us
    pallas_call x2, Pallas kernels, run_kernel(): pl.pallas_call(functools.partial(kernel, reads, sources, joins, height, w...  33.4 us
    ppermute x9, waiting for transfers between devices, on_device(): lax.ppermute(sums, axis, [(d, d ^ bit) for d in range(lax.axis_size(axis))])  19.1 us
    ppermute x2, starting transfers between devices, on_device(): zq = [lax.ppermute(x, 'rows', hop) for x in q]  8.27 us
    ppermute x1, starting transfers between devices, on_device(): zo.append(lax.ppermute(outward(own[1]), 'rows', hop))  4.63 us
    ppermute x1, waiting for transfers between devices, on_device(): right = lax.ppermute(n[..., :LANES], 'maps', to_left)  4.27 us
    ppermute x2, starting transfers between devices, on_device(): q = [lax.ppermute(x, 'rows', swap) for x in own]  3.97 us
  transfers between devices with their start and end apart: 19, of which 14 were waited for; matrix products, arithmetic and copies ran while one was open for 2% of the time, Pallas kernels for 10%

profile of v3, /device:TPU:56, one launch (start us, length us, event | category | flops | bytes accessed | tf_op | source)
XLA Modules:
  0.0 193.2 jit_solution(13249719135982282884)
XLA Ops:
  2.8 2.1 %collective-permute-start.1 = (f32[8,16,2816]{2,1,0:T(8,128)S(1)}, f32[8,16,2816]{2,1,0:T(8,128)S(1)}, u32[]{:S(2)}, u32[]{:S(2)}) collective-permute-start(f32[8,16,2816]{2,1,0:T(8,128)S(1)} %slice.20.refs_1_), channel_id=1, source_target_pairs={{0,8},{8,0},{16,24},{24,16},{32,40},{40,32},{48,56},{56,48},{64,72... | collective-permute-start | bytes 4325384 | tf_op jit(solution)/shard_map/ppermute | solution.py:345
  4.9 3.2 %collective-permute-done.1.refs_2_ = f32[8,16,2816]{2,1,0:T(8,128)S(1)} collective-permute-done((f32[8,16,2816]{2,1,0:T(8,128)S(1)}, f32[8,16,2816]{2,1,0:T(8,128)S(1)}, u32[]{:S(2)}, u32[]{:S(2)}) %collective-permute-start.1) | collective-permute-done | bytes 1441824 | tf_op jit(solution)/shard_map/ppermute | solution.py:345
  8.1 3.8 %collective-permute-start.2 = (f32[8,16,2816]{2,1,0:T(8,128)S(1)}, f32[8,16,2816]{2,1,0:T(8,128)}, u32[]{:S(2)}, u32[]{:S(2)}) collective-permute-start(f32[8,16,2816]{2,1,0:T(8,128)S(1)} %collective-permute-done.1.refs_2_), channel_id=1, source_target_pairs={{0,16},{16,32},{32,48},{48,64},{64,80},{80,96},{96,112},{112,128},... | collective-permute-start | bytes 4325384 | tf_op jit(solution)/shard_map/ppermute | solution.py:346
  11.9 3.4 %collective-permute-start.5 = (f32[8,16,128]{2,1,0:T(8,128)S(1)}, f32[8,16,128]{2,1,0:T(8,128)S(1)}, u32[]{:S(2)}, u32[]{:S(2)}) collective-permute-start(f32[8,16,128]{2,1,0:T(8,128)S(1)} %get-tuple-element.9), channel_id=1, source_target_pairs={{0,1},{1,2},{2,3},{3,4},{4,5},{5,6},{6,7},{8,9},{9,10},{10,11},{11... | collective-permute-start | bytes 196616 | tf_op jit(solution)/shard_map/ppermute | solution.py:340
  17.2 4.3 %collective-permute-done.4 = f32[8,16,128]{2,1,0:T(8,128)S(1)} collective-permute-done((f32[8,16,128]{2,1,0:T(8,128)S(1)}, f32[8,16,128]{2,1,0:T(8,128)S(1)}, u32[]{:S(2)}, u32[]{:S(2)}) %collective-permute-start.4) | collective-permute-done | bytes 65568 | tf_op jit(solution)/shard_map/ppermute | solution.py:341
  21.6 1.9 collective-permute-start.7
  23.5 22.5 %collective-permute-done.2.refs_3_ = f32[8,16,2816]{2,1,0:T(8,128)} collective-permute-done((f32[8,16,2816]{2,1,0:T(8,128)S(1)}, f32[8,16,2816]{2,1,0:T(8,128)}, u32[]{:S(2)}, u32[]{:S(2)}) %collective-permute-start.2) | collective-permute-done | bytes 1441824 | tf_op jit(solution)/shard_map/ppermute | solution.py:346
  48.8 4.5 %collective-permute-start.8 = (f32[8,16,1408]{2,1,0:T(8,128)S(1)}, f32[8,16,1408]{2,1,0:T(8,128)}, u32[]{:S(2)}, u32[]{:S(2)}) collective-permute-start(f32[8,16,1408]{2,1,0:T(8,128)S(1)} %collective-permute-done.7.refs_7_), channel_id=1, source_target_pairs={{0,16},{16,32},{32,48},{48,64},{64,80},{80,96},{96,112},{112,128},... | collective-permute-start | bytes 2162696 | tf_op jit(solution)/shard_map/ppermute | solution.py:346
  53.3 3.7 %collective-permute-start = (f32[8,8,2816]{2,1,0:T(8,128)}, f32[8,8,2816]{2,1,0:T(8,128)}, u32[]{:S(2)}, u32[]{:S(2)}) collective-permute-start(f32[8,8,2816]{2,1,0:T(8,128)} %convert_add_fusion.1), channel_id=1, source_target_pairs={{0,16},{16,32},{32,48},{48,64},{64,80},{80,96},{96,112},{112,128},... | collective-permute-start | bytes 2162696 | tf_op jit(solution)/shard_map/ppermute | solution.py:338
  56.9 21.2 %collective-permute-done.8.refs_8_ = f32[8,16,1408]{2,1,0:T(8,128)} collective-permute-done((f32[8,16,1408]{2,1,0:T(8,128)S(1)}, f32[8,16,1408]{2,1,0:T(8,128)}, u32[]{:S(2)}, u32[]{:S(2)}) %collective-permute-start.8) | collective-permute-done | bytes 720928 | tf_op jit(solution)/shard_map/ppermute | solution.py:346
  80.0 5.4 %collective-permute-start.10 = (f32[8]{0:T(128)S(1)}, f32[8]{0:T(128)S(1)}, u32[]{:S(2)}, u32[]{:S(2)}) collective-permute-start(f32[8]{0:T(128)S(1)} %get-tuple-element.7), channel_id=1, source_target_pairs={{0,4},{1,5},{2,6},{3,7},{4,0},{5,1},{6,2},{7,3},{8,12},{9,13},{10,... | collective-permute-start | bytes 104 | tf_op jit(solution)/shard_map/ppermute | solution.py:352
  87.7 4.6 %collective-permute-start.6 = (f32[8,8,1408]{2,1,0:T(8,128)}, f32[8,8,1408]{2,1,0:T(8,128)S(1)}, u32[]{:S(2)}, u32[]{:S(2)}) collective-permute-start(f32[8,8,1408]{2,1,0:T(8,128)} %fusion), channel_id=1, source_target_pairs={{0,16},{16,32},{32,48},{48,64},{64,80},{80,96},{96,112},{112,128},... | collective-permute-start | bytes 1081352 | tf_op jit(solution)/shard_map/ppermute | solution.py:344
  94.2 6.9 %collective-permute-start.11 = (f32[8]{0:T(128)S(1)}, f32[8]{0:T(128)S(1)}, u32[]{:S(2)}, u32[]{:S(2)}) collective-permute-start(f32[8]{0:T(128)S(1)} %add.53), channel_id=1, source_target_pairs={{0,8},{8,0},{16,24},{24,16},{32,40},{40,32},{48,56},{56,48},{64,72... | collective-permute-start | bytes 104 | tf_op jit(solution)/shard_map/ppermute | solution.py:352
  101.9 5.3 %collective-permute-start.12 = (f32[8]{0:T(128)S(1)}, f32[8]{0:T(128)S(1)}, u32[]{:S(2)}, u32[]{:S(2)}) collective-permute-start(f32[8]{0:T(128)S(1)} %add.54), channel_id=1, source_target_pairs={{0,1},{1,0},{2,3},{3,2},{4,5},{5,4},{6,7},{7,6},{8,9},{9,8},{10,11... | collective-permute-start | bytes 104 | tf_op jit(solution)/shard_map/ppermute | solution.py:352
  108.8 8.8 %collective-permute-start.13 = (f32[8]{0:T(128)S(1)}, f32[8]{0:T(128)S(1)}, u32[]{:S(2)}, u32[]{:S(2)}) collective-permute-start(f32[8]{0:T(128)S(1)} %add.55), channel_id=1, source_target_pairs={{0,2},{1,3},{2,0},{3,1},{4,6},{5,7},{6,4},{7,5},{8,10},{9,11},{10,... | collective-permute-start | bytes 104 | tf_op jit(solution)/shard_map/ppermute | solution.py:352
  119.2 2.3 %collective-permute-start.14 = (f32[8]{0:T(128)S(1)}, f32[8]{0:T(128)S(1)}, u32[]{:S(2)}, u32[]{:S(2)}) collective-permute-start(f32[8]{0:T(128)S(1)} %add.56), channel_id=1, source_target_pairs={{0,128},{8,136},{16,144},{24,152},{32,160},{40,168},{48,176},{56,1... | collective-permute-start | bytes 104 | tf_op jit(solution)/shard_map/ppermute | solution.py:352
  121.5 3.1 %collective-permute-done.14 = f32[8]{0:T(128)S(1)} collective-permute-done((f32[8]{0:T(128)S(1)}, f32[8]{0:T(128)S(1)}, u32[]{:S(2)}, u32[]{:S(2)}) %collective-permute-start.14) | collective-permute-done | bytes 64 | tf_op jit(solution)/shard_map/ppermute | solution.py:352
  124.6 2.8 %collective-permute-start.15 = (f32[8]{0:T(128)S(1)}, f32[8]{0:T(128)S(1)}, u32[]{:S(2)}, u32[]{:S(2)}) collective-permute-start(f32[8]{0:T(128)S(1)} %add.57), channel_id=1, source_target_pairs={{0,256},{8,264},{16,272},{24,280},{32,288},{40,296},{48,304},{56,3... | collective-permute-start | bytes 104 | tf_op jit(solution)/shard_map/ppermute | solution.py:352
  127.5 4.1 %collective-permute-done.15 = f32[8]{0:T(128)S(1)} collective-permute-done((f32[8]{0:T(128)S(1)}, f32[8]{0:T(128)S(1)}, u32[]{:S(2)}, u32[]{:S(2)}) %collective-permute-start.15) | collective-permute-done | bytes 64 | tf_op jit(solution)/shard_map/ppermute | solution.py:352
  131.6 7.0 %collective-permute-start.16 = (f32[8]{0:T(128)S(1)}, f32[8]{0:T(128)S(1)}, u32[]{:S(2)}, u32[]{:S(2)}) collective-permute-start(f32[8]{0:T(128)S(1)} %add.58), channel_id=1, source_target_pairs={{0,16},{8,24},{16,0},{24,8},{32,48},{40,56},{48,32},{56,40},{64,80... | collective-permute-start | bytes 104 | tf_op jit(solution)/shard_map/ppermute | solution.py:352
  142.0 4.4 %collective-permute-done.17 = f32[8]{0:T(128)S(1)} collective-permute-done((f32[8]{0:T(128)S(1)}, f32[8]{0:T(128)S(1)}, u32[]{:S(2)}, u32[]{:S(2)}) %collective-permute-start.17) | collective-permute-done | bytes 64 | tf_op jit(solution)/shard_map/ppermute | solution.py:352
  146.5 10.4 %collective-permute-start.18 = (f32[8]{0:T(128)S(1)}, f32[8]{0:T(128)S(1)}, u32[]{:S(2)}, u32[]{:S(2)}) collective-permute-start(f32[8]{0:T(128)S(1)} %add.60), channel_id=1, source_target_pairs={{0,64},{8,72},{16,80},{24,88},{32,96},{40,104},{48,112},{56,120},{... | collective-permute-start | bytes 104 | tf_op jit(solution)/shard_map/ppermute | solution.py:352
  159.0 19.0 %shard_map.118.refs_15_ = f32[16,2816]{1,0:T(8,128)} custom-call(s32[4]{0:T(128)} %pad_add_fusion.scal, f32[8]{0:T(128)} %copy-done.7, s32[8,2816]{1,0:T(8,128)} %constant.53.clone.relcol, f32[8,8,2816]{2,1,0:T(8,128)} %collective-permute-done.refs_0_, f32[8,16,2816]{2,1,0:T(8,128)} %copy-done, f32[8,16,2816]{2,1,0:T(8,128)} %copy-done.2, ...), custom_call_target="tpu_custom_call" | custom-call | tf_op jit(solution)/shard_map/pallas_call | solution.py:304
  178.8 14.5 %shard_map.119 = f32[16,4096]{1,0:T(8,128)} custom-call(s32[4]{0:T(128)} %pad_add_fusion.scal, f32[8]{0:T(128)} %copy-done.7, s32[8,2048]{1,0:T(8,128)} %constant.58.clone.relcol, f32[8,8,2816]{2,1,0:T(8,128)} %collective-permute-done.refs_0_, f32[8,16,2816]{2,1,0:T(8,128)} %copy-done, f32[8,16,2816]{2,1,0:T(8,128)} %copy-done.2, ...), custom_call_target="tpu_custom_call" | custom-call | tf_op jit(solution)/shard_map/pallas_call | solution.py:304
  (57 shorter events, 23.8 us)
Async XLA Ops:
  2.8 84.8 %copy-start = (f32[8,16,2816]{2,1,0:T(8,128)}, f32[8,16,2816]{2,1,0:T(8,128)S(1)}, u32[]{:S(2)}) copy-start(f32[8,16,2816]{2,1,0:T(8,128)S(1)} %slice.20.refs_1_) | copy-start | bytes 4325380
  2.8 82.6 %copy-start.8 = (f32[8]{0:T(128)S(1)}, f32[8]{0:T(128)}, u32[]{:S(2)}) copy-start(f32[8]{0:T(128)} %param.13) | copy-start | bytes 100
  2.8 5.2 %collective-permute-start.1 = (f32[8,16,2816]{2,1,0:T(8,128)S(1)}, f32[8,16,2816]{2,1,0:T(8,128)S(1)}, u32[]{:S(2)}, u32[]{:S(2)}) collective-permute-start(f32[8,16,2816]{2,1,0:T(8,128)S(1)} %slice.20.refs_1_), channel_id=1, source_target_pairs={{0,8},{8,0},{16,24},{24,16},{32,40},{40,32},{48,56},{56,48},{64,72... | collective-permute-start | bytes 4325384 | tf_op jit(solution)/shard_map/ppermute | solution.py:345
  8.1 79.6 %copy-start.2 = (f32[8,16,2816]{2,1,0:T(8,128)}, f32[8,16,2816]{2,1,0:T(8,128)S(1)}, u32[]{:S(2)}) copy-start(f32[8,16,2816]{2,1,0:T(8,128)S(1)} %collective-permute-done.1.refs_2_) | copy-start | bytes 4325380
  8.1 37.9 %collective-permute-start.2 = (f32[8,16,2816]{2,1,0:T(8,128)S(1)}, f32[8,16,2816]{2,1,0:T(8,128)}, u32[]{:S(2)}, u32[]{:S(2)}) collective-permute-start(f32[8,16,2816]{2,1,0:T(8,128)S(1)} %collective-permute-done.1.refs_2_), channel_id=1, source_target_pairs={{0,16},{16,32},{32,48},{48,64},{64,80},{80,96},{96,112},{112,128},... | collective-permute-start | bytes 4325384 | tf_op jit(solution)/shard_map/ppermute | solution.py:346
  11.9 5.3 %collective-permute-start.5 = (f32[8,16,128]{2,1,0:T(8,128)S(1)}, f32[8,16,128]{2,1,0:T(8,128)S(1)}, u32[]{:S(2)}, u32[]{:S(2)}) collective-permute-start(f32[8,16,128]{2,1,0:T(8,128)S(1)} %get-tuple-element.9), channel_id=1, source_target_pairs={{0,1},{1,2},{2,3},{3,4},{4,5},{5,6},{6,7},{8,9},{9,10},{10,11},{11... | collective-permute-start | bytes 196616 | tf_op jit(solution)/shard_map/ppermute | solution.py:340
  15.3 6.2 %collective-permute-start.4 = (f32[8,16,128]{2,1,0:T(8,128)S(1)}, f32[8,16,128]{2,1,0:T(8,128)S(1)}, u32[]{:S(2)}, u32[]{:S(2)}) collective-permute-start(f32[8,16,128]{2,1,0:T(8,128)S(1)} %get-tuple-element.10), channel_id=1, source_target_pairs={{1,0},{2,1},{3,2},{4,3},{5,4},{6,5},{7,6},{9,8},{10,9},{11,10},{12... | collective-permute-start | bytes 196616 | tf_op jit(solution)/shard_map/ppermute | solution.py:341
  21.5 56.6 %copy-start.5 = (f32[8,16,128]{2,1,0:T(8,128)}, f32[8,16,128]{2,1,0:T(8,128)S(1)}, u32[]{:S(2)}) copy-start(f32[8,16,128]{2,1,0:T(8,128)S(1)} %broadcast_select_fusion) | copy-start | bytes 196612
  21.6 26.3 %collective-permute-start.7 = (f32[8,16,1408]{2,1,0:T(8,128)S(1)}, f32[8,16,1408]{2,1,0:T(8,128)S(1)}, u32[]{:S(2)}, u32[]{:S(2)}) collective-permute-start(f32[8,16,1408]{2,1,0:T(8,128)S(1)} %pad_maximum_fusion.refs_6_), channel_id=1, source_target_pairs={{0,8},{8,0},{16,24},{24,16},{32,40},{40,32},{48,56},{56,48},{64,72... | collective-permute-start | bytes 2162696 | tf_op jit(solution)/shard_map/ppermute | solution.py:345
  46.0 113.0 %collective-permute-start.3 = (f32[8,16,2816]{2,1,0:T(8,128)}, f32[8,16,2816]{2,1,0:T(8,128)}, u32[]{:S(2)}, u32[]{:S(2)}) collective-permute-start(f32[8,16,2816]{2,1,0:T(8,128)} %collective-permute-done.2.refs_3_), channel_id=1, source_target_pairs={{0,8},{8,0},{16,24},{24,16},{32,40},{40,32},{48,56},{56,48},{64,72... | collective-permute-start | bytes 4325384 | tf_op jit(solution)/shard_map/ppermute | solution.py:347
  48.8 29.3 %collective-permute-start.8 = (f32[8,16,1408]{2,1,0:T(8,128)S(1)}, f32[8,16,1408]{2,1,0:T(8,128)}, u32[]{:S(2)}, u32[]{:S(2)}) collective-permute-start(f32[8,16,1408]{2,1,0:T(8,128)S(1)} %collective-permute-done.7.refs_7_), channel_id=1, source_target_pairs={{0,16},{16,32},{32,48},{48,64},{64,80},{80,96},{96,112},{112,128},... | collective-permute-start | bytes 2162696 | tf_op jit(solution)/shard_map/ppermute | solution.py:346
  53.3 105.8 %collective-permute-start = (f32[8,8,2816]{2,1,0:T(8,128)}, f32[8,8,2816]{2,1,0:T(8,128)}, u32[]{:S(2)}, u32[]{:S(2)}) collective-permute-start(f32[8,8,2816]{2,1,0:T(8,128)} %convert_add_fusion.1), channel_id=1, source_target_pairs={{0,16},{16,32},{32,48},{48,64},{64,80},{80,96},{96,112},{112,128},... | collective-permute-start | bytes 2162696 | tf_op jit(solution)/shard_map/ppermute | solution.py:338
  78.1 99.9 %collective-permute-start.9 = (f32[8,16,1408]{2,1,0:T(8,128)}, f32[8,16,1408]{2,1,0:T(8,128)}, u32[]{:S(2)}, u32[]{:S(2)}) collective-permute-start(f32[8,16,1408]{2,1,0:T(8,128)} %collective-permute-done.8.refs_8_), channel_id=1, source_target_pairs={{0,8},{8,0},{16,24},{24,16},{32,40},{40,32},{48,56},{56,48},{64,72... | collective-permute-start | bytes 2162696 | tf_op jit(solution)/shard_map/ppermute | solution.py:347
  80.0 14.2 %collective-permute-start.10 = (f32[8]{0:T(128)S(1)}, f32[8]{0:T(128)S(1)}, u32[]{:S(2)}, u32[]{:S(2)}) collective-permute-start(f32[8]{0:T(128)S(1)} %get-tuple-element.7), channel_id=1, source_target_pairs={{0,4},{1,5},{2,6},{3,7},{4,0},{5,1},{6,2},{7,3},{8,12},{9,13},{10,... | collective-permute-start | bytes 104 | tf_op jit(solution)/shard_map/ppermute | solution.py:352
  87.7 90.4 %collective-permute-start.6 = (f32[8,8,1408]{2,1,0:T(8,128)}, f32[8,8,1408]{2,1,0:T(8,128)S(1)}, u32[]{:S(2)}, u32[]{:S(2)}) collective-permute-start(f32[8,8,1408]{2,1,0:T(8,128)} %fusion), channel_id=1, source_target_pairs={{0,16},{16,32},{32,48},{48,64},{64,80},{80,96},{96,112},{112,128},... | collective-permute-start | bytes 1081352 | tf_op jit(solution)/shard_map/ppermute | solution.py:344
  93.0 66.0 %copy-start.7 = (f32[8]{0:T(128)}, f32[8]{0:T(128)S(1)}, u32[]{:S(2)}) copy-start(f32[8]{0:T(128)S(1)} %broadcast_divide_fusion.mix) | copy-start | bytes 100
  94.2 7.7 %collective-permute-start.11 = (f32[8]{0:T(128)S(1)}, f32[8]{0:T(128)S(1)}, u32[]{:S(2)}, u32[]{:S(2)}) collective-permute-start(f32[8]{0:T(128)S(1)} %add.53), channel_id=1, source_target_pairs={{0,8},{8,0},{16,24},{24,16},{32,40},{40,32},{48,56},{56,48},{64,72... | collective-permute-start | bytes 104 | tf_op jit(solution)/shard_map/ppermute | solution.py:352
  101.9 6.9 %collective-permute-start.12 = (f32[8]{0:T(128)S(1)}, f32[8]{0:T(128)S(1)}, u32[]{:S(2)}, u32[]{:S(2)}) collective-permute-start(f32[8]{0:T(128)S(1)} %add.54), channel_id=1, source_target_pairs={{0,1},{1,0},{2,3},{3,2},{4,5},{5,4},{6,7},{7,6},{8,9},{9,8},{10,11... | collective-permute-start | bytes 104 | tf_op jit(solution)/shard_map/ppermute | solution.py:352
  108.8 10.4 %collective-permute-start.13 = (f32[8]{0:T(128)S(1)}, f32[8]{0:T(128)S(1)}, u32[]{:S(2)}, u32[]{:S(2)}) collective-permute-start(f32[8]{0:T(128)S(1)} %add.55), channel_id=1, source_target_pairs={{0,2},{1,3},{2,0},{3,1},{4,6},{5,7},{6,4},{7,5},{8,10},{9,11},{10,... | collective-permute-start | bytes 104 | tf_op jit(solution)/shard_map/ppermute | solution.py:352
  119.2 5.5 %collective-permute-start.14 = (f32[8]{0:T(128)S(1)}, f32[8]{0:T(128)S(1)}, u32[]{:S(2)}, u32[]{:S(2)}) collective-permute-start(f32[8]{0:T(128)S(1)} %add.56), channel_id=1, source_target_pairs={{0,128},{8,136},{16,144},{24,152},{32,160},{40,168},{48,176},{56,1... | collective-permute-start | bytes 104 | tf_op jit(solution)/shard_map/ppermute | solution.py:352
  124.6 7.0 %collective-permute-start.15 = (f32[8]{0:T(128)S(1)}, f32[8]{0:T(128)S(1)}, u32[]{:S(2)}, u32[]{:S(2)}) collective-permute-start(f32[8]{0:T(128)S(1)} %add.57), channel_id=1, source_target_pairs={{0,256},{8,264},{16,272},{24,280},{32,288},{40,296},{48,304},{56,3... | collective-permute-start | bytes 104 | tf_op jit(solution)/shard_map/ppermute | solution.py:352
  131.6 8.5 %collective-permute-start.16 = (f32[8]{0:T(128)S(1)}, f32[8]{0:T(128)S(1)}, u32[]{:S(2)}, u32[]{:S(2)}) collective-permute-start(f32[8]{0:T(128)S(1)} %add.58), channel_id=1, source_target_pairs={{0,16},{8,24},{16,0},{24,8},{32,48},{40,56},{48,32},{56,40},{64,80... | collective-permute-start | bytes 104 | tf_op jit(solution)/shard_map/ppermute | solution.py:352
  140.1 6.3 %collective-permute-start.17 = (f32[8]{0:T(128)S(1)}, f32[8]{0:T(128)S(1)}, u32[]{:S(2)}, u32[]{:S(2)}) collective-permute-start(f32[8]{0:T(128)S(1)} %add.59), channel_id=1, source_target_pairs={{0,32},{8,40},{16,48},{24,56},{32,0},{40,8},{48,16},{56,24},{64,96... | collective-permute-start | bytes 104 | tf_op jit(solution)/shard_map/ppermute | solution.py:352
  146.5 12.0 %collective-permute-start.18 = (f32[8]{0:T(128)S(1)}, f32[8]{0:T(128)S(1)}, u32[]{:S(2)}, u32[]{:S(2)}) collective-permute-start(f32[8]{0:T(128)S(1)} %add.60), channel_id=1, source_target_pairs={{0,64},{8,72},{16,80},{24,88},{32,96},{40,104},{48,112},{56,120},{... | collective-permute-start | bytes 104 | tf_op jit(solution)/shard_map/ppermute | solution.py:352
  (5 other events, 29.7 us)

commit v4 on v3

--- a/solution.py
+++ b/solution.py
@@ -116,8 +116,8 @@
     g1, g2, g3, bm = refs[n_in : n_in + 4]
     n_in += 4
     if joins:
-        log_scale, earlier = refs[n_in], refs[n_in + 1 : n_in + len(joins)]
-        n_in += len(joins)
+        earlier = refs[n_in : n_in + len(joins) - 1]
+        n_in += len(joins) - 1
     out = refs[n_in]
     n_ref, rr, rc, cv, h1h, h1l, h2h, h2l, h3h, h3l, u_ref, w_ref, sems = refs[n_in + 1 :][:13]
     acc_ref = refs[-1] if joins else out
@@ -259,8 +259,7 @@
     for i, moved in enumerate(joins):
         ref = acc_ref if i == len(joins) - 1 else earlier[i]
         for src, dst, count in moved:
-            piece = ref[:, src * LANES : (src + count) * LANES] + log_scale[0]
-            out[:, dst * LANES : (dst + count) * LANES] = jnp.exp(piece)
+            out[:, dst * LANES : (dst + count) * LANES] = ref[:, src * LANES : (src + count) * LANES]
 
 
 def relative_columns(reads):
@@ -269,7 +268,7 @@
     return np.tile(np.concatenate(cols).astype(np.int32)[None], (8, 1))
 
 
-def run_kernel(which, height, width, scal, mix, arrays, earlier, log_scale):
+def run_kernel(which, height, width, scal, mix, arrays, earlier):
     reads, sources = KERNELS[which]
     blocks = len(reads)
     lanes = blocks * LANES
@@ -298,8 +297,8 @@
         joins = tuple(
             tuple((KERNELS[i][0].index(lo), lo, hi - lo + 1) for lo, hi in kept) for i, kept in enumerate(KEPT)
         )
-        in_specs += [smem] + [vmem] * len(earlier)
-        args += [log_scale.reshape(1), *earlier]
+        in_specs += [vmem] * len(earlier)
+        args += earlier
         scratch.append(pltpu.VMEM((16, lanes), jnp.float32))
     return pl.pallas_call(
         functools.partial(kernel, reads, sources, joins, height, width),
@@ -358,8 +357,8 @@
         for c in KERNELS[which][1]:
             arrays += [zo[c], own[c], q[c], zq[c], f[c]]
         earlier = outs if which == len(KERNELS) - 1 else []
-        outs.append(run_kernel(which, height, width, scal, mix, arrays, earlier, log_scale))
-    return outs[-1]
+        outs.append(run_kernel(which, height, width, scal, mix, arrays, earlier))
+    return jnp.exp(outs[-1] + log_scale)
 
 
 def solution(mesh):

time: 194 us -> 196 us (1.010)
  other arithmetic: 5.6 us -> 7.85 us
    exp x0 -> x1, other arithmetic: none -> 2.25 us  [on_device(): return jnp.exp(outs[-1] + log_scale)]
where the time goes in v4:
time: 196 us; the launch traced here: 195 us
  starting transfers between devices  79.9 us (41%)
  waiting for transfers between devices  70.8 us (36%)
  Pallas kernels  32.8 us (17%)
  other arithmetic  7.85 us (4%)
  local copies, waits for them, and re-layouts  3.15 us (2%)
    ppermute x9, starting transfers between devices, on_device(): lax.ppermute(sums, axis, [(d, d ^ bit) for d in range(lax.axis_size(axis))])  50.9 us
    ppermute x2, waiting for transfers between devices, on_device(): zq = [lax.ppermute(x, 'rows', hop) for x in q]  43.7 us
    pallas_call x2, Pallas kernels, run_kernel(): pl.pallas_call(functools.partial(kernel, reads, sources, joins, height, w...  32.8 us
    ppermute x9, waiting for transfers between devices, on_device(): lax.ppermute(sums, axis, [(d, d ^ bit) for d in range(lax.axis_size(axis))])  19.1 us
    ppermute x2, starting transfers between devices, on_device(): zq = [lax.ppermute(x, 'rows', hop) for x in q]  8.27 us
    ppermute x1, starting transfers between devices, on_device(): zo.append(lax.ppermute(outward(own[1]), 'rows', hop))  4.63 us
    ppermute x1, waiting for transfers between devices, on_device(): right = lax.ppermute(n[..., :LANES], 'maps', to_left)  4.27 us
    ppermute x2, starting transfers between devices, on_device(): q = [lax.ppermute(x, 'rows', swap) for x in own]  3.97 us
  transfers between devices with their start and end apart: 19, of which 14 were waited for; matrix products, arithmetic and copies ran while one was open for 2% of the time, Pallas kernels for 10%

profile of v4, /device:TPU:56, one launch (start us, length us, event | category | flops | bytes accessed | tf_op | source)
XLA Modules:
  0.0 194.9 jit_solution(1590825216127903439)
XLA Ops:
  2.8 2.1 %collective-permute-start.1 = (f32[8,16,2816]{2,1,0:T(8,128)S(1)}, f32[8,16,2816]{2,1,0:T(8,128)S(1)}, u32[]{:S(2)}, u32[]{:S(2)}) collective-permute-start(f32[8,16,2816]{2,1,0:T(8,128)S(1)} %slice.20.refs_1_), channel_id=1, source_target_pairs={{0,8},{8,0},{16,24},{24,16},{32,40},{40,32},{48,56},{56,48},{64,72... | collective-permute-start | bytes 4325384 | tf_op jit(solution)/shard_map/ppermute | solution.py:344
  4.9 3.2 %collective-permute-done.1.refs_2_ = f32[8,16,2816]{2,1,0:T(8,128)S(1)} collective-permute-done((f32[8,16,2816]{2,1,0:T(8,128)S(1)}, f32[8,16,2816]{2,1,0:T(8,128)S(1)}, u32[]{:S(2)}, u32[]{:S(2)}) %collective-permute-start.1) | collective-permute-done | bytes 1441824 | tf_op jit(solution)/shard_map/ppermute | solution.py:344
  8.1 3.8 %collective-permute-start.2 = (f32[8,16,2816]{2,1,0:T(8,128)S(1)}, f32[8,16,2816]{2,1,0:T(8,128)}, u32[]{:S(2)}, u32[]{:S(2)}) collective-permute-start(f32[8,16,2816]{2,1,0:T(8,128)S(1)} %collective-permute-done.1.refs_2_), channel_id=1, source_target_pairs={{0,16},{16,32},{32,48},{48,64},{64,80},{80,96},{96,112},{112,128},... | collective-permute-start | bytes 4325384 | tf_op jit(solution)/shard_map/ppermute | solution.py:345
  11.9 3.4 %collective-permute-start.5 = (f32[8,16,128]{2,1,0:T(8,128)S(1)}, f32[8,16,128]{2,1,0:T(8,128)S(1)}, u32[]{:S(2)}, u32[]{:S(2)}) collective-permute-start(f32[8,16,128]{2,1,0:T(8,128)S(1)} %get-tuple-element.9), channel_id=1, source_target_pairs={{0,1},{1,2},{2,3},{3,4},{4,5},{5,6},{6,7},{8,9},{9,10},{10,11},{11... | collective-permute-start | bytes 196616 | tf_op jit(solution)/shard_map/ppermute | solution.py:339
  17.2 4.3 %collective-permute-done.4 = f32[8,16,128]{2,1,0:T(8,128)S(1)} collective-permute-done((f32[8,16,128]{2,1,0:T(8,128)S(1)}, f32[8,16,128]{2,1,0:T(8,128)S(1)}, u32[]{:S(2)}, u32[]{:S(2)}) %collective-permute-start.4) | collective-permute-done | bytes 65568 | tf_op jit(solution)/shard_map/ppermute | solution.py:340
  23.5 22.5 %collective-permute-done.2.refs_3_ = f32[8,16,2816]{2,1,0:T(8,128)} collective-permute-done((f32[8,16,2816]{2,1,0:T(8,128)S(1)}, f32[8,16,2816]{2,1,0:T(8,128)}, u32[]{:S(2)}, u32[]{:S(2)}) %collective-permute-start.2) | collective-permute-done | bytes 1441824 | tf_op jit(solution)/shard_map/ppermute | solution.py:345
  48.8 4.5 %collective-permute-start.8 = (f32[8,16,1408]{2,1,0:T(8,128)S(1)}, f32[8,16,1408]{2,1,0:T(8,128)}, u32[]{:S(2)}, u32[]{:S(2)}) collective-permute-start(f32[8,16,1408]{2,1,0:T(8,128)S(1)} %collective-permute-done.7.refs_7_), channel_id=1, source_target_pairs={{0,16},{16,32},{32,48},{48,64},{64,80},{80,96},{96,112},{112,128},... | collective-permute-start | bytes 2162696 | tf_op jit(solution)/shard_map/ppermute | solution.py:345
  53.3 3.7 %collective-permute-start = (f32[8,8,2816]{2,1,0:T(8,128)}, f32[8,8,2816]{2,1,0:T(8,128)}, u32[]{:S(2)}, u32[]{:S(2)}) collective-permute-start(f32[8,8,2816]{2,1,0:T(8,128)} %convert_add_fusion.1), channel_id=1, source_target_pairs={{0,16},{16,32},{32,48},{48,64},{64,80},{80,96},{96,112},{112,128},... | collective-permute-start | bytes 2162696 | tf_op jit(solution)/shard_map/ppermute | solution.py:337
  56.9 21.2 %collective-permute-done.8.refs_8_ = f32[8,16,1408]{2,1,0:T(8,128)} collective-permute-done((f32[8,16,1408]{2,1,0:T(8,128)S(1)}, f32[8,16,1408]{2,1,0:T(8,128)}, u32[]{:S(2)}, u32[]{:S(2)}) %collective-permute-start.8) | collective-permute-done | bytes 720928 | tf_op jit(solution)/shard_map/ppermute | solution.py:345
  80.0 5.4 %collective-permute-start.10 = (f32[8]{0:T(128)S(1)}, f32[8]{0:T(128)S(1)}, u32[]{:S(2)}, u32[]{:S(2)}) collective-permute-start(f32[8]{0:T(128)S(1)} %get-tuple-element.7), channel_id=1, source_target_pairs={{0,4},{1,5},{2,6},{3,7},{4,0},{5,1},{6,2},{7,3},{8,12},{9,13},{10,... | collective-permute-start | bytes 104 | tf_op jit(solution)/shard_map/ppermute | solution.py:351
  87.7 4.6 %collective-permute-start.6 = (f32[8,8,1408]{2,1,0:T(8,128)}, f32[8,8,1408]{2,1,0:T(8,128)S(1)}, u32[]{:S(2)}, u32[]{:S(2)}) collective-permute-start(f32[8,8,1408]{2,1,0:T(8,128)} %fusion), channel_id=1, source_target_pairs={{0,16},{16,32},{32,48},{48,64},{64,80},{80,96},{96,112},{112,128},... | collective-permute-start | bytes 1081352 | tf_op jit(solution)/shard_map/ppermute | solution.py:343
  94.2 6.9 %collective-permute-start.11 = (f32[8]{0:T(128)S(1)}, f32[8]{0:T(128)S(1)}, u32[]{:S(2)}, u32[]{:S(2)}) collective-permute-start(f32[8]{0:T(128)S(1)} %add.59), channel_id=1, source_target_pairs={{0,8},{8,0},{16,24},{24,16},{32,40},{40,32},{48,56},{56,48},{64,72... | collective-permute-start | bytes 104 | tf_op jit(solution)/shard_map/ppermute | solution.py:351
  101.9 5.3 %collective-permute-start.12 = (f32[8]{0:T(128)S(1)}, f32[8]{0:T(128)S(1)}, u32[]{:S(2)}, u32[]{:S(2)}) collective-permute-start(f32[8]{0:T(128)S(1)} %add.60), channel_id=1, source_target_pairs={{0,1},{1,0},{2,3},{3,2},{4,5},{5,4},{6,7},{7,6},{8,9},{9,8},{10,11... | collective-permute-start | bytes 104 | tf_op jit(solution)/shard_map/ppermute | solution.py:351
  108.8 8.8 %collective-permute-start.13 = (f32[8]{0:T(128)S(1)}, f32[8]{0:T(128)S(1)}, u32[]{:S(2)}, u32[]{:S(2)}) collective-permute-start(f32[8]{0:T(128)S(1)} %add.61), channel_id=1, source_target_pairs={{0,2},{1,3},{2,0},{3,1},{4,6},{5,7},{6,4},{7,5},{8,10},{9,11},{10,... | collective-permute-start | bytes 104 | tf_op jit(solution)/shard_map/ppermute | solution.py:351
  119.2 2.3 %collective-permute-start.14 = (f32[8]{0:T(128)S(1)}, f32[8]{0:T(128)S(1)}, u32[]{:S(2)}, u32[]{:S(2)}) collective-permute-start(f32[8]{0:T(128)S(1)} %add.62), channel_id=1, source_target_pairs={{0,128},{8,136},{16,144},{24,152},{32,160},{40,168},{48,176},{56,1... | collective-permute-start | bytes 104 | tf_op jit(solution)/shard_map/ppermute | solution.py:351
  121.5 3.1 %collective-permute-done.14 = f32[8]{0:T(128)S(1)} collective-permute-done((f32[8]{0:T(128)S(1)}, f32[8]{0:T(128)S(1)}, u32[]{:S(2)}, u32[]{:S(2)}) %collective-permute-start.14) | collective-permute-done | bytes 64 | tf_op jit(solution)/shard_map/ppermute | solution.py:351
  124.6 2.8 %collective-permute-start.15 = (f32[8]{0:T(128)S(1)}, f32[8]{0:T(128)S(1)}, u32[]{:S(2)}, u32[]{:S(2)}) collective-permute-start(f32[8]{0:T(128)S(1)} %add.63), channel_id=1, source_target_pairs={{0,256},{8,264},{16,272},{24,280},{32,288},{40,296},{48,304},{56,3... | collective-permute-start | bytes 104 | tf_op jit(solution)/shard_map/ppermute | solution.py:351
  127.5 4.1 %collective-permute-done.15 = f32[8]{0:T(128)S(1)} collective-permute-done((f32[8]{0:T(128)S(1)}, f32[8]{0:T(128)S(1)}, u32[]{:S(2)}, u32[]{:S(2)}) %collective-permute-start.15) | collective-permute-done | bytes 64 | tf_op jit(solution)/shard_map/ppermute | solution.py:351
  131.6 7.0 %collective-permute-start.16 = (f32[8]{0:T(128)S(1)}, f32[8]{0:T(128)S(1)}, u32[]{:S(2)}, u32[]{:S(2)}) collective-permute-start(f32[8]{0:T(128)S(1)} %add.64), channel_id=1, source_target_pairs={{0,16},{8,24},{16,0},{24,8},{32,48},{40,56},{48,32},{56,40},{64,80... | collective-permute-start | bytes 104 | tf_op jit(solution)/shard_map/ppermute | solution.py:351
  142.0 4.4 %collective-permute-done.17 = f32[8]{0:T(128)S(1)} collective-permute-done((f32[8]{0:T(128)S(1)}, f32[8]{0:T(128)S(1)}, u32[]{:S(2)}, u32[]{:S(2)}) %collective-permute-start.17) | collective-permute-done | bytes 64 | tf_op jit(solution)/shard_map/ppermute | solution.py:351
  146.5 10.4 %collective-permute-start.18 = (f32[8]{0:T(128)S(1)}, f32[8]{0:T(128)S(1)}, u32[]{:S(2)}, u32[]{:S(2)}) collective-permute-start(f32[8]{0:T(128)S(1)} %add.66), channel_id=1, source_target_pairs={{0,64},{8,72},{16,80},{24,88},{32,96},{40,104},{48,112},{56,120},{... | collective-permute-start | bytes 104 | tf_op jit(solution)/shard_map/ppermute | solution.py:351
  159.0 19.0 %shard_map.118.refs_14_ = f32[16,2816]{1,0:T(8,128)} custom-call(s32[4]{0:T(128)} %pad_add_fusion.scal, f32[8]{0:T(128)} %copy-done.7, s32[8,2816]{1,0:T(8,128)} %constant.53.clone.relcol, f32[8,8,2816]{2,1,0:T(8,128)} %collective-permute-done.refs_0_, f32[8,16,2816]{2,1,0:T(8,128)} %copy-done, f32[8,16,2816]{2,1,0:T(8,128)} %copy-done.2, ...), custom_call_target="tpu_custom_call" | custom-call | tf_op jit(solution)/shard_map/pallas_call | solution.py:303
  178.8 13.9 %shard_map.119 = f32[16,4096]{1,0:T(8,128)} custom-call(s32[4]{0:T(128)} %pad_add_fusion.scal, f32[8]{0:T(128)} %copy-done.7, s32[8,2048]{1,0:T(8,128)} %constant.58.clone.relcol, f32[8,8,2816]{2,1,0:T(8,128)} %collective-permute-done.refs_0_, f32[8,16,2816]{2,1,0:T(8,128)} %copy-done, f32[8,16,2816]{2,1,0:T(8,128)} %copy-done.2, ...), custom_call_target="tpu_custom_call" | custom-call | tf_op jit(solution)/shard_map/pallas_call | solution.py:303
  192.6 2.3 %add_exponential_fusion = f32[16,4096]{1,0:T(8,128)} fusion(f32[16,4096]{1,0:T(8,128)} %shard_map.119, f32[]{:T(128)} %multiply_reduce_fusion), kind=kLoop, calls=%fused_computation.6 | loop fusion | flops 65536 | bytes 524292 | tf_op jit(solution)/shard_map/exp | solution.py:361
  (58 shorter events, 25.7 us)
Async XLA Ops:
  2.8 84.8 %copy-start = (f32[8,16,2816]{2,1,0:T(8,128)}, f32[8,16,2816]{2,1,0:T(8,128)S(1)}, u32[]{:S(2)}) copy-start(f32[8,16,2816]{2,1,0:T(8,128)S(1)} %slice.20.refs_1_) | copy-start | bytes 4325380
  2.8 82.6 %copy-start.8 = (f32[8]{0:T(128)S(1)}, f32[8]{0:T(128)}, u32[]{:S(2)}) copy-start(f32[8]{0:T(128)} %param.13) | copy-start | bytes 100
  2.8 5.2 %collective-permute-start.1 = (f32[8,16,2816]{2,1,0:T(8,128)S(1)}, f32[8,16,2816]{2,1,0:T(8,128)S(1)}, u32[]{:S(2)}, u32[]{:S(2)}) collective-permute-start(f32[8,16,2816]{2,1,0:T(8,128)S(1)} %slice.20.refs_1_), channel_id=1, source_target_pairs={{0,8},{8,0},{16,24},{24,16},{32,40},{40,32},{48,56},{56,48},{64,72... | collective-permute-start | bytes 4325384 | tf_op jit(solution)/shard_map/ppermute | solution.py:344
  8.1 79.6 %copy-start.2 = (f32[8,16,2816]{2,1,0:T(8,128)}, f32[8,16,2816]{2,1,0:T(8,128)S(1)}, u32[]{:S(2)}) copy-start(f32[8,16,2816]{2,1,0:T(8,128)S(1)} %collective-permute-done.1.refs_2_) | copy-start | bytes 4325380
  8.1 37.9 %collective-permute-start.2 = (f32[8,16,2816]{2,1,0:T(8,128)S(1)}, f32[8,16,2816]{2,1,0:T(8,128)}, u32[]{:S(2)}, u32[]{:S(2)}) collective-permute-start(f32[8,16,2816]{2,1,0:T(8,128)S(1)} %collective-permute-done.1.refs_2_), channel_id=1, source_target_pairs={{0,16},{16,32},{32,48},{48,64},{64,80},{80,96},{96,112},{112,128},... | collective-permute-start | bytes 4325384 | tf_op jit(solution)/shard_map/ppermute | solution.py:345
  11.9 5.3 %collective-permute-start.5 = (f32[8,16,128]{2,1,0:T(8,128)S(1)}, f32[8,16,128]{2,1,0:T(8,128)S(1)}, u32[]{:S(2)}, u32[]{:S(2)}) collective-permute-start(f32[8,16,128]{2,1,0:T(8,128)S(1)} %get-tuple-element.9), channel_id=1, source_target_pairs={{0,1},{1,2},{2,3},{3,4},{4,5},{5,6},{6,7},{8,9},{9,10},{10,11},{11... | collective-permute-start | bytes 196616 | tf_op jit(solution)/shard_map/ppermute | solution.py:339
  15.3 6.2 %collective-permute-start.4 = (f32[8,16,128]{2,1,0:T(8,128)S(1)}, f32[8,16,128]{2,1,0:T(8,128)S(1)}, u32[]{:S(2)}, u32[]{:S(2)}) collective-permute-start(f32[8,16,128]{2,1,0:T(8,128)S(1)} %get-tuple-element.10), channel_id=1, source_target_pairs={{1,0},{2,1},{3,2},{4,3},{5,4},{6,5},{7,6},{9,8},{10,9},{11,10},{12... | collective-permute-start | bytes 196616 | tf_op jit(solution)/shard_map/ppermute | solution.py:340
  21.5 56.6 %copy-start.5 = (f32[8,16,128]{2,1,0:T(8,128)}, f32[8,16,128]{2,1,0:T(8,128)S(1)}, u32[]{:S(2)}) copy-start(f32[8,16,128]{2,1,0:T(8,128)S(1)} %broadcast_select_fusion) | copy-start | bytes 196612
  21.6 26.3 %collective-permute-start.7 = (f32[8,16,1408]{2,1,0:T(8,128)S(1)}, f32[8,16,1408]{2,1,0:T(8,128)S(1)}, u32[]{:S(2)}, u32[]{:S(2)}) collective-permute-start(f32[8,16,1408]{2,1,0:T(8,128)S(1)} %pad_maximum_fusion.refs_6_), channel_id=1, source_target_pairs={{0,8},{8,0},{16,24},{24,16},{32,40},{40,32},{48,56},{56,48},{64,72... | collective-permute-start | bytes 2162696 | tf_op jit(solution)/shard_map/ppermute | solution.py:344
  46.0 113.0 %collective-permute-start.3 = (f32[8,16,2816]{2,1,0:T(8,128)}, f32[8,16,2816]{2,1,0:T(8,128)}, u32[]{:S(2)}, u32[]{:S(2)}) collective-permute-start(f32[8,16,2816]{2,1,0:T(8,128)} %collective-permute-done.2.refs_3_), channel_id=1, source_target_pairs={{0,8},{8,0},{16,24},{24,16},{32,40},{40,32},{48,56},{56,48},{64,72... | collective-permute-start | bytes 4325384 | tf_op jit(solution)/shard_map/ppermute | solution.py:346
  48.8 29.3 %collective-permute-start.8 = (f32[8,16,1408]{2,1,0:T(8,128)S(1)}, f32[8,16,1408]{2,1,0:T(8,128)}, u32[]{:S(2)}, u32[]{:S(2)}) collective-permute-start(f32[8,16,1408]{2,1,0:T(8,128)S(1)} %collective-permute-done.7.refs_7_), channel_id=1, source_target_pairs={{0,16},{16,32},{32,48},{48,64},{64,80},{80,96},{96,112},{112,128},... | collective-permute-start | bytes 2162696 | tf_op jit(solution)/shard_map/ppermute | solution.py:345
  53.3 105.8 %collective-permute-start = (f32[8,8,2816]{2,1,0:T(8,128)}, f32[8,8,2816]{2,1,0:T(8,128)}, u32[]{:S(2)}, u32[]{:S(2)}) collective-permute-start(f32[8,8,2816]{2,1,0:T(8,128)} %convert_add_fusion.1), channel_id=1, source_target_pairs={{0,16},{16,32},{32,48},{48,64},{64,80},{80,96},{96,112},{112,128},... | collective-permute-start | bytes 2162696 | tf_op jit(solution)/shard_map/ppermute | solution.py:337
  78.1 99.9 %collective-permute-start.9 = (f32[8,16,1408]{2,1,0:T(8,128)}, f32[8,16,1408]{2,1,0:T(8,128)}, u32[]{:S(2)}, u32[]{:S(2)}) collective-permute-start(f32[8,16,1408]{2,1,0:T(8,128)} %collective-permute-done.8.refs_8_), channel_id=1, source_target_pairs={{0,8},{8,0},{16,24},{24,16},{32,40},{40,32},{48,56},{56,48},{64,72... | collective-permute-start | bytes 2162696 | tf_op jit(solution)/shard_map/ppermute | solution.py:346
  80.0 14.2 %collective-permute-start.10 = (f32[8]{0:T(128)S(1)}, f32[8]{0:T(128)S(1)}, u32[]{:S(2)}, u32[]{:S(2)}) collective-permute-start(f32[8]{0:T(128)S(1)} %get-tuple-element.7), channel_id=1, source_target_pairs={{0,4},{1,5},{2,6},{3,7},{4,0},{5,1},{6,2},{7,3},{8,12},{9,13},{10,... | collective-permute-start | bytes 104 | tf_op jit(solution)/shard_map/ppermute | solution.py:351
  87.7 90.4 %collective-permute-start.6 = (f32[8,8,1408]{2,1,0:T(8,128)}, f32[8,8,1408]{2,1,0:T(8,128)S(1)}, u32[]{:S(2)}, u32[]{:S(2)}) collective-permute-start(f32[8,8,1408]{2,1,0:T(8,128)} %fusion), channel_id=1, source_target_pairs={{0,16},{16,32},{32,48},{48,64},{64,80},{80,96},{96,112},{112,128},... | collective-permute-start | bytes 1081352 | tf_op jit(solution)/shard_map/ppermute | solution.py:343
  93.0 66.0 %copy-start.7 = (f32[8]{0:T(128)}, f32[8]{0:T(128)S(1)}, u32[]{:S(2)}) copy-start(f32[8]{0:T(128)S(1)} %broadcast_divide_fusion.mix) | copy-start | bytes 100
  94.2 7.7 %collective-permute-start.11 = (f32[8]{0:T(128)S(1)}, f32[8]{0:T(128)S(1)}, u32[]{:S(2)}, u32[]{:S(2)}) collective-permute-start(f32[8]{0:T(128)S(1)} %add.59), channel_id=1, source_target_pairs={{0,8},{8,0},{16,24},{24,16},{32,40},{40,32},{48,56},{56,48},{64,72... | collective-permute-start | bytes 104 | tf_op jit(solution)/shard_map/ppermute | solution.py:351
  101.9 6.9 %collective-permute-start.12 = (f32[8]{0:T(128)S(1)}, f32[8]{0:T(128)S(1)}, u32[]{:S(2)}, u32[]{:S(2)}) collective-permute-start(f32[8]{0:T(128)S(1)} %add.60), channel_id=1, source_target_pairs={{0,1},{1,0},{2,3},{3,2},{4,5},{5,4},{6,7},{7,6},{8,9},{9,8},{10,11... | collective-permute-start | bytes 104 | tf_op jit(solution)/shard_map/ppermute | solution.py:351
  108.8 10.4 %collective-permute-start.13 = (f32[8]{0:T(128)S(1)}, f32[8]{0:T(128)S(1)}, u32[]{:S(2)}, u32[]{:S(2)}) collective-permute-start(f32[8]{0:T(128)S(1)} %add.61), channel_id=1, source_target_pairs={{0,2},{1,3},{2,0},{3,1},{4,6},{5,7},{6,4},{7,5},{8,10},{9,11},{10,... | collective-permute-start | bytes 104 | tf_op jit(solution)/shard_map/ppermute | solution.py:351
  119.2 5.5 %collective-permute-start.14 = (f32[8]{0:T(128)S(1)}, f32[8]{0:T(128)S(1)}, u32[]{:S(2)}, u32[]{:S(2)}) collective-permute-start(f32[8]{0:T(128)S(1)} %add.62), channel_id=1, source_target_pairs={{0,128},{8,136},{16,144},{24,152},{32,160},{40,168},{48,176},{56,1... | collective-permute-start | bytes 104 | tf_op jit(solution)/shard_map/ppermute | solution.py:351
  124.6 7.0 %collective-permute-start.15 = (f32[8]{0:T(128)S(1)}, f32[8]{0:T(128)S(1)}, u32[]{:S(2)}, u32[]{:S(2)}) collective-permute-start(f32[8]{0:T(128)S(1)} %add.63), channel_id=1, source_target_pairs={{0,256},{8,264},{16,272},{24,280},{32,288},{40,296},{48,304},{56,3... | collective-permute-start | bytes 104 | tf_op jit(solution)/shard_map/ppermute | solution.py:351
  131.6 8.5 %collective-permute-start.16 = (f32[8]{0:T(128)S(1)}, f32[8]{0:T(128)S(1)}, u32[]{:S(2)}, u32[]{:S(2)}) collective-permute-start(f32[8]{0:T(128)S(1)} %add.64), channel_id=1, source_target_pairs={{0,16},{8,24},{16,0},{24,8},{32,48},{40,56},{48,32},{56,40},{64,80... | collective-permute-start | bytes 104 | tf_op jit(solution)/shard_map/ppermute | solution.py:351
  140.1 6.3 %collective-permute-start.17 = (f32[8]{0:T(128)S(1)}, f32[8]{0:T(128)S(1)}, u32[]{:S(2)}, u32[]{:S(2)}) collective-permute-start(f32[8]{0:T(128)S(1)} %add.65), channel_id=1, source_target_pairs={{0,32},{8,40},{16,48},{24,56},{32,0},{40,8},{48,16},{56,24},{64,96... | collective-permute-start | bytes 104 | tf_op jit(solution)/shard_map/ppermute | solution.py:351
  146.5 12.0 %collective-permute-start.18 = (f32[8]{0:T(128)S(1)}, f32[8]{0:T(128)S(1)}, u32[]{:S(2)}, u32[]{:S(2)}) collective-permute-start(f32[8]{0:T(128)S(1)} %add.66), channel_id=1, source_target_pairs={{0,64},{8,72},{16,80},{24,88},{32,96},{40,104},{48,112},{56,120},{... | collective-permute-start | bytes 104 | tf_op jit(solution)/shard_map/ppermute | solution.py:351
  (5 other events, 29.7 us)

commit v5 on v4

--- a/solution.py
+++ b/solution.py
@@ -143,7 +143,7 @@
     for ref in (h1h, h1l, h2h, h2l, h3h, h3l):
         rows = ref.shape[0]
         ref[:, 0:LANES] = jnp.zeros((rows, LANES), jnp.bfloat16)
-        ref[:, pl.ds((blocks + 1) * LANES, LANES)] = jnp.zeros((rows, LANES), jnp.bfloat16)
+        ref[:, pl.ds((blocks + 1) * LANES, 3 * LANES)] = jnp.zeros((rows, 3 * LANES), jnp.bfloat16)
 
     def tile(j):
         return pl.ds(pl.multiple_of(j * 256, 256), 256)
@@ -159,6 +159,24 @@
         el = jnp.where(first, low[:, at(j, 3 * LANES, LANES)], low[:, at(j, 0, LANES)])
         return dot(jnp.concatenate([mh, ml, mh, eh, el, eh], axis=1), bm[...])
 
+    def pipelined(high, low, step):
+        rows = high.shape[0]
+
+        def column(j, p):
+            u_ref[p, 0:rows, :] = column_pass(high, low, j)
+
+        column(0, 0)
+
+        @pl.loop(0, tiles // 2)
+        def _(i):
+            column(2 * i + 1, 1)
+            step(2 * i, 0)
+            column(2 * i + 2, 0)
+            step(2 * i + 1, 1)
+
+        if tiles % 2:
+            step(tiles - 1, 0)
+
     def arrived(j):
         window = n_ref.at[:, :, tile(j)]
         pltpu.make_async_copy(window, window, sems.at[j]).wait()
@@ -198,18 +216,7 @@
             h2h[32 * k : 32 * k + 32, at(j, LANES, 256)] = hh
             h2l[32 * k : 32 * k + 32, at(j, LANES, 256)] = hl
 
-    def stage(j, count):
-        for p in range(count):
-            u_ref[p] = column_pass(h1h, h1l, j + p)
-        for p in range(count):
-            step(j + p, p)
-
-    @pl.loop(0, tiles // 2)
-    def _(j):
-        stage(2 * j, 2)
-
-    if tiles % 2:
-        stage(tiles - 1, 1)
+    pipelined(h1h, h1l, step)
 
     zrow = pl.ds(pl.multiple_of(jnp.where(core == 0, 16, 8), 8), 8)
     qrow = pl.ds(pl.multiple_of(jnp.where(core == 0, 40, 48), 8), 8)
@@ -223,18 +230,7 @@
             h3h[16 * k : 16 * k + 16, at(j, LANES, 256)] = hh
             h3l[16 * k : 16 * k + 16, at(j, LANES, 256)] = hl
 
-    def stage(j, count):
-        for p in range(count):
-            u_ref[p, 0 : 32 * K, :] = column_pass(h2h, h2l, j + p)
-        for p in range(count):
-            step(j + p, p)
-
-    @pl.loop(0, tiles // 2)
-    def _(j):
-        stage(2 * j, 2)
-
-    if tiles % 2:
-        stage(tiles - 1, 1)
+    pipelined(h2h, h2l, step)
 
     def step(j, p):
         acc = jnp.zeros((16, 256), jnp.float32)
@@ -242,18 +238,7 @@
             acc = acc + mix[k] * jnp.log(w_ref[k, :, tile(j)] * u_ref[p, 16 * k : 16 * k + 16, :])
         acc_ref[:, tile(j)] = acc
 
-    def stage(j, count):
-        for p in range(count):
-            u_ref[p, 0 : 16 * K, :] = column_pass(h3h, h3l, j + p)
-        for p in range(count):
-            step(j + p, p)
-
-    @pl.loop(0, tiles // 2)
-    def _(j):
-        stage(2 * j, 2)
-
-    if tiles % 2:
-        stage(tiles - 1, 1)
+    pipelined(h3h, h3l, step)
 
 
     for i, moved in enumerate(joins):
@@ -272,7 +257,7 @@
     reads, sources = KERNELS[which]
     blocks = len(reads)
     lanes = blocks * LANES
-    wide = (blocks + 2) * LANES
+    wide = (blocks + 4) * LANES
     consts = matrices()
     smem = pl.BlockSpec(memory_space=pltpu.SMEM)
     vmem = pl.BlockSpec(memory_space=pltpu.VMEM)
@@ -345,10 +330,22 @@
     zq = [lax.ppermute(x, "rows", hop) for x in q]
     f = [lax.ppermute(x, "rows", swap) for x in zq]
 
+    def exchange(x, axis, bits):
+        size = lax.axis_size(axis)
+        got = [lax.ppermute(x, axis, [(d, d ^ bit) for d in range(size)]) for bit in bits]
+        return functools.reduce(jnp.add, got, x)
+
     sums = jnp.sum(n, axis=(1, 2))
-    rounds = [("maps", 4), ("rows", 1), ("maps", 1), ("maps", 2), ("rows", 16), ("rows", 32), ("rows", 2), ("rows", 4), ("rows", 8)]
-    for axis, bit in rounds:
-        sums = sums + lax.ppermute(sums, axis, [(d, d ^ bit) for d in range(lax.axis_size(axis))])
+    for axis, bits in (
+        ("maps", (4,)),
+        ("rows", (1,)),
+        ("maps", (1,)),
+        ("maps", (2,)),
+        ("rows", (16, 32, 48)),
+        ("rows", (8,)),
+        ("rows", (2, 4, 6)),
+    ):
+        sums = exchange(sums, axis, bits)
     log_scale = jnp.sum(mix * jnp.log(float(height * width) / sums))
 
     outs = []

time: 196 us -> 201 us (1.026)
  the two profiles are of different devices: /device:TPU:56 before, /device:TPU:24 now
where the time goes in v5:
time: 201 us; the launch traced here: 200 us
  waiting for transfers between devices  83.2 us (41%)
  starting transfers between devices  75.7 us (38%)
  Pallas kernels  31.2 us (16%)
  other arithmetic  7.64 us (4%)
  local copies, waits for them, and re-layouts  2.31 us (1%)
    ppermute x11, waiting for transfers between devices, exchange(): lax.ppermute(x, axis, [(d, d ^ bit) for d in range(size)])  49.4 us
    ppermute x11, starting transfers between devices, exchange(): lax.ppermute(x, axis, [(d, d ^ bit) for d in range(size)])  43 us
    pallas_call x2, Pallas kernels, run_kernel(): pl.pallas_call(functools.partial(kernel, reads, sources, joins, height, w...  31.2 us
    ppermute x2, waiting for transfers between devices, on_device(): zq = [lax.ppermute(x, 'rows', hop) for x in q]  30.9 us
    ppermute x2, starting transfers between devices, on_device(): q = [lax.ppermute(x, 'rows', swap) for x in own]  12.5 us
    ppermute x2, starting transfers between devices, on_device(): f = [lax.ppermute(x, 'rows', swap) for x in zq]  5.95 us
    ppermute x2, starting transfers between devices, on_device(): zq = [lax.ppermute(x, 'rows', hop) for x in q]  5.74 us
  transfers between devices with their start and end apart: 21, of which 14 were waited for; matrix products, arithmetic and copies ran while one was open for 2% of the time, Pallas kernels for 9%

profile of v5, /device:TPU:24, one launch (start us, length us, event | category | flops | bytes accessed | tf_op | source)
XLA Modules:
  0.0 200.4 jit_solution(3668371275449794967)
XLA Ops:
  2.8 2.1 %collective-permute-start.1 = (f32[8,16,2816]{2,1,0:T(8,128)S(1)}, f32[8,16,2816]{2,1,0:T(8,128)S(1)}, u32[]{:S(2)}, u32[]{:S(2)}) collective-permute-start(f32[8,16,2816]{2,1,0:T(8,128)S(1)} %slice.20.refs_1_), channel_id=1, source_target_pairs={{0,8},{8,0},{16,24},{24,16},{32,40},{40,32},{48,56},{56,48},{64,72... | collective-permute-start | bytes 4325384 | tf_op jit(solution)/shard_map/ppermute | solution.py:329
  4.9 3.4 %collective-permute-start.5 = (f32[8,16,128]{2,1,0:T(8,128)S(1)}, f32[8,16,128]{2,1,0:T(8,128)S(1)}, u32[]{:S(2)}, u32[]{:S(2)}) collective-permute-start(f32[8,16,128]{2,1,0:T(8,128)S(1)} %get-tuple-element.9), channel_id=1, source_target_pairs={{0,1},{1,2},{2,3},{3,4},{4,5},{5,6},{6,7},{8,9},{9,10},{10,11},{11... | collective-permute-start | bytes 196616 | tf_op jit(solution)/shard_map/ppermute | solution.py:324
  9.6 3.8 %collective-permute-start.2 = (f32[8,16,2816]{2,1,0:T(8,128)S(1)}, f32[8,16,2816]{2,1,0:T(8,128)}, u32[]{:S(2)}, u32[]{:S(2)}) collective-permute-start(f32[8,16,2816]{2,1,0:T(8,128)S(1)} %collective-permute-done.1.refs_2_), channel_id=1, source_target_pairs={{0,16},{16,32},{32,48},{48,64},{64,80},{80,96},{96,112},{112,128},... | collective-permute-start | bytes 4325384 | tf_op jit(solution)/shard_map/ppermute | solution.py:330
  14.6 10.4 %collective-permute-start.7 = (f32[8,16,1408]{2,1,0:T(8,128)S(1)}, f32[8,16,1408]{2,1,0:T(8,128)}, u32[]{:S(2)}, u32[]{:S(2)}) collective-permute-start(f32[8,16,1408]{2,1,0:T(8,128)S(1)} %pad_maximum_fusion.refs_6_), channel_id=1, source_target_pairs={{0,8},{8,0},{16,24},{24,16},{32,40},{40,32},{48,56},{56,48},{64,72... | collective-permute-start | bytes 2162696 | tf_op jit(solution)/shard_map/ppermute | solution.py:329
  25.0 1.9 collective-permute-done.7.refs_7_
  28.9 30.9 %collective-permute-done.2.refs_3_ = f32[8,16,2816]{2,1,0:T(8,128)} collective-permute-done((f32[8,16,2816]{2,1,0:T(8,128)S(1)}, f32[8,16,2816]{2,1,0:T(8,128)}, u32[]{:S(2)}, u32[]{:S(2)}) %collective-permute-start.2) | collective-permute-done | bytes 1441824 | tf_op jit(solution)/shard_map/ppermute | solution.py:330
  61.7 1.9 collective-permute-start
  63.6 21.6 %collective-permute-start.10 = (f32[8]{0:T(128)S(1)}, f32[8]{0:T(128)S(1)}, u32[]{:S(2)}, u32[]{:S(2)}) collective-permute-start(f32[8]{0:T(128)S(1)} %get-tuple-element.7), channel_id=1, source_target_pairs={{0,4},{1,5},{2,6},{3,7},{4,0},{5,1},{6,2},{7,3},{8,12},{9,13},{10,... | collective-permute-start | bytes 104 | tf_op jit(solution)/shard_map/ppermute | solution.py:335
  85.8 4.0 %collective-permute-start.9 = (f32[8,16,1408]{2,1,0:T(8,128)}, f32[8,16,1408]{2,1,0:T(8,128)}, u32[]{:S(2)}, u32[]{:S(2)}) collective-permute-start(f32[8,16,1408]{2,1,0:T(8,128)} %collective-permute-done.8.refs_8_), channel_id=1, source_target_pairs={{0,8},{8,0},{16,24},{24,16},{32,40},{40,32},{48,56},{56,48},{64,72... | collective-permute-start | bytes 2162696 | tf_op jit(solution)/shard_map/ppermute | solution.py:331
  94.5 6.0 %collective-permute-done.10 = f32[8]{0:T(128)S(1)} collective-permute-done((f32[8]{0:T(128)S(1)}, f32[8]{0:T(128)S(1)}, u32[]{:S(2)}, u32[]{:S(2)}) %collective-permute-start.10) | collective-permute-done | bytes 64 | tf_op jit(solution)/shard_map/ppermute | solution.py:335
  100.5 4.2 %collective-permute-start.11 = (f32[8]{0:T(128)S(1)}, f32[8]{0:T(128)S(1)}, u32[]{:S(2)}, u32[]{:S(2)}) collective-permute-start(f32[8]{0:T(128)S(1)} %add.65), channel_id=1, source_target_pairs={{0,8},{8,0},{16,24},{24,16},{32,40},{40,32},{48,56},{56,48},{64,72... | collective-permute-start | bytes 104 | tf_op jit(solution)/shard_map/ppermute | solution.py:335
  107.4 3.5 %collective-permute-done.12 = f32[8]{0:T(128)S(1)} collective-permute-done((f32[8]{0:T(128)S(1)}, f32[8]{0:T(128)S(1)}, u32[]{:S(2)}, u32[]{:S(2)}) %collective-permute-start.12) | collective-permute-done | bytes 64 | tf_op jit(solution)/shard_map/ppermute | solution.py:335
  112.9 5.0 %collective-permute-done.13 = f32[8]{0:T(128)S(1)} collective-permute-done((f32[8]{0:T(128)S(1)}, f32[8]{0:T(128)S(1)}, u32[]{:S(2)}, u32[]{:S(2)}) %collective-permute-start.13) | collective-permute-done | bytes 64 | tf_op jit(solution)/shard_map/ppermute | solution.py:335
  119.8 4.7 %collective-permute-done.16 = f32[8]{0:T(128)S(1)} collective-permute-done((f32[8]{0:T(128)S(1)}, f32[8]{0:T(128)S(1)}, u32[]{:S(2)}, u32[]{:S(2)}) %collective-permute-start.16) | collective-permute-done | bytes 64 | tf_op jit(solution)/shard_map/ppermute | solution.py:335
  124.6 1.9 collective-permute-start.15
  126.5 5.0 %collective-permute-done.15 = f32[8]{0:T(128)S(1)} collective-permute-done((f32[8]{0:T(128)S(1)}, f32[8]{0:T(128)S(1)}, u32[]{:S(2)}, u32[]{:S(2)}) %collective-permute-start.15) | collective-permute-done | bytes 64 | tf_op jit(solution)/shard_map/ppermute | solution.py:335
  133.4 3.5 %collective-permute-done.14 = f32[8]{0:T(128)S(1)} collective-permute-done((f32[8]{0:T(128)S(1)}, f32[8]{0:T(128)S(1)}, u32[]{:S(2)}, u32[]{:S(2)}) %collective-permute-start.14) | collective-permute-done | bytes 64 | tf_op jit(solution)/shard_map/ppermute | solution.py:335
  138.9 7.4 %collective-permute-done.17 = f32[8]{0:T(128)S(1)} collective-permute-done((f32[8]{0:T(128)S(1)}, f32[8]{0:T(128)S(1)}, u32[]{:S(2)}, u32[]{:S(2)}) %collective-permute-start.17) | collective-permute-done | bytes 64 | tf_op jit(solution)/shard_map/ppermute | solution.py:335
  148.2 5.3 %collective-permute-done.20 = f32[8]{0:T(128)S(1)} collective-permute-done((f32[8]{0:T(128)S(1)}, f32[8]{0:T(128)S(1)}, u32[]{:S(2)}, u32[]{:S(2)}) %collective-permute-start.20) | collective-permute-done | bytes 64 | tf_op jit(solution)/shard_map/ppermute | solution.py:335
  155.5 4.4 %collective-permute-done.19 = f32[8]{0:T(128)S(1)} collective-permute-done((f32[8]{0:T(128)S(1)}, f32[8]{0:T(128)S(1)}, u32[]{:S(2)}, u32[]{:S(2)}) %collective-permute-start.19) | collective-permute-done | bytes 64 | tf_op jit(solution)/shard_map/ppermute | solution.py:335
  161.8 3.5 %collective-permute-done.18 = f32[8]{0:T(128)S(1)} collective-permute-done((f32[8]{0:T(128)S(1)}, f32[8]{0:T(128)S(1)}, u32[]{:S(2)}, u32[]{:S(2)}) %collective-permute-start.18) | collective-permute-done | bytes 64 | tf_op jit(solution)/shard_map/ppermute | solution.py:335
  166.0 17.1 %shard_map.118.refs_14_ = f32[16,2816]{1,0:T(8,128)} custom-call(s32[4]{0:T(128)} %pad_add_fusion.scal, f32[8]{0:T(128)} %copy-done.6, s32[8,2816]{1,0:T(8,128)} %constant.53.clone.relcol, f32[8,8,2816]{2,1,0:T(8,128)} %collective-permute-done.refs_0_, f32[8,16,2816]{2,1,0:T(8,128)} %copy-done, f32[8,16,2816]{2,1,0:T(8,128)} %copy-done.2, ...), custom_call_target="tpu_custom_call" | custom-call | tf_op jit(solution)/shard_map/pallas_call | solution.py:288
  183.9 14.1 %shard_map.119 = f32[16,4096]{1,0:T(8,128)} custom-call(s32[4]{0:T(128)} %pad_add_fusion.scal, f32[8]{0:T(128)} %copy-done.6, s32[8,2048]{1,0:T(8,128)} %constant.58.clone.relcol, f32[8,8,2816]{2,1,0:T(8,128)} %collective-permute-done.refs_0_, f32[8,16,2816]{2,1,0:T(8,128)} %copy-done, f32[8,16,2816]{2,1,0:T(8,128)} %copy-done.2, ...), custom_call_target="tpu_custom_call" | custom-call | tf_op jit(solution)/shard_map/pallas_call | solution.py:288
  198.0 2.3 %add_exponential_fusion = f32[16,4096]{1,0:T(8,128)} fusion(f32[16,4096]{1,0:T(8,128)} %shard_map.119, f32[]{:T(128)} %multiply_reduce_fusion), kind=kLoop, calls=%fused_computation.6 | loop fusion | flops 65536 | bytes 524292 | tf_op jit(solution)/shard_map/exp | solution.py:358
  (58 shorter events, 31.7 us)
Async XLA Ops:
  2.8 89.1 %copy-start = (f32[8,16,2816]{2,1,0:T(8,128)}, f32[8,16,2816]{2,1,0:T(8,128)S(1)}, u32[]{:S(2)}) copy-start(f32[8,16,2816]{2,1,0:T(8,128)S(1)} %slice.20.refs_1_) | copy-start | bytes 4325380
  2.8 82.4 %copy-start.7 = (f32[8]{0:T(128)S(1)}, f32[8]{0:T(128)}, u32[]{:S(2)}) copy-start(f32[8]{0:T(128)} %param.13) | copy-start | bytes 100
  2.8 6.8 %collective-permute-start.1 = (f32[8,16,2816]{2,1,0:T(8,128)S(1)}, f32[8,16,2816]{2,1,0:T(8,128)S(1)}, u32[]{:S(2)}, u32[]{:S(2)}) collective-permute-start(f32[8,16,2816]{2,1,0:T(8,128)S(1)} %slice.20.refs_1_), channel_id=1, source_target_pairs={{0,8},{8,0},{16,24},{24,16},{32,40},{40,32},{48,56},{56,48},{64,72... | collective-permute-start | bytes 4325384 | tf_op jit(solution)/shard_map/ppermute | solution.py:329
  4.9 8.6 %collective-permute-start.5 = (f32[8,16,128]{2,1,0:T(8,128)S(1)}, f32[8,16,128]{2,1,0:T(8,128)S(1)}, u32[]{:S(2)}, u32[]{:S(2)}) collective-permute-start(f32[8,16,128]{2,1,0:T(8,128)S(1)} %get-tuple-element.9), channel_id=1, source_target_pairs={{0,1},{1,2},{2,3},{3,4},{4,5},{5,6},{6,7},{8,9},{9,10},{10,11},{11... | collective-permute-start | bytes 196616 | tf_op jit(solution)/shard_map/ppermute | solution.py:324
  8.3 6.2 %collective-permute-start.4 = (f32[8,16,128]{2,1,0:T(8,128)S(1)}, f32[8,16,128]{2,1,0:T(8,128)S(1)}, u32[]{:S(2)}, u32[]{:S(2)}) collective-permute-start(f32[8,16,128]{2,1,0:T(8,128)S(1)} %get-tuple-element.10), channel_id=1, source_target_pairs={{1,0},{2,1},{3,2},{4,3},{5,4},{6,5},{7,6},{9,8},{10,9},{11,10},{12... | collective-permute-start | bytes 196616 | tf_op jit(solution)/shard_map/ppermute | solution.py:325
  9.6 156.4 %copy-start.2 = (f32[8,16,2816]{2,1,0:T(8,128)}, f32[8,16,2816]{2,1,0:T(8,128)S(1)}, u32[]{:S(2)}) copy-start(f32[8,16,2816]{2,1,0:T(8,128)S(1)} %collective-permute-done.1.refs_2_) | copy-start | bytes 4325380
  9.6 50.1 %collective-permute-start.2 = (f32[8,16,2816]{2,1,0:T(8,128)S(1)}, f32[8,16,2816]{2,1,0:T(8,128)}, u32[]{:S(2)}, u32[]{:S(2)}) collective-permute-start(f32[8,16,2816]{2,1,0:T(8,128)S(1)} %collective-permute-done.1.refs_2_), channel_id=1, source_target_pairs={{0,16},{16,32},{32,48},{48,64},{64,80},{80,96},{96,112},{112,128},... | collective-permute-start | bytes 4325384 | tf_op jit(solution)/shard_map/ppermute | solution.py:330
  14.6 12.4 %collective-permute-start.7 = (f32[8,16,1408]{2,1,0:T(8,128)S(1)}, f32[8,16,1408]{2,1,0:T(8,128)}, u32[]{:S(2)}, u32[]{:S(2)}) collective-permute-start(f32[8,16,1408]{2,1,0:T(8,128)S(1)} %pad_maximum_fusion.refs_6_), channel_id=1, source_target_pairs={{0,8},{8,0},{16,24},{24,16},{32,40},{40,32},{48,56},{56,48},{64,72... | collective-permute-start | bytes 2162696 | tf_op jit(solution)/shard_map/ppermute | solution.py:329
  26.9 58.8 %collective-permute-start.8 = (f32[8,16,1408]{2,1,0:T(8,128)}, f32[8,16,1408]{2,1,0:T(8,128)}, u32[]{:S(2)}, u32[]{:S(2)}) collective-permute-start(f32[8,16,1408]{2,1,0:T(8,128)} %collective-permute-done.7.refs_7_), channel_id=1, source_target_pairs={{0,16},{16,32},{32,48},{48,64},{64,80},{80,96},{96,112},{112,128},... | collective-permute-start | bytes 2162696 | tf_op jit(solution)/shard_map/ppermute | solution.py:330
  59.7 106.3 %collective-permute-start.3 = (f32[8,16,2816]{2,1,0:T(8,128)}, f32[8,16,2816]{2,1,0:T(8,128)}, u32[]{:S(2)}, u32[]{:S(2)}) collective-permute-start(f32[8,16,2816]{2,1,0:T(8,128)} %collective-permute-done.2.refs_3_), channel_id=1, source_target_pairs={{0,8},{8,0},{16,24},{24,16},{32,40},{40,32},{48,56},{56,48},{64,72... | collective-permute-start | bytes 4325384 | tf_op jit(solution)/shard_map/ppermute | solution.py:331
  61.7 104.4 %collective-permute-start = (f32[8,8,2816]{2,1,0:T(8,128)}, f32[8,8,2816]{2,1,0:T(8,128)}, u32[]{:S(2)}, u32[]{:S(2)}) collective-permute-start(f32[8,8,2816]{2,1,0:T(8,128)} %convert_add_fusion.1), channel_id=1, source_target_pairs={{0,16},{16,32},{32,48},{48,64},{64,80},{80,96},{96,112},{112,128},... | collective-permute-start | bytes 2162696 | tf_op jit(solution)/shard_map/ppermute | solution.py:322
  63.6 36.9 %collective-permute-start.10 = (f32[8]{0:T(128)S(1)}, f32[8]{0:T(128)S(1)}, u32[]{:S(2)}, u32[]{:S(2)}) collective-permute-start(f32[8]{0:T(128)S(1)} %get-tuple-element.7), channel_id=1, source_target_pairs={{0,4},{1,5},{2,6},{3,7},{4,0},{5,1},{6,2},{7,3},{8,12},{9,13},{10,... | collective-permute-start | bytes 104 | tf_op jit(solution)/shard_map/ppermute | solution.py:335
  85.8 97.4 %collective-permute-start.9 = (f32[8,16,1408]{2,1,0:T(8,128)}, f32[8,16,1408]{2,1,0:T(8,128)}, u32[]{:S(2)}, u32[]{:S(2)}) collective-permute-start(f32[8,16,1408]{2,1,0:T(8,128)} %collective-permute-done.8.refs_8_), channel_id=1, source_target_pairs={{0,8},{8,0},{16,24},{24,16},{32,40},{40,32},{48,56},{56,48},{64,72... | collective-permute-start | bytes 2162696 | tf_op jit(solution)/shard_map/ppermute | solution.py:331
  91.9 91.2 %collective-permute-start.6 = (f32[8,8,1408]{2,1,0:T(8,128)}, f32[8,8,1408]{2,1,0:T(8,128)S(1)}, u32[]{:S(2)}, u32[]{:S(2)}) collective-permute-start(f32[8,8,1408]{2,1,0:T(8,128)} %fusion), channel_id=1, source_target_pairs={{0,16},{16,32},{32,48},{48,64},{64,80},{80,96},{96,112},{112,128},... | collective-permute-start | bytes 1081352 | tf_op jit(solution)/shard_map/ppermute | solution.py:328
  100.5 5.0 %collective-permute-start.11 = (f32[8]{0:T(128)S(1)}, f32[8]{0:T(128)S(1)}, u32[]{:S(2)}, u32[]{:S(2)}) collective-permute-start(f32[8]{0:T(128)S(1)} %add.65), channel_id=1, source_target_pairs={{0,8},{8,0},{16,24},{24,16},{32,40},{40,32},{48,56},{56,48},{64,72... | collective-permute-start | bytes 104 | tf_op jit(solution)/shard_map/ppermute | solution.py:335
  105.5 5.5 %collective-permute-start.12 = (f32[8]{0:T(128)S(1)}, f32[8]{0:T(128)S(1)}, u32[]{:S(2)}, u32[]{:S(2)}) collective-permute-start(f32[8]{0:T(128)S(1)} %add.66), channel_id=1, source_target_pairs={{0,1},{1,0},{2,3},{3,2},{4,5},{5,4},{6,7},{7,6},{8,9},{9,8},{10,11... | collective-permute-start | bytes 104 | tf_op jit(solution)/shard_map/ppermute | solution.py:335
  110.9 7.0 %collective-permute-start.13 = (f32[8]{0:T(128)S(1)}, f32[8]{0:T(128)S(1)}, u32[]{:S(2)}, u32[]{:S(2)}) collective-permute-start(f32[8]{0:T(128)S(1)} %add.67), channel_id=1, source_target_pairs={{0,2},{1,3},{2,0},{3,1},{4,6},{5,7},{6,4},{7,5},{8,10},{9,11},{10,... | collective-permute-start | bytes 104 | tf_op jit(solution)/shard_map/ppermute | solution.py:335
  117.9 6.7 %collective-permute-start.16 = (f32[8]{0:T(128)S(1)}, f32[8]{0:T(128)S(1)}, u32[]{:S(2)}, u32[]{:S(2)}) collective-permute-start(f32[8]{0:T(128)S(1)} %add.68), channel_id=1, source_target_pairs={{0,384},{8,392},{16,400},{24,408},{32,416},{40,424},{48,432},{56,4... | collective-permute-start | bytes 104 | tf_op jit(solution)/shard_map/ppermute | solution.py:335
  124.6 7.0 %collective-permute-start.15 = (f32[8]{0:T(128)S(1)}, f32[8]{0:T(128)S(1)}, u32[]{:S(2)}, u32[]{:S(2)}) collective-permute-start(f32[8]{0:T(128)S(1)} %add.68), channel_id=1, source_target_pairs={{0,256},{8,264},{16,272},{24,280},{32,288},{40,296},{48,304},{56,3... | collective-permute-start | bytes 104 | tf_op jit(solution)/shard_map/ppermute | solution.py:335
  131.5 5.5 %collective-permute-start.14 = (f32[8]{0:T(128)S(1)}, f32[8]{0:T(128)S(1)}, u32[]{:S(2)}, u32[]{:S(2)}) collective-permute-start(f32[8]{0:T(128)S(1)} %add.68), channel_id=1, source_target_pairs={{0,128},{8,136},{16,144},{24,152},{32,160},{40,168},{48,176},{56,1... | collective-permute-start | bytes 104 | tf_op jit(solution)/shard_map/ppermute | solution.py:335
  137.0 9.4 %collective-permute-start.17 = (f32[8]{0:T(128)S(1)}, f32[8]{0:T(128)S(1)}, u32[]{:S(2)}, u32[]{:S(2)}) collective-permute-start(f32[8]{0:T(128)S(1)} %add_add_fusion), channel_id=1, source_target_pairs={{0,64},{8,72},{16,80},{24,88},{32,96},{40,104},{48,112},{56,120},{... | collective-permute-start | bytes 104 | tf_op jit(solution)/shard_map/ppermute | solution.py:335
  146.3 7.2 %collective-permute-start.20 = (f32[8]{0:T(128)S(1)}, f32[8]{0:T(128)S(1)}, u32[]{:S(2)}, u32[]{:S(2)}) collective-permute-start(f32[8]{0:T(128)S(1)} %add.72), channel_id=1, source_target_pairs={{0,48},{8,56},{16,32},{24,40},{32,16},{40,24},{48,0},{56,8},{64,11... | collective-permute-start | bytes 104 | tf_op jit(solution)/shard_map/ppermute | solution.py:335
  153.6 6.3 %collective-permute-start.19 = (f32[8]{0:T(128)S(1)}, f32[8]{0:T(128)S(1)}, u32[]{:S(2)}, u32[]{:S(2)}) collective-permute-start(f32[8]{0:T(128)S(1)} %add.72), channel_id=1, source_target_pairs={{0,32},{8,40},{16,48},{24,56},{32,0},{40,8},{48,16},{56,24},{64,96... | collective-permute-start | bytes 104 | tf_op jit(solution)/shard_map/ppermute | solution.py:335
  159.9 5.5 %collective-permute-start.18 = (f32[8]{0:T(128)S(1)}, f32[8]{0:T(128)S(1)}, u32[]{:S(2)}, u32[]{:S(2)}) collective-permute-start(f32[8]{0:T(128)S(1)} %add.72), channel_id=1, source_target_pairs={{0,16},{8,24},{16,0},{24,8},{32,48},{40,56},{48,32},{56,40},{64,80... | collective-permute-start | bytes 104 | tf_op jit(solution)/shard_map/ppermute | solution.py:335
  (6 other events, 172.4 us)

commit v6 on v5

--- a/solution.py
+++ b/solution.py
@@ -318,11 +318,12 @@
         return lax.dynamic_slice_in_dim(x, (1 - core) * 8, 8, axis=1)
 
     edge = FIRST * LANES
-    zo_own = to_float(outward(counts[..., :edge]))
+    last, first = to_float(counts[..., -LANES:]), to_float(counts[..., :LANES])
+    left = lax.ppermute(last, "maps", to_right)
+    right = lax.ppermute(first, "maps", to_left)
+    zo_own = to_float(outward(after(counts, last, first)[..., :edge]))
     zo = [lax.ppermute(zo_own, "rows", hop)]
     n = to_float(after(counts, zo_own))
-    left = lax.ppermute(n[..., -LANES:], "maps", to_right)
-    right = lax.ppermute(n[..., :LANES], "maps", to_left)
     lane = lax.broadcasted_iota(jnp.int32, left.shape, 2)
     own = [n[..., :edge], jnp.concatenate([n[..., edge:], jnp.where(lane < 64, right, left)], axis=-1)]
     zo.append(lax.ppermute(outward(own[1]), "rows", hop))

time: 201 us -> 193 us (0.960)
  the two profiles are of different devices: /device:TPU:24 before, /device:TPU:30 now
where the time goes in v6:
time: 193 us; the launch traced here: 192 us
  waiting for transfers between devices  77.1 us (40%)
  starting transfers between devices  71.8 us (37%)
  Pallas kernels  31.2 us (16%)
  other arithmetic  9.55 us (5%)
    ppermute x11, waiting for transfers between devices, exchange(): lax.ppermute(x, axis, [(d, d ^ bit) for d in range(size)])  41.9 us
    ppermute x2, waiting for transfers between devices, on_device(): zq = [lax.ppermute(x, 'rows', hop) for x in q]  33.3 us
    pallas_call x2, Pallas kernels, run_kernel(): pl.pallas_call(functools.partial(kernel, reads, sources, joins, height, w...  31.2 us
    ppermute x11, starting transfers between devices, exchange(): lax.ppermute(x, axis, [(d, d ^ bit) for d in range(size)])  28.7 us
    ppermute x1, starting transfers between devices, on_device(): left = lax.ppermute(last, 'maps', to_right)  14.8 us
    ppermute x2, starting transfers between devices, on_device(): q = [lax.ppermute(x, 'rows', swap) for x in own]  13.1 us
    ppermute x2, starting transfers between devices, on_device(): zq = [lax.ppermute(x, 'rows', hop) for x in q]  4.84 us
  transfers between devices with their start and end apart: 21, of which 14 were waited for; matrix products, arithmetic and copies ran while one was open for 2% of the time, Pallas kernels for 9%

profile of v6, /device:TPU:30, one launch (start us, length us, event | category | flops | bytes accessed | tf_op | source)
XLA Modules:
  0.0 192.0 jit_solution(6832298805945912862)
XLA Ops:
  4.1 2.1 %collective-permute-start.1 = (f32[8,16,2816]{2,1,0:T(8,128)S(1)}, f32[8,16,2816]{2,1,0:T(8,128)S(1)}, u32[]{:S(2)}, u32[]{:S(2)}) collective-permute-start(f32[8,16,2816]{2,1,0:T(8,128)S(1)} %slice.20.refs_1_), channel_id=1, source_target_pairs={{0,8},{8,0},{16,24},{24,16},{32,40},{40,32},{48,56},{56,48},{64,72... | collective-permute-start | bytes 4325384 | tf_op jit(solution)/shard_map/ppermute | solution.py:330
  6.1 2.7 %collective-permute-start.4 = (f32[8,16,128]{2,1,0:T(8,128)S(1)}, f32[8,16,128]{2,1,0:T(8,128)S(1)}, u32[]{:S(2)}, u32[]{:S(2)}) collective-permute-start(f32[8,16,128]{2,1,0:T(8,128)S(1)} %copy-done.7), channel_id=1, source_target_pairs={{1,0},{2,1},{3,2},{4,3},{5,4},{6,5},{7,6},{9,8},{10,9},{11,10},{12... | collective-permute-start | bytes 196616 | tf_op jit(solution)/shard_map/ppermute | solution.py:323
  8.9 14.8 %collective-permute-start.5 = (f32[8,16,128]{2,1,0:T(8,128)S(1)}, f32[8,16,128]{2,1,0:T(8,128)S(1)}, u32[]{:S(2)}, u32[]{:S(2)}) collective-permute-start(f32[8,16,128]{2,1,0:T(8,128)S(1)} %copy-done.6), channel_id=1, source_target_pairs={{0,1},{1,2},{2,3},{3,4},{4,5},{5,6},{6,7},{8,9},{9,10},{10,11},{11... | collective-permute-start | bytes 196616 | tf_op jit(solution)/shard_map/ppermute | solution.py:322
  23.7 2.9 %collective-permute-start.2 = (f32[8,16,2816]{2,1,0:T(8,128)S(1)}, f32[8,16,2816]{2,1,0:T(8,128)}, u32[]{:S(2)}, u32[]{:S(2)}) collective-permute-start(f32[8,16,2816]{2,1,0:T(8,128)S(1)} %collective-permute-done.1.refs_2_), channel_id=1, source_target_pairs={{0,16},{16,32},{32,48},{48,64},{64,80},{80,96},{96,112},{112,128},... | collective-permute-start | bytes 4325384 | tf_op jit(solution)/shard_map/ppermute | solution.py:331
  26.9 11.1 %collective-permute-start.7 = (f32[8,16,1408]{2,1,0:T(8,128)S(1)}, f32[8,16,1408]{2,1,0:T(8,128)}, u32[]{:S(2)}, u32[]{:S(2)}) collective-permute-start(f32[8,16,1408]{2,1,0:T(8,128)S(1)} %pad_maximum_fusion.refs_6_), channel_id=1, source_target_pairs={{0,8},{8,0},{16,24},{24,16},{32,40},{40,32},{48,56},{56,48},{64,72... | collective-permute-start | bytes 2162696 | tf_op jit(solution)/shard_map/ppermute | solution.py:330
  37.9 1.9 %collective-permute-done.7.refs_7_ = f32[8,16,1408]{2,1,0:T(8,128)} collective-permute-done((f32[8,16,1408]{2,1,0:T(8,128)S(1)}, f32[8,16,1408]{2,1,0:T(8,128)}, u32[]{:S(2)}, u32[]{:S(2)}) %collective-permute-start.7) | collective-permute-done | bytes 720928 | tf_op jit(solution)/shard_map/ppermute | solution.py:330
  41.8 26.9 %collective-permute-done.2.refs_3_ = f32[8,16,2816]{2,1,0:T(8,128)} collective-permute-done((f32[8,16,2816]{2,1,0:T(8,128)S(1)}, f32[8,16,2816]{2,1,0:T(8,128)}, u32[]{:S(2)}, u32[]{:S(2)}) %collective-permute-start.2) | collective-permute-done | bytes 1441824 | tf_op jit(solution)/shard_map/ppermute | solution.py:331
  72.6 4.6 %collective-permute-start.10 = (f32[8]{0:T(128)S(1)}, f32[8]{0:T(128)S(1)}, u32[]{:S(2)}, u32[]{:S(2)}) collective-permute-start(f32[8]{0:T(128)S(1)} %get-tuple-element.9), channel_id=1, source_target_pairs={{0,4},{1,5},{2,6},{3,7},{4,0},{5,1},{6,2},{7,3},{8,12},{9,13},{10,... | collective-permute-start | bytes 104 | tf_op jit(solution)/shard_map/ppermute | solution.py:336
  77.9 6.3 %collective-permute-done.8.refs_8_ = f32[8,16,1408]{2,1,0:T(8,128)} collective-permute-done((f32[8,16,1408]{2,1,0:T(8,128)}, f32[8,16,1408]{2,1,0:T(8,128)}, u32[]{:S(2)}, u32[]{:S(2)}) %collective-permute-start.8) | collective-permute-done | bytes 720928 | tf_op jit(solution)/shard_map/ppermute | solution.py:331
  92.5 3.7 %collective-permute-start.11 = (f32[8]{0:T(128)S(1)}, f32[8]{0:T(128)S(1)}, u32[]{:S(2)}, u32[]{:S(2)}) collective-permute-start(f32[8]{0:T(128)S(1)} %add.73), channel_id=1, source_target_pairs={{0,8},{8,0},{16,24},{24,16},{32,40},{40,32},{48,56},{56,48},{64,72... | collective-permute-start | bytes 104 | tf_op jit(solution)/shard_map/ppermute | solution.py:336
  98.9 3.5 %collective-permute-done.12 = f32[8]{0:T(128)S(1)} collective-permute-done((f32[8]{0:T(128)S(1)}, f32[8]{0:T(128)S(1)}, u32[]{:S(2)}, u32[]{:S(2)}) %collective-permute-start.12) | collective-permute-done | bytes 64 | tf_op jit(solution)/shard_map/ppermute | solution.py:336
  102.5 2.2 %collective-permute-start.13 = (f32[8]{0:T(128)S(1)}, f32[8]{0:T(128)S(1)}, u32[]{:S(2)}, u32[]{:S(2)}) collective-permute-start(f32[8]{0:T(128)S(1)} %add.75), channel_id=1, source_target_pairs={{0,2},{1,3},{2,0},{3,1},{4,6},{5,7},{6,4},{7,5},{8,10},{9,11},{10,... | collective-permute-start | bytes 104 | tf_op jit(solution)/shard_map/ppermute | solution.py:336
  104.7 4.8 %collective-permute-done.13 = f32[8]{0:T(128)S(1)} collective-permute-done((f32[8]{0:T(128)S(1)}, f32[8]{0:T(128)S(1)}, u32[]{:S(2)}, u32[]{:S(2)}) %collective-permute-start.13) | collective-permute-done | bytes 64 | tf_op jit(solution)/shard_map/ppermute | solution.py:336
  111.4 4.7 %collective-permute-done.16 = f32[8]{0:T(128)S(1)} collective-permute-done((f32[8]{0:T(128)S(1)}, f32[8]{0:T(128)S(1)}, u32[]{:S(2)}, u32[]{:S(2)}) %collective-permute-start.16) | collective-permute-done | bytes 64 | tf_op jit(solution)/shard_map/ppermute | solution.py:336
  118.0 5.0 %collective-permute-done.15 = f32[8]{0:T(128)S(1)} collective-permute-done((f32[8]{0:T(128)S(1)}, f32[8]{0:T(128)S(1)}, u32[]{:S(2)}, u32[]{:S(2)}) %collective-permute-start.15) | collective-permute-done | bytes 64 | tf_op jit(solution)/shard_map/ppermute | solution.py:336
  125.0 3.5 %collective-permute-done.14 = f32[8]{0:T(128)S(1)} collective-permute-done((f32[8]{0:T(128)S(1)}, f32[8]{0:T(128)S(1)}, u32[]{:S(2)}, u32[]{:S(2)}) %collective-permute-start.14) | collective-permute-done | bytes 64 | tf_op jit(solution)/shard_map/ppermute | solution.py:336
  128.5 4.8 %collective-permute-start.17 = (f32[8]{0:T(128)S(1)}, f32[8]{0:T(128)S(1)}, u32[]{:S(2)}, u32[]{:S(2)}) collective-permute-start(f32[8]{0:T(128)S(1)} %add_add_fusion), channel_id=1, source_target_pairs={{0,64},{8,72},{16,80},{24,88},{32,96},{40,104},{48,112},{56,120},{... | collective-permute-start | bytes 104 | tf_op jit(solution)/shard_map/ppermute | solution.py:336
  133.3 4.6 %collective-permute-done.17 = f32[8]{0:T(128)S(1)} collective-permute-done((f32[8]{0:T(128)S(1)}, f32[8]{0:T(128)S(1)}, u32[]{:S(2)}, u32[]{:S(2)}) %collective-permute-start.17) | collective-permute-done | bytes 64 | tf_op jit(solution)/shard_map/ppermute | solution.py:336
  139.8 5.3 %collective-permute-done.20 = f32[8]{0:T(128)S(1)} collective-permute-done((f32[8]{0:T(128)S(1)}, f32[8]{0:T(128)S(1)}, u32[]{:S(2)}, u32[]{:S(2)}) %collective-permute-start.20) | collective-permute-done | bytes 64 | tf_op jit(solution)/shard_map/ppermute | solution.py:336
  147.0 4.4 %collective-permute-done.19 = f32[8]{0:T(128)S(1)} collective-permute-done((f32[8]{0:T(128)S(1)}, f32[8]{0:T(128)S(1)}, u32[]{:S(2)}, u32[]{:S(2)}) %collective-permute-start.19) | collective-permute-done | bytes 64 | tf_op jit(solution)/shard_map/ppermute | solution.py:336
  153.4 3.5 %collective-permute-done.18 = f32[8]{0:T(128)S(1)} collective-permute-done((f32[8]{0:T(128)S(1)}, f32[8]{0:T(128)S(1)}, u32[]{:S(2)}, u32[]{:S(2)}) %collective-permute-start.18) | collective-permute-done | bytes 64 | tf_op jit(solution)/shard_map/ppermute | solution.py:336
  157.7 17.1 %shard_map.118.refs_14_ = f32[16,2816]{1,0:T(8,128)} custom-call(s32[4]{0:T(128)} %pad_add_fusion.scal, f32[8]{0:T(128)} %copy-done.8, s32[8,2816]{1,0:T(8,128)} %constant.54.clone.relcol, f32[8,8,2816]{2,1,0:T(8,128)} %collective-permute-done.refs_0_, f32[8,16,2816]{2,1,0:T(8,128)} %copy-done, f32[8,16,2816]{2,1,0:T(8,128)} %copy-done.2, ...), custom_call_target="tpu_custom_call" | custom-call | tf_op jit(solution)/shard_map/pallas_call | solution.py:288
  175.5 14.1 %shard_map.119 = f32[16,4096]{1,0:T(8,128)} custom-call(s32[4]{0:T(128)} %pad_add_fusion.scal, f32[8]{0:T(128)} %copy-done.8, s32[8,2048]{1,0:T(8,128)} %constant.59.clone.relcol, f32[8,8,2816]{2,1,0:T(8,128)} %collective-permute-done.refs_0_, f32[8,16,2816]{2,1,0:T(8,128)} %copy-done, f32[8,16,2816]{2,1,0:T(8,128)} %copy-done.2, ...), custom_call_target="tpu_custom_call" | custom-call | tf_op jit(solution)/shard_map/pallas_call | solution.py:288
  189.6 2.4 %add_exponential_fusion = f32[16,4096]{1,0:T(8,128)} fusion(f32[16,4096]{1,0:T(8,128)} %shard_map.119, f32[]{:T(128)} %multiply_reduce_fusion), kind=kLoop, calls=%fused_computation.6 | loop fusion | flops 65536 | bytes 524292 | tf_op jit(solution)/shard_map/exp | solution.py:359
  (62 shorter events, 34.4 us)
Async XLA Ops:
  4.0 153.6 %copy-start = (f32[8,16,2816]{2,1,0:T(8,128)}, f32[8,16,2816]{2,1,0:T(8,128)S(1)}, u32[]{:S(2)}) copy-start(f32[8,16,2816]{2,1,0:T(8,128)S(1)} %slice.20.refs_1_) | copy-start | bytes 4325380
  4.0 73.2 %copy-start.9 = (f32[8]{0:T(128)S(1)}, f32[8]{0:T(128)}, u32[]{:S(2)}) copy-start(f32[8]{0:T(128)} %param.13) | copy-start | bytes 100
  4.1 19.7 %collective-permute-start.1 = (f32[8,16,2816]{2,1,0:T(8,128)S(1)}, f32[8,16,2816]{2,1,0:T(8,128)S(1)}, u32[]{:S(2)}, u32[]{:S(2)}) collective-permute-start(f32[8,16,2816]{2,1,0:T(8,128)S(1)} %slice.20.refs_1_), channel_id=1, source_target_pairs={{0,8},{8,0},{16,24},{24,16},{32,40},{40,32},{48,56},{56,48},{64,72... | collective-permute-start | bytes 4325384 | tf_op jit(solution)/shard_map/ppermute | solution.py:330
  6.1 20.6 %collective-permute-start.4 = (f32[8,16,128]{2,1,0:T(8,128)S(1)}, f32[8,16,128]{2,1,0:T(8,128)S(1)}, u32[]{:S(2)}, u32[]{:S(2)}) collective-permute-start(f32[8,16,128]{2,1,0:T(8,128)S(1)} %copy-done.7), channel_id=1, source_target_pairs={{1,0},{2,1},{3,2},{4,3},{5,4},{6,5},{7,6},{9,8},{10,9},{11,10},{12... | collective-permute-start | bytes 196616 | tf_op jit(solution)/shard_map/ppermute | solution.py:323
  8.9 17.9 %collective-permute-start.5 = (f32[8,16,128]{2,1,0:T(8,128)S(1)}, f32[8,16,128]{2,1,0:T(8,128)S(1)}, u32[]{:S(2)}, u32[]{:S(2)}) collective-permute-start(f32[8,16,128]{2,1,0:T(8,128)S(1)} %copy-done.6), channel_id=1, source_target_pairs={{0,1},{1,2},{2,3},{3,4},{4,5},{5,6},{6,7},{8,9},{9,10},{10,11},{11... | collective-permute-start | bytes 196616 | tf_op jit(solution)/shard_map/ppermute | solution.py:322
  23.7 133.9 %copy-start.2 = (f32[8,16,2816]{2,1,0:T(8,128)}, f32[8,16,2816]{2,1,0:T(8,128)S(1)}, u32[]{:S(2)}) copy-start(f32[8,16,2816]{2,1,0:T(8,128)S(1)} %collective-permute-done.1.refs_2_) | copy-start | bytes 4325380
  23.7 45.0 %collective-permute-start.2 = (f32[8,16,2816]{2,1,0:T(8,128)S(1)}, f32[8,16,2816]{2,1,0:T(8,128)}, u32[]{:S(2)}, u32[]{:S(2)}) collective-permute-start(f32[8,16,2816]{2,1,0:T(8,128)S(1)} %collective-permute-done.1.refs_2_), channel_id=1, source_target_pairs={{0,16},{16,32},{32,48},{48,64},{64,80},{80,96},{96,112},{112,128},... | collective-permute-start | bytes 4325384 | tf_op jit(solution)/shard_map/ppermute | solution.py:331
  26.9 13.0 %collective-permute-start.7 = (f32[8,16,1408]{2,1,0:T(8,128)S(1)}, f32[8,16,1408]{2,1,0:T(8,128)}, u32[]{:S(2)}, u32[]{:S(2)}) collective-permute-start(f32[8,16,1408]{2,1,0:T(8,128)S(1)} %pad_maximum_fusion.refs_6_), channel_id=1, source_target_pairs={{0,8},{8,0},{16,24},{24,16},{32,40},{40,32},{48,56},{56,48},{64,72... | collective-permute-start | bytes 2162696 | tf_op jit(solution)/shard_map/ppermute | solution.py:330
  39.9 44.3 %collective-permute-start.8 = (f32[8,16,1408]{2,1,0:T(8,128)}, f32[8,16,1408]{2,1,0:T(8,128)}, u32[]{:S(2)}, u32[]{:S(2)}) collective-permute-start(f32[8,16,1408]{2,1,0:T(8,128)} %collective-permute-done.7.refs_7_), channel_id=1, source_target_pairs={{0,16},{16,32},{32,48},{48,64},{64,80},{80,96},{96,112},{112,128},... | collective-permute-start | bytes 2162696 | tf_op jit(solution)/shard_map/ppermute | solution.py:331
  68.7 88.9 %collective-permute-start.3 = (f32[8,16,2816]{2,1,0:T(8,128)}, f32[8,16,2816]{2,1,0:T(8,128)}, u32[]{:S(2)}, u32[]{:S(2)}) collective-permute-start(f32[8,16,2816]{2,1,0:T(8,128)} %collective-permute-done.2.refs_3_), channel_id=1, source_target_pairs={{0,8},{8,0},{16,24},{24,16},{32,40},{40,32},{48,56},{56,48},{64,72... | collective-permute-start | bytes 4325384 | tf_op jit(solution)/shard_map/ppermute | solution.py:332
  70.7 87.0 %collective-permute-start = (f32[8,8,2816]{2,1,0:T(8,128)}, f32[8,8,2816]{2,1,0:T(8,128)}, u32[]{:S(2)}, u32[]{:S(2)}) collective-permute-start(f32[8,8,2816]{2,1,0:T(8,128)} %convert_add_fusion.1), channel_id=1, source_target_pairs={{0,16},{16,32},{32,48},{48,64},{64,80},{80,96},{96,112},{112,128},... | collective-permute-start | bytes 2162696 | tf_op jit(solution)/shard_map/ppermute | solution.py:325
  72.6 19.9 %collective-permute-start.10 = (f32[8]{0:T(128)S(1)}, f32[8]{0:T(128)S(1)}, u32[]{:S(2)}, u32[]{:S(2)}) collective-permute-start(f32[8]{0:T(128)S(1)} %get-tuple-element.9), channel_id=1, source_target_pairs={{0,4},{1,5},{2,6},{3,7},{4,0},{5,1},{6,2},{7,3},{8,12},{9,13},{10,... | collective-permute-start | bytes 104 | tf_op jit(solution)/shard_map/ppermute | solution.py:336
  84.2 90.6 %collective-permute-start.9 = (f32[8,16,1408]{2,1,0:T(8,128)}, f32[8,16,1408]{2,1,0:T(8,128)}, u32[]{:S(2)}, u32[]{:S(2)}) collective-permute-start(f32[8,16,1408]{2,1,0:T(8,128)} %collective-permute-done.8.refs_8_), channel_id=1, source_target_pairs={{0,8},{8,0},{16,24},{24,16},{32,40},{40,32},{48,56},{56,48},{64,72... | collective-permute-start | bytes 2162696 | tf_op jit(solution)/shard_map/ppermute | solution.py:332
  88.3 86.5 %collective-permute-start.6 = (f32[8,8,1408]{2,1,0:T(8,128)}, f32[8,8,1408]{2,1,0:T(8,128)S(1)}, u32[]{:S(2)}, u32[]{:S(2)}) collective-permute-start(f32[8,8,1408]{2,1,0:T(8,128)} %fusion), channel_id=1, source_target_pairs={{0,16},{16,32},{32,48},{48,64},{64,80},{80,96},{96,112},{112,128},... | collective-permute-start | bytes 1081352 | tf_op jit(solution)/shard_map/ppermute | solution.py:329
  92.5 4.5 %collective-permute-start.11 = (f32[8]{0:T(128)S(1)}, f32[8]{0:T(128)S(1)}, u32[]{:S(2)}, u32[]{:S(2)}) collective-permute-start(f32[8]{0:T(128)S(1)} %add.73), channel_id=1, source_target_pairs={{0,8},{8,0},{16,24},{24,16},{32,40},{40,32},{48,56},{56,48},{64,72... | collective-permute-start | bytes 104 | tf_op jit(solution)/shard_map/ppermute | solution.py:336
  97.0 5.5 %collective-permute-start.12 = (f32[8]{0:T(128)S(1)}, f32[8]{0:T(128)S(1)}, u32[]{:S(2)}, u32[]{:S(2)}) collective-permute-start(f32[8]{0:T(128)S(1)} %add.74), channel_id=1, source_target_pairs={{0,1},{1,0},{2,3},{3,2},{4,5},{5,4},{6,7},{7,6},{8,9},{9,8},{10,11... | collective-permute-start | bytes 104 | tf_op jit(solution)/shard_map/ppermute | solution.py:336
  102.5 7.0 %collective-permute-start.13 = (f32[8]{0:T(128)S(1)}, f32[8]{0:T(128)S(1)}, u32[]{:S(2)}, u32[]{:S(2)}) collective-permute-start(f32[8]{0:T(128)S(1)} %add.75), channel_id=1, source_target_pairs={{0,2},{1,3},{2,0},{3,1},{4,6},{5,7},{6,4},{7,5},{8,10},{9,11},{10,... | collective-permute-start | bytes 104 | tf_op jit(solution)/shard_map/ppermute | solution.py:336
  109.4 6.7 %collective-permute-start.16 = (f32[8]{0:T(128)S(1)}, f32[8]{0:T(128)S(1)}, u32[]{:S(2)}, u32[]{:S(2)}) collective-permute-start(f32[8]{0:T(128)S(1)} %add.76), channel_id=1, source_target_pairs={{0,384},{8,392},{16,400},{24,408},{32,416},{40,424},{48,432},{56,4... | collective-permute-start | bytes 104 | tf_op jit(solution)/shard_map/ppermute | solution.py:336
  116.1 7.0 %collective-permute-start.15 = (f32[8]{0:T(128)S(1)}, f32[8]{0:T(128)S(1)}, u32[]{:S(2)}, u32[]{:S(2)}) collective-permute-start(f32[8]{0:T(128)S(1)} %add.76), channel_id=1, source_target_pairs={{0,256},{8,264},{16,272},{24,280},{32,288},{40,296},{48,304},{56,3... | collective-permute-start | bytes 104 | tf_op jit(solution)/shard_map/ppermute | solution.py:336
  123.1 5.5 %collective-permute-start.14 = (f32[8]{0:T(128)S(1)}, f32[8]{0:T(128)S(1)}, u32[]{:S(2)}, u32[]{:S(2)}) collective-permute-start(f32[8]{0:T(128)S(1)} %add.76), channel_id=1, source_target_pairs={{0,128},{8,136},{16,144},{24,152},{32,160},{40,168},{48,176},{56,1... | collective-permute-start | bytes 104 | tf_op jit(solution)/shard_map/ppermute | solution.py:336
  128.5 9.4 %collective-permute-start.17 = (f32[8]{0:T(128)S(1)}, f32[8]{0:T(128)S(1)}, u32[]{:S(2)}, u32[]{:S(2)}) collective-permute-start(f32[8]{0:T(128)S(1)} %add_add_fusion), channel_id=1, source_target_pairs={{0,64},{8,72},{16,80},{24,88},{32,96},{40,104},{48,112},{56,120},{... | collective-permute-start | bytes 104 | tf_op jit(solution)/shard_map/ppermute | solution.py:336
  137.9 7.2 %collective-permute-start.20 = (f32[8]{0:T(128)S(1)}, f32[8]{0:T(128)S(1)}, u32[]{:S(2)}, u32[]{:S(2)}) collective-permute-start(f32[8]{0:T(128)S(1)} %add.80), channel_id=1, source_target_pairs={{0,48},{8,56},{16,32},{24,40},{32,16},{40,24},{48,0},{56,8},{64,11... | collective-permute-start | bytes 104 | tf_op jit(solution)/shard_map/ppermute | solution.py:336
  145.1 6.3 %collective-permute-start.19 = (f32[8]{0:T(128)S(1)}, f32[8]{0:T(128)S(1)}, u32[]{:S(2)}, u32[]{:S(2)}) collective-permute-start(f32[8]{0:T(128)S(1)} %add.80), channel_id=1, source_target_pairs={{0,32},{8,40},{16,48},{24,56},{32,0},{40,8},{48,16},{56,24},{64,96... | collective-permute-start | bytes 104 | tf_op jit(solution)/shard_map/ppermute | solution.py:336
  151.5 5.5 %collective-permute-start.18 = (f32[8]{0:T(128)S(1)}, f32[8]{0:T(128)S(1)}, u32[]{:S(2)}, u32[]{:S(2)}) collective-permute-start(f32[8]{0:T(128)S(1)} %add.80), channel_id=1, source_target_pairs={{0,16},{8,24},{16,0},{24,8},{32,48},{40,56},{48,32},{56,40},{64,80... | collective-permute-start | bytes 104 | tf_op jit(solution)/shard_map/ppermute | solution.py:336
  (8 other events, 168.1 us)

commit v7 on v6

--- a/solution.py
+++ b/solution.py
@@ -14,7 +14,7 @@
 LANES = 128
 EDGE = -1
 
-FIRST = 22
+FIRST = 18
 CHUNKS = (tuple(range(FIRST)), tuple(range(FIRST, 32)) + (EDGE,))
 KERNELS = (
     (tuple(range(FIRST)), (0,)),
@@ -116,8 +116,8 @@
     g1, g2, g3, bm = refs[n_in : n_in + 4]
     n_in += 4
     if joins:
-        earlier = refs[n_in : n_in + len(joins) - 1]
-        n_in += len(joins) - 1
+        log_scale, earlier = refs[n_in], refs[n_in + 1 : n_in + len(joins)]
+        n_in += len(joins)
     out = refs[n_in]
     n_ref, rr, rc, cv, h1h, h1l, h2h, h2l, h3h, h3l, u_ref, w_ref, sems = refs[n_in + 1 :][:13]
     acc_ref = refs[-1] if joins else out
@@ -244,7 +244,8 @@
     for i, moved in enumerate(joins):
         ref = acc_ref if i == len(joins) - 1 else earlier[i]
         for src, dst, count in moved:
-            out[:, dst * LANES : (dst + count) * LANES] = ref[:, src * LANES : (src + count) * LANES]
+            piece = ref[:, src * LANES : (src + count) * LANES] + log_scale[0]
+            out[:, dst * LANES : (dst + count) * LANES] = jnp.exp(piece)
 
 
 def relative_columns(reads):
@@ -253,7 +254,7 @@
     return np.tile(np.concatenate(cols).astype(np.int32)[None], (8, 1))
 
 
-def run_kernel(which, height, width, scal, mix, arrays, earlier):
+def run_kernel(which, height, width, scal, mix, arrays, earlier, log_scale):
     reads, sources = KERNELS[which]
     blocks = len(reads)
     lanes = blocks * LANES
@@ -282,8 +283,8 @@
         joins = tuple(
             tuple((KERNELS[i][0].index(lo), lo, hi - lo + 1) for lo, hi in kept) for i, kept in enumerate(KEPT)
         )
-        in_specs += [vmem] * len(earlier)
-        args += earlier
+        in_specs += [smem] + [vmem] * len(earlier)
+        args += [log_scale.reshape(1), *earlier]
         scratch.append(pltpu.VMEM((16, lanes), jnp.float32))
     return pl.pallas_call(
         functools.partial(kernel, reads, sources, joins, height, width),
@@ -326,27 +327,17 @@
     n = to_float(after(counts, zo_own))
     lane = lax.broadcasted_iota(jnp.int32, left.shape, 2)
     own = [n[..., :edge], jnp.concatenate([n[..., edge:], jnp.where(lane < 64, right, left)], axis=-1)]
+    q = [lax.ppermute(x, "rows", swap) for x in own]
+    zq = [lax.ppermute(q[0], "rows", hop)]
+
+    axes = ("rows", "maps")
+    sums = jnp.sum(n, axis=(1, 2))
+    copies_out = after(jnp.broadcast_to(sums, (n_rows * n_cols,) + sums.shape), q[0], own[1])
+    everyone = lax.all_to_all(copies_out, axes, 0, 0, tiled=True)
+    sums = jnp.sum(everyone, axis=0)
     zo.append(lax.ppermute(outward(own[1]), "rows", hop))
-    q = [lax.ppermute(x, "rows", swap) for x in own]
-    zq = [lax.ppermute(x, "rows", hop) for x in q]
+    zq.append(lax.ppermute(q[1], "rows", hop))
     f = [lax.ppermute(x, "rows", swap) for x in zq]
-
-    def exchange(x, axis, bits):
-        size = lax.axis_size(axis)
-        got = [lax.ppermute(x, axis, [(d, d ^ bit) for d in range(size)]) for bit in bits]
-        return functools.reduce(jnp.add, got, x)
-
-    sums = jnp.sum(n, axis=(1, 2))
-    for axis, bits in (
-        ("maps", (4,)),
-        ("rows", (1,)),
-        ("maps", (1,)),
-        ("maps", (2,)),
-        ("rows", (16, 32, 48)),
-        ("rows", (8,)),
-        ("rows", (2, 4, 6)),
-    ):
-        sums = exchange(sums, axis, bits)
     log_scale = jnp.sum(mix * jnp.log(float(height * width) / sums))
 
     outs = []
@@ -355,8 +346,8 @@
         for c in KERNELS[which][1]:
             arrays += [zo[c], own[c], q[c], zq[c], f[c]]
         earlier = outs if which == len(KERNELS) - 1 else []
-        outs.append(run_kernel(which, height, width, scal, mix, arrays, earlier))
-    return jnp.exp(outs[-1] + log_scale)
+        outs.append(run_kernel(which, height, width, scal, mix, arrays, earlier, log_scale))
+    return outs[-1]
 
 
 def solution(mesh):

time: 193 us -> 176 us (0.912)
  the two profiles are of different devices: /device:TPU:30 before, /device:TPU:37 now
where the time goes in v7:
time: 176 us; the launch traced here: 175 us
  starting transfers between devices  73.8 us (42%)
  waiting for transfers between devices  61.6 us (35%)
  Pallas kernels  32.1 us (18%)
  other arithmetic  6.34 us (4%)
    all_to_all x1, starting transfers between devices, on_device(): everyone = lax.all_to_all(copies_out, axes, 0, 0, tiled=True)  46.9 us
    pallas_call x2, Pallas kernels, run_kernel(): pl.pallas_call(functools.partial(kernel, reads, sources, joins, height, w...  32.1 us
    all_to_all x1, waiting for transfers between devices, on_device(): everyone = lax.all_to_all(copies_out, axes, 0, 0, tiled=True)  25.8 us
    ppermute x1, waiting for transfers between devices, on_device(): zq.append(lax.ppermute(q[1], 'rows', hop))  19.1 us
    ppermute x1, waiting for transfers between devices, on_device(): zq = [lax.ppermute(q[0], 'rows', hop)]  16.3 us
    ppermute x2, starting transfers between devices, on_device(): q = [lax.ppermute(x, 'rows', swap) for x in own]  5.06 us
    ppermute x1, starting transfers between devices, on_device(): zq = [lax.ppermute(q[0], 'rows', hop)]  4.61 us
    ppermute x1, starting transfers between devices, on_device(): zo = [lax.ppermute(zo_own, 'rows', hop)]  4.06 us
  transfers between devices with their start and end apart: 11, of which 4 were waited for; matrix products, arithmetic and copies ran while one was open for 4% of the time, Pallas kernels for 8%

profile of v7, /device:TPU:37, one launch (start us, length us, event | category | flops | bytes accessed | tf_op | source)
XLA Modules:
  0.0 175.1 jit_solution(2403499868651605638)
XLA Ops:
  0.0 1.0 convert_add_fusion.2
  1.0 2.2 %collective-permute-start.4 = (f32[8,16,128]{2,1,0:T(8,128)S(1)}, f32[8,16,128]{2,1,0:T(8,128)S(1)}, u32[]{:S(2)}, u32[]{:S(2)}) collective-permute-start(f32[8,16,128]{2,1,0:T(8,128)S(1)} %get-tuple-element.13), channel_id=1, source_target_pairs={{1,0},{2,1},{3,2},{4,3},{5,4},{6,5},{7,6},{9,8},{10,9},{11,10},{12... | collective-permute-start | bytes 196616 | tf_op jit(solution)/shard_map/ppermute | solution.py:324
  3.2 3.1 %collective-permute-start.5 = (f32[8,16,128]{2,1,0:T(8,128)S(1)}, f32[8,16,128]{2,1,0:T(8,128)S(1)}, u32[]{:S(2)}, u32[]{:S(2)}) collective-permute-start(f32[8,16,128]{2,1,0:T(8,128)S(1)} %get-tuple-element.14), channel_id=1, source_target_pairs={{0,1},{1,2},{2,3},{3,4},{4,5},{5,6},{6,7},{8,9},{9,10},{10,11},{11... | collective-permute-start | bytes 196616 | tf_op jit(solution)/shard_map/ppermute | solution.py:323
  6.4 0.9 convert_add_fusion.1
  7.8 3.1 %collective-permute-start.1 = (f32[8,16,2304]{2,1,0:T(8,128)S(1)}, f32[8,16,2304]{2,1,0:T(8,128)S(1)}, u32[]{:S(2)}, u32[]{:S(2)}) collective-permute-start(f32[8,16,2304]{2,1,0:T(8,128)S(1)} %slice.20.refs_1_), channel_id=1, source_target_pairs={{0,8},{8,0},{16,24},{24,16},{32,40},{40,32},{48,56},{56,48},{64,72... | collective-permute-start | bytes 3538952 | tf_op jit(solution)/shard_map/ppermute | solution.py:330
  11.1 1.9 %collective-permute-start.7 = (f32[8,16,1920]{2,1,0:T(8,128)S(1)}, f32[8,16,1920]{2,1,0:T(8,128)S(1)}, u32[]{:S(2)}, u32[]{:S(2)}) collective-permute-start(f32[8,16,1920]{2,1,0:T(8,128)S(1)} %pad_maximum_fusion.refs_6_), channel_id=1, source_target_pairs={{0,8},{8,0},{16,24},{24,16},{32,40},{40,32},{48,56},{56,48},{64,72... | collective-permute-start | bytes 2949128 | tf_op jit(solution)/shard_map/ppermute | solution.py:330
  13.4 4.6 %collective-permute-start.2 = (f32[8,16,2304]{2,1,0:T(8,128)S(1)}, f32[8,16,2304]{2,1,0:T(8,128)S(1)}, u32[]{:S(2)}, u32[]{:S(2)}) collective-permute-start(f32[8,16,2304]{2,1,0:T(8,128)S(1)} %collective-permute-done.1.refs_2_), channel_id=1, source_target_pairs={{0,16},{16,32},{32,48},{48,64},{64,80},{80,96},{96,112},{112,128},... | collective-permute-start | bytes 3538952 | tf_op jit(solution)/shard_map/ppermute | solution.py:331
  18.0 2.1 %collective-permute-start.8 = (f32[8,16,1920]{2,1,0:T(8,128)S(1)}, f32[8,16,1920]{2,1,0:T(8,128)}, u32[]{:S(2)}, u32[]{:S(2)}) collective-permute-start(f32[8,16,1920]{2,1,0:T(8,128)S(1)} %collective-permute-done.7.refs_7_), channel_id=1, source_target_pairs={{0,16},{16,32},{32,48},{48,64},{64,80},{80,96},{96,112},{112,128},... | collective-permute-start | bytes 2949128 | tf_op jit(solution)/shard_map/ppermute | solution.py:339
  20.1 16.3 %collective-permute-done.2.refs_3_ = f32[8,16,2304]{2,1,0:T(8,128)S(1)} collective-permute-done((f32[8,16,2304]{2,1,0:T(8,128)S(1)}, f32[8,16,2304]{2,1,0:T(8,128)S(1)}, u32[]{:S(2)}, u32[]{:S(2)}) %collective-permute-start.2) | collective-permute-done | bytes 1179680 | tf_op jit(solution)/shard_map/ppermute | solution.py:331
  36.4 1.9 %collective-permute-start.3 = (f32[8,16,2304]{2,1,0:T(8,128)S(1)}, f32[8,16,2304]{2,1,0:T(8,128)}, u32[]{:S(2)}, u32[]{:S(2)}) collective-permute-start(f32[8,16,2304]{2,1,0:T(8,128)S(1)} %collective-permute-done.2.refs_3_), channel_id=1, source_target_pairs={{0,8},{8,0},{16,24},{24,16},{32,40},{40,32},{48,56},{56,48},{64,72... | collective-permute-start | bytes 3538952 | tf_op jit(solution)/shard_map/ppermute | solution.py:340
  38.3 19.1 %collective-permute-done.8.refs_8_ = f32[8,16,1920]{2,1,0:T(8,128)} collective-permute-done((f32[8,16,1920]{2,1,0:T(8,128)S(1)}, f32[8,16,1920]{2,1,0:T(8,128)}, u32[]{:S(2)}, u32[]{:S(2)}) %collective-permute-start.8) | collective-permute-done | bytes 983072 | tf_op jit(solution)/shard_map/ppermute | solution.py:339
  57.5 1.9 %collective-permute-start.9 = (f32[8,16,1920]{2,1,0:T(8,128)}, f32[8,16,1920]{2,1,0:T(8,128)}, u32[]{:S(2)}, u32[]{:S(2)}) collective-permute-start(f32[8,16,1920]{2,1,0:T(8,128)} %collective-permute-done.8.refs_8_), channel_id=1, source_target_pairs={{0,8},{8,0},{16,24},{24,16},{32,40},{40,32},{48,56},{56,48},{64,72... | collective-permute-start | bytes 2949128 | tf_op jit(solution)/shard_map/ppermute | solution.py:340
  59.4 4.1 %collective-permute-start = (f32[8,8,2304]{2,1,0:T(8,128)}, f32[8,8,2304]{2,1,0:T(8,128)}, u32[]{:S(2)}, u32[]{:S(2)}) collective-permute-start(f32[8,8,2304]{2,1,0:T(8,128)} %convert_add_fusion.1), channel_id=1, source_target_pairs={{0,16},{16,32},{32,48},{48,64},{64,80},{80,96},{96,112},{112,128},... | collective-permute-start | bytes 1769480 | tf_op jit(solution)/shard_map/ppermute | solution.py:326
  63.5 0.9 fusion
  64.3 1.9 %collective-permute-start.6 = (f32[8,8,1920]{2,1,0:T(8,128)}, f32[8,8,1920]{2,1,0:T(8,128)}, u32[]{:S(2)}, u32[]{:S(2)}) collective-permute-start(f32[8,8,1920]{2,1,0:T(8,128)} %fusion), channel_id=1, source_target_pairs={{0,16},{16,32},{32,48},{48,64},{64,80},{80,96},{96,112},{112,128},... | collective-permute-start | bytes 1474568 | tf_op jit(solution)/shard_map/ppermute | solution.py:338
  66.3 0.6 reduce_sum.36
  66.9 0.6 broadcast_divide_fusion.mix
  67.5 0.7 broadcast_in_dim.3
  68.2 46.9 %all-to-all-start = ((f32[512,1,8]{2,1,0:T(1,128)}), f32[512,1,8]{2,1,0:T(1,128)S(1)}, u32[]{:S(2)}, u32[]{:S(2)}) async-start(f32[512,1,8]{2,1,0:T(1,128)} %bitcast.4), calls=%async_computation | async-start | bytes 524288 | tf_op jit(solution)/shard_map/all_to_all | solution.py:336
  115.2 0.7 pad_add_fusion.scal
  115.8 25.8 %all-to-all-done = f32[512,1,8]{2,1,0:T(1,128)S(1)} async-done(((f32[512,1,8]{2,1,0:T(1,128)}), f32[512,1,8]{2,1,0:T(1,128)S(1)}, u32[]{:S(2)}, u32[]{:S(2)}) %all-to-all-start) | async-done | bytes 16416 | tf_op jit(solution)/shard_map/all_to_all | solution.py:336
  142.2 0.6 multiply_reduce_fusion
  142.9 14.6 %shard_map.118.refs_15_ = f32[16,2304]{1,0:T(8,128)} custom-call(s32[4]{0:T(128)} %pad_add_fusion.scal, f32[8]{0:T(128)} %copy-done.6, s32[8,2304]{1,0:T(8,128)} %constant.54.clone.relcol, f32[8,8,2304]{2,1,0:T(8,128)} %collective-permute-done.refs_0_, f32[8,16,2304]{2,1,0:T(8,128)} %copy-done, f32[8,16,2304]{2,1,0:T(8,128)} %copy-done.2, ...), custom_call_target="tpu_custom_call" | custom-call | tf_op jit(solution)/shard_map/pallas_call | solution.py:289
  157.5 17.5 %shard_map.119 = f32[16,4096]{1,0:T(8,128)} custom-call(s32[4]{0:T(128)} %pad_add_fusion.scal, f32[8]{0:T(128)} %copy-done.6, s32[8,2560]{1,0:T(8,128)} %constant.59.clone.relcol, f32[8,8,2304]{2,1,0:T(8,128)} %collective-permute-done.refs_0_, f32[8,16,2304]{2,1,0:T(8,128)} %copy-done, f32[8,16,2304]{2,1,0:T(8,128)} %copy-done.2, f32[8,16,2304]{2,1,0:T(8,128)} %copy-done.3, ...), custom_call_target="tpu_custom_call" | custom-call | tf_op jit(solution)/shard_map/pallas_call | solution.py:289
  (33 shorter events, 1.6 us)
Async XLA Ops:
  0.0 6.4 %slice-start = ((s32[8,16,4096]{2,1,0:T(8,128)}), s32[8,16,2304]{2,1,0:T(8,128)S(1)}, s32[]{:S(2)}) async-start(s32[8,16,4096]{2,1,0:T(8,128)} %param.12), calls=%async_computation.1 | async-start | bytes 2359296 | tf_op jit(solution)/shard_map/slice | solution.py:325
  0.0 7.2 %copy-start.1 = (s32[8,16,4096]{2,1,0:T(8,128)S(1)}, s32[8,16,4096]{2,1,0:T(8,128)}, u32[]{:S(2)}) copy-start(s32[8,16,4096]{2,1,0:T(8,128)} %param.12) | copy-start | bytes 6291460
  1.0 10.0 %collective-permute-start.4 = (f32[8,16,128]{2,1,0:T(8,128)S(1)}, f32[8,16,128]{2,1,0:T(8,128)S(1)}, u32[]{:S(2)}, u32[]{:S(2)}) collective-permute-start(f32[8,16,128]{2,1,0:T(8,128)S(1)} %get-tuple-element.13), channel_id=1, source_target_pairs={{1,0},{2,1},{3,2},{4,3},{5,4},{6,5},{7,6},{9,8},{10,9},{11,10},{12... | collective-permute-start | bytes 196616 | tf_op jit(solution)/shard_map/ppermute | solution.py:324
  3.2 7.8 %collective-permute-start.5 = (f32[8,16,128]{2,1,0:T(8,128)S(1)}, f32[8,16,128]{2,1,0:T(8,128)S(1)}, u32[]{:S(2)}, u32[]{:S(2)}) collective-permute-start(f32[8,16,128]{2,1,0:T(8,128)S(1)} %get-tuple-element.14), channel_id=1, source_target_pairs={{0,1},{1,2},{2,3},{3,4},{4,5},{5,6},{6,7},{8,9},{9,10},{10,11},{11... | collective-permute-start | bytes 196616 | tf_op jit(solution)/shard_map/ppermute | solution.py:323
  7.7 56.6 %copy-start = (f32[8,16,2304]{2,1,0:T(8,128)}, f32[8,16,2304]{2,1,0:T(8,128)S(1)}, u32[]{:S(2)}) copy-start(f32[8,16,2304]{2,1,0:T(8,128)S(1)} %slice.20.refs_1_) | copy-start | bytes 3538948
  7.8 5.6 %collective-permute-start.1 = (f32[8,16,2304]{2,1,0:T(8,128)S(1)}, f32[8,16,2304]{2,1,0:T(8,128)S(1)}, u32[]{:S(2)}, u32[]{:S(2)}) collective-permute-start(f32[8,16,2304]{2,1,0:T(8,128)S(1)} %slice.20.refs_1_), channel_id=1, source_target_pairs={{0,8},{8,0},{16,24},{24,16},{32,40},{40,32},{48,56},{56,48},{64,72... | collective-permute-start | bytes 3538952 | tf_op jit(solution)/shard_map/ppermute | solution.py:330
  11.0 55.3 %copy-start.7 = (f32[8]{0:T(128)S(1)}, f32[8]{0:T(128)}, u32[]{:S(2)}) copy-start(f32[8]{0:T(128)} %param.13) | copy-start | bytes 100
  11.1 53.2 %copy-start.4 = (f32[8,16,1920]{2,1,0:T(8,128)}, f32[8,16,1920]{2,1,0:T(8,128)S(1)}, u32[]{:S(2)}) copy-start(f32[8,16,1920]{2,1,0:T(8,128)S(1)} %pad_maximum_fusion.refs_6_) | copy-start | bytes 2949124
  11.1 6.8 %collective-permute-start.7 = (f32[8,16,1920]{2,1,0:T(8,128)S(1)}, f32[8,16,1920]{2,1,0:T(8,128)S(1)}, u32[]{:S(2)}, u32[]{:S(2)}) collective-permute-start(f32[8,16,1920]{2,1,0:T(8,128)S(1)} %pad_maximum_fusion.refs_6_), channel_id=1, source_target_pairs={{0,8},{8,0},{16,24},{24,16},{32,40},{40,32},{48,56},{56,48},{64,72... | collective-permute-start | bytes 2949128 | tf_op jit(solution)/shard_map/ppermute | solution.py:330
  13.4 129.5 %copy-start.2 = (f32[8,16,2304]{2,1,0:T(8,128)}, f32[8,16,2304]{2,1,0:T(8,128)S(1)}, u32[]{:S(2)}) copy-start(f32[8,16,2304]{2,1,0:T(8,128)S(1)} %collective-permute-done.1.refs_2_) | copy-start | bytes 3538948
  13.4 23.0 %collective-permute-start.2 = (f32[8,16,2304]{2,1,0:T(8,128)S(1)}, f32[8,16,2304]{2,1,0:T(8,128)S(1)}, u32[]{:S(2)}, u32[]{:S(2)}) collective-permute-start(f32[8,16,2304]{2,1,0:T(8,128)S(1)} %collective-permute-done.1.refs_2_), channel_id=1, source_target_pairs={{0,16},{16,32},{32,48},{48,64},{64,80},{80,96},{96,112},{112,128},... | collective-permute-start | bytes 3538952 | tf_op jit(solution)/shard_map/ppermute | solution.py:331
  18.0 18.4 %copy-start.5 = (f32[8,16,1920]{2,1,0:T(8,128)}, f32[8,16,1920]{2,1,0:T(8,128)S(1)}, u32[]{:S(2)}) copy-start(f32[8,16,1920]{2,1,0:T(8,128)S(1)} %collective-permute-done.7.refs_7_) | copy-start | bytes 2949124
  18.0 39.5 %collective-permute-start.8 = (f32[8,16,1920]{2,1,0:T(8,128)S(1)}, f32[8,16,1920]{2,1,0:T(8,128)}, u32[]{:S(2)}, u32[]{:S(2)}) collective-permute-start(f32[8,16,1920]{2,1,0:T(8,128)S(1)} %collective-permute-done.7.refs_7_), channel_id=1, source_target_pairs={{0,16},{16,32},{32,48},{48,64},{64,80},{80,96},{96,112},{112,128},... | collective-permute-start | bytes 2949128 | tf_op jit(solution)/shard_map/ppermute | solution.py:339
  36.4 106.5 %copy-start.3 = (f32[8,16,2304]{2,1,0:T(8,128)}, f32[8,16,2304]{2,1,0:T(8,128)S(1)}, u32[]{:S(2)}) copy-start(f32[8,16,2304]{2,1,0:T(8,128)S(1)} %collective-permute-done.2.refs_3_) | copy-start | bytes 3538948
  36.4 106.5 %collective-permute-start.3 = (f32[8,16,2304]{2,1,0:T(8,128)S(1)}, f32[8,16,2304]{2,1,0:T(8,128)}, u32[]{:S(2)}, u32[]{:S(2)}) collective-permute-start(f32[8,16,2304]{2,1,0:T(8,128)S(1)} %collective-permute-done.2.refs_3_), channel_id=1, source_target_pairs={{0,8},{8,0},{16,24},{24,16},{32,40},{40,32},{48,56},{56,48},{64,72... | collective-permute-start | bytes 3538952 | tf_op jit(solution)/shard_map/ppermute | solution.py:340
  57.5 100.0 %collective-permute-start.9 = (f32[8,16,1920]{2,1,0:T(8,128)}, f32[8,16,1920]{2,1,0:T(8,128)}, u32[]{:S(2)}, u32[]{:S(2)}) collective-permute-start(f32[8,16,1920]{2,1,0:T(8,128)} %collective-permute-done.8.refs_8_), channel_id=1, source_target_pairs={{0,8},{8,0},{16,24},{24,16},{32,40},{40,32},{48,56},{56,48},{64,72... | collective-permute-start | bytes 2949128 | tf_op jit(solution)/shard_map/ppermute | solution.py:340
  59.4 83.5 %collective-permute-start = (f32[8,8,2304]{2,1,0:T(8,128)}, f32[8,8,2304]{2,1,0:T(8,128)}, u32[]{:S(2)}, u32[]{:S(2)}) collective-permute-start(f32[8,8,2304]{2,1,0:T(8,128)} %convert_add_fusion.1), channel_id=1, source_target_pairs={{0,16},{16,32},{32,48},{48,64},{64,80},{80,96},{96,112},{112,128},... | collective-permute-start | bytes 1769480 | tf_op jit(solution)/shard_map/ppermute | solution.py:326
  64.3 93.2 %collective-permute-start.6 = (f32[8,8,1920]{2,1,0:T(8,128)}, f32[8,8,1920]{2,1,0:T(8,128)}, u32[]{:S(2)}, u32[]{:S(2)}) collective-permute-start(f32[8,8,1920]{2,1,0:T(8,128)} %fusion), channel_id=1, source_target_pairs={{0,16},{16,32},{32,48},{48,64},{64,80},{80,96},{96,112},{112,128},... | collective-permute-start | bytes 1474568 | tf_op jit(solution)/shard_map/ppermute | solution.py:338
  67.5 75.4 %copy-start.6 = (f32[8]{0:T(128)}, f32[8]{0:T(128)S(1)}, u32[]{:S(2)}) copy-start(f32[8]{0:T(128)S(1)} %broadcast_divide_fusion.mix) | copy-start | bytes 100
  68.2 73.4 %all-to-all-start = ((f32[512,1,8]{2,1,0:T(1,128)}), f32[512,1,8]{2,1,0:T(1,128)S(1)}, u32[]{:S(2)}, u32[]{:S(2)}) async-start(f32[512,1,8]{2,1,0:T(1,128)} %bitcast.4), calls=%async_computation | async-start | bytes 524288 | tf_op jit(solution)/shard_map/all_to_all | solution.py:336
